TPU v7x, 256 devices: a whole 4x4x8 slice. The times are simulated.
256 devices in a mesh: lon: 32 (over x, z_lo, core), lat: 8 (over y, z_hi).
Axes of the slice: x: 4, y: 4, z: 8 (z_hi: 2, z_lo: 4; z = z_hi * 4 + z_lo), core: 2. Of those that a mesh axis runs over, the one named last changes fastest.
Arguments:
- state: float32 [3, 256, 64, 8192], P(None, None, 'lat', 'lon'), may hold values from -6 to 6
- bathymetry: float32 [64, 8192], P('lat', 'lon'), may hold values from 0.5 to 2
- obs_index: int32 [8, 32, 256], P('lat', 'lon'), may hold values from 0 to 2047
- obs_count: int32 [8, 32], P('lat', 'lon'), may hold values from 85 to 256, as said below
- obs_value: float32 [8, 32, 256], P('lat', 'lon'), may hold values from -6 to 6
- obs_sd: float32 [8, 32, 256], P('lat', 'lon'), may hold values from 0.5 to 2
Outputs:
- analysis: float32 [3, 256, 64, 8192], P(None, None, 'lat', 'lon')
Inputs may be any that keep to these rules, and one draw needn't show every extreme that they name: `obs_count`: at least 85 slots of every tile are used; at least one tile uses all 256. `obs_index`: several slots may name the same cell.
All inputs are finite; a program needn't handle non-finite values.
Results may differ from a plain program's by a relative error of at most 0.000051.
Values sent between devices are 32-bit elements; how exact they have to be, the bound alone decides.
No kernel may reach another device: no remote copies, remote signals or barrier semaphores. Data moves between devices by JAX's collectives and lax.ppermute only.
A program may use at most 128 MiB of HBM per device.

v0:
```python
import math

import jax
import jax.numpy as jnp
from jax import lax
from jax.sharding import PartitionSpec as P


def with_halo(value, sides, width, wrap):
    for axis, dim in sides:
        count, length = (lax.axis_size(axis), value.shape[dim])
        up = [(i, (i + 1) % count) for i in range(count if wrap else count - 1)]
        down = [(j, i) for i, j in up]
        last = lax.slice_in_dim(value, length - width, length, axis=dim)
        first = lax.slice_in_dim(value, 0, width, axis=dim)
        before = lax.ppermute(last, axis, up)
        after = lax.ppermute(first, axis, down)
        value = jnp.concatenate([before, value, after], axis=dim)
    return value


def coriolis(rows, total):
    return jnp.sin(math.pi / 3.0 * ((rows.astype(jnp.float32) + 0.5) / total - 0.5))[:, None]


def extend(field, width):
    wide = with_halo(field, (("lat", 2),), width, False)
    return with_halo(wide, (("lon", 3),), width, True)


def new_height(height, flux, keep):
    div = (
        flux[0][:, 1:-1, 2:] - flux[0][:, 1:-1, :-2] + flux[1][:, 2:, 1:-1] - flux[1][:, :-2, 1:-1]
    )
    return (height - 0.25 * div) * keep


def new_wind(east, north, height, fcor, keep):
    grad_x = height[:, 1:-1, 2:] - height[:, 1:-1, :-2]
    grad_y = height[:, 2:, 1:-1] - height[:, :-2, 1:-1]
    east_new = (east + 0.5 * (fcor * north - 0.5 * grad_x)) * keep
    north_new = (north - 0.5 * (fcor * east + 0.5 * grad_y)) * keep
    return (east_new, north_new)


def shards(state, bathymetry, obs_index, obs_count, obs_value, obs_sd):
    members, nrows, ncols = (state.shape[1], state.shape[2], state.shape[3])
    total_rows = nrows * lax.axis_size("lat")
    base = lax.axis_index("lat") * nrows
    fcor = coriolis(base + jnp.arange(nrows), total_rows)
    height, east, north = (state[0], state[1], state[2])
    for step in range(2):
        flux = extend(jnp.stack([bathymetry * east, bathymetry * north]), 1)
        height = new_height(height, flux, 1.0)
        tall = extend(height[None], 1)[0]
        east, north = new_wind(east, north, tall, fcor, 1.0)
    slots = obs_index.shape[2]
    flat_height = height.reshape(members, nrows * ncols)
    hx = jnp.take(flat_height, obs_index.reshape(-1), axis=1)
    valid = (jnp.arange(slots) < obs_count.reshape(())).astype(jnp.float32)
    sigma = obs_sd.reshape(-1) * (
        math.sqrt(slots * lax.axis_size("lat") * lax.axis_size("lon")) / 16.0
    )
    hmean = jnp.mean(hx, axis=0)
    anomal = (hx - hmean) / (math.sqrt(members - 1) * sigma) * valid
    innov = (obs_value.reshape(-1) - hmean) / sigma * valid
    gram = jnp.dot(anomal, anomal.T, precision=lax.Precision.HIGHEST)
    proj = jnp.dot(anomal, innov, precision=lax.Precision.HIGHEST)
    gram, proj = lax.psum((gram, proj), ("lon", "lat"))
    eye = jnp.eye(members, dtype=jnp.float32)
    lower = jnp.linalg.cholesky(gram + eye)
    inv_lower = jax.scipy.linalg.solve_triangular(lower, eye, lower=True)
    weights = jax.scipy.linalg.cho_solve((lower, True), proj)
    transform = inv_lower.T + weights[:, None] / math.sqrt(members - 1)
    fields = jnp.stack([height, east, north])
    center = jnp.mean(fields, axis=1, keepdims=True)
    mixed = jnp.einsum("nm,cnab->cmab", transform, fields - center, precision=lax.Precision.HIGHEST)
    return center + mixed


def solution(mesh):
    return jax.shard_map(
        shards,
        mesh=mesh,
        in_specs=(
            P(None, None, "lat", "lon"),
            P("lat", "lon"),
            P("lat", "lon", None),
            P("lat", "lon"),
            P("lat", "lon", None),
            P("lat", "lon", None),
        ),
        out_specs=P(None, None, "lat", "lon"),
        check_vma=False,
    )
```

profile of v0, /device:TPU:8, one launch (start us, length us, event | category | flops | bytes accessed | tf_op | source)
XLA Modules:
  0.0 588.7 jit_solution(7116847816058828899)
XLA Ops:
  27.2 9.1 %collective-permute-start = (f32[2,256,1,256]{1,0,3,2:T(2,128)S(1)}, f32[2,256,1,256]{1,0,3,2:T(2,128)S(1)}, u32[]{:S(2)}, u32[]{:S(2)}) collective-permute-start(f32[2,256,1,256]{1,0,3,2:T(2,128)S(1)} %get-tuple-element.44), channel_id=1, source_target_pairs={{0,1},{1,2},{2,3},{3,4},{4,5},{5,6},{6,7},{8,9},{9,10},{10,11},{11... | collective-permute-start | bytes 1572872 | tf_op jit(solution)/shard_map/ppermute | solution.py:16
  38.3 12.9 %collective-permute-done = f32[2,256,1,256]{1,0,3,2:T(2,128)S(1)} collective-permute-done((f32[2,256,1,256]{1,0,3,2:T(2,128)S(1)}, f32[2,256,1,256]{1,0,3,2:T(2,128)S(1)}, u32[]{:S(2)}, u32[]{:S(2)}) %collective-permute-start) | collective-permute-done | bytes 524320 | tf_op jit(solution)/shard_map/ppermute | solution.py:16
  51.2 30.3 %collective-permute-done.1 = f32[2,256,1,256]{1,0,3,2:T(2,128)S(1)} collective-permute-done((f32[2,256,1,256]{1,0,3,2:T(2,128)S(1)}, f32[2,256,1,256]{1,0,3,2:T(2,128)S(1)}, u32[]{:S(2)}, u32[]{:S(2)}) %collective-permute-start.1) | collective-permute-done | bytes 524320 | tf_op jit(solution)/shard_map/ppermute | solution.py:17
  81.6 6.2 %collective-permute-start.3 = (f32[2,256,10,1]{1,0,3,2:T(2,128)S(1)}, f32[2,256,10,1]{1,0,3,2:T(2,128)S(1)}, u32[]{:S(2)}, u32[]{:S(2)}) collective-permute-start(f32[2,256,10,1]{1,0,3,2:T(2,128)S(1)} %get-tuple-element.41), channel_id=1, source_target_pairs={{8,0},{16,8},{24,16},{32,24},{40,32},{48,40},{56,48},{64,56},{72,6... | collective-permute-start | bytes 61448 | tf_op jit(solution)/shard_map/ppermute | solution.py:17
  90.7 9.7 %pad_maximum_fusion.2 = f32[2,256,10,258]{1,0,3,2:T(2,128)} fusion(f32[2,256,10,1]{1,0,3,2:T(2,128)S(1)} %collective-permute-done.3, f32[2,256,1,256]{1,0,3,2:T(2,128)S(1)} %collective-permute-done.1, f32[1,256,8,256]{1,0,3,2:T(1,128)} %copy-done, f32[1,256,8,256]{1,0,3,2:T(1,128)S(1)} %copy.43, f32[2,256,1,256]{1,0,3,2:T(2,128)S(1)} %collective-permute-done, ...), kind=kLoop, calls=%fused_computation.8 | loop fusion | flops 6604800 | bytes 10567680 | tf_op jit(solution)/shard_map/concatenate | solution.py:18
  100.5 10.4 %fusion.63 = (f32[1,256,10,258]{1,0,3,2:T(1,128)S(1)}, f32[1,256,10,258]{1,0,3,2:T(1,128)}) fusion(f32[2,256,10,258]{1,0,3,2:T(2,128)} %pad_maximum_fusion.2), kind=kLoop, calls=%fused_computation.141 | loop fusion | bytes 10567680 | tf_op jit(solution)/shard_map/slice | solution.py:33
  114.0 9.3 %collective-permute-start.4 = (f32[1,256,1,256]{1,3,2,0:T(8,128)S(1)}, f32[1,256,1,256]{1,3,2,0:T(8,128)S(1)}, u32[]{:S(2)}, u32[]{:S(2)}) collective-permute-start(f32[1,256,1,256]{1,3,2,0:T(8,128)S(1)} %get-tuple-element.52), channel_id=1, source_target_pairs={{0,1},{1,2},{2,3},{3,4},{4,5},{5,6},{6,7},{8,9},{9,10},{10,11},{11... | collective-permute-start | bytes 786440 | tf_op jit(solution)/shard_map/ppermute | solution.py:16
  125.3 10.7 %collective-permute-done.4 = f32[1,256,1,256]{1,3,2,0:T(8,128)S(1)} collective-permute-done((f32[1,256,1,256]{1,3,2,0:T(8,128)S(1)}, f32[1,256,1,256]{1,3,2,0:T(8,128)S(1)}, u32[]{:S(2)}, u32[]{:S(2)}) %collective-permute-start.4) | collective-permute-done | bytes 262176 | tf_op jit(solution)/shard_map/ppermute | solution.py:16
  136.0 6.7 %collective-permute-done.5 = f32[1,256,1,256]{1,3,2,0:T(8,128)S(1)} collective-permute-done((f32[1,256,1,256]{1,3,2,0:T(8,128)S(1)}, f32[1,256,1,256]{1,3,2,0:T(8,128)S(1)}, u32[]{:S(2)}, u32[]{:S(2)}) %collective-permute-start.5) | collective-permute-done | bytes 262176 | tf_op jit(solution)/shard_map/ppermute | solution.py:17
  144.5 5.8 collective-permute-start.7
  164.4 6.4 %collective-permute-start.8 = (f32[2,256,1,256]{1,3,2,0:T(8,128)S(1)}, f32[2,256,1,256]{1,3,2,0:T(8,128)S(1)}, u32[]{:S(2)}, u32[]{:S(2)}) collective-permute-start(f32[2,256,1,256]{1,3,2,0:T(8,128)S(1)} %get-tuple-element.42), channel_id=1, source_target_pairs={{0,1},{1,2},{2,3},{3,4},{4,5},{5,6},{6,7},{8,9},{9,10},{10,11},{11... | collective-permute-start | bytes 1572872 | tf_op jit(solution)/shard_map/ppermute | solution.py:16
  176.8 17.5 %collective-permute-done.8 = f32[2,256,1,256]{1,3,2,0:T(8,128)S(1)} collective-permute-done((f32[2,256,1,256]{1,3,2,0:T(8,128)S(1)}, f32[2,256,1,256]{1,3,2,0:T(8,128)S(1)}, u32[]{:S(2)}, u32[]{:S(2)}) %collective-permute-start.8) | collective-permute-done | bytes 524320 | tf_op jit(solution)/shard_map/ppermute | solution.py:16
  194.5 7.4 %collective-permute-start.11 = (f32[2,256,10,1]{1,0,3,2:T(2,128)S(1)}, f32[2,256,10,1]{1,0,3,2:T(2,128)S(1)}, u32[]{:S(2)}, u32[]{:S(2)}) collective-permute-start(f32[2,256,10,1]{1,0,3,2:T(2,128)S(1)} %copy.50), channel_id=1, source_target_pairs={{8,0},{16,8},{24,16},{32,24},{40,32},{48,40},{56,48},{64,56},{72,6... | collective-permute-start | bytes 61448 | tf_op jit(solution)/shard_map/ppermute | solution.py:17
  202.4 13.6 %collective-permute-done.10 = f32[2,256,10,1]{1,0,3,2:T(2,128)S(1)} collective-permute-done((f32[2,256,10,1]{1,0,3,2:T(2,128)S(1)}, f32[2,256,10,1]{1,0,3,2:T(2,128)S(1)}, u32[]{:S(2)}, u32[]{:S(2)}) %collective-permute-start.10) | collective-permute-done | bytes 20512 | tf_op jit(solution)/shard_map/ppermute | solution.py:16
  224.2 7.3 %collective-permute-start.12 = (f32[1,256,1,256]{1,3,2,0:T(8,128)}, f32[1,256,1,256]{1,3,2,0:T(8,128)S(1)}, u32[]{:S(2)}, u32[]{:S(2)}) collective-permute-start(f32[1,256,1,256]{1,3,2,0:T(8,128)} %get-tuple-element.50), channel_id=1, source_target_pairs={{0,1},{1,2},{2,3},{3,4},{4,5},{5,6},{6,7},{8,9},{9,10},{10,11},{11... | collective-permute-start | bytes 786440 | tf_op jit(solution)/shard_map/ppermute | solution.py:16
  231.5 5.8 collective-permute-start.13
  237.5 78.8 %psum.15 = f32[256]{0:T(256)S(1)} all-reduce(f32[256]{0:T(256)S(1)} %bitcast.156), channel_id=1, replica_groups=mesh['lon'=32,'lat'=8] {'lon','lat'}, use_global_device_ids=true, to_apply=%region_7.8 | all-reduce | flops 256 | bytes 2048 | tf_op jit(solution)/shard_map/psum | solution.py:69
  316.3 167.8 %all-reduce.3.cloned.1.call-done = f32[256,256]{0,1:T(8,128)} async-done(((f32[256,256]{0,1:T(8,128)}), f32[256,256]{0,1:T(8,128)}) %all-reduce.3.cloned.1.call-update) | async-done | bytes 262160 | tf_op jit(solution)/shard_map/psum | solution.py:69
  486.2 11.7 %cholesky.49 = f32[128,128]{1,0:T(8,128)S(1)} custom-call(f32[128,128]{1,0:T(8,128)S(1)} %cholesky.115), custom_call_target="Cholesky" | custom-call | tf_op jit(solution)/shard_map/jit(cholesky)/cholesky | solution.py:71
  498.0 9.8 %custom-call.21 = f32[1,128,128]{1,2,0:T(8,128)S(1)} custom-call(f32[1,128,128]{2,1,0:T(8,128)S(1)} %get-tuple-element.57), custom_call_target="InvertDiagBlocksLowerTriangular" | custom-call | tf_op jit(solution)/shard_map/jit(cholesky)/cholesky | solution.py:71
  508.3 11.7 %cholesky.103 = f32[128,128]{1,0:T(8,128)S(1)} custom-call(f32[128,128]{1,0:T(8,128)S(1)} %convolution_subtract_fusion.1), custom_call_target="Cholesky" | custom-call | tf_op jit(solution)/shard_map/jit(cholesky)/cholesky | solution.py:71
  528.0 20.7 %custom-call.22 = f32[2,128,128]{1,2,0:T(8,128)S(1)} custom-call(f32[2,128,128]{2,1,0:T(8,128)} %get-tuple-element.12), custom_call_target="InvertDiagBlocksLowerTriangular" | custom-call | tf_op jit(solution)/shard_map/jit(_solve_triangular)/triangular_solve | solution.py:72
  567.6 7.1 %add_bitcast_fusion = f32[3,256,8,256]{1,3,2,0:T(8,128)} fusion(f32[3,8,256]{2,1,0:T(8,128)S(1)} %broadcast_multiply_fusion.2, f32[1,256,8,256]{1,3,2,0:T(8,128)S(1)} %get-tuple-element.30, f32[1,256,8,256]{1,3,2,0:T(8,128)S(1)} %get-tuple-element.29, f32[1,256,8,256]{1,3,2,0:T(8,128)S(1)} %bitcast.145, f32[128,256]{1,0:T(8,128)S(1)} %fusion.48, ...), kind=kOutput, calls=%fused_computation.4 | convolution fusion | flops 4838260736 | bytes 12870656 | tf_op jit(solution)/shard_map/nm,cnab->cmab/dot_general | solution.py:77
  574.7 6.6 %copy.59 = f32[3,256,8,256]{3,2,1,0:T(8,128)} copy(f32[3,256,8,256]{1,3,2,0:T(8,128)} %add_bitcast_fusion) | data formatting | bytes 12582912 | tf_op jit(solution)/shard_map/add | solution.py:78
  (148 shorter events, 93.8 us)
Async XLA Ops:
  6.5 477.6 %all-reduce.3.cloned.1.call-start = ((), (), s32[]{:S(2)}) async-start(), calls=%async_computation | async-start | bytes 524288 | tf_op jit(solution)/shard_map/psum | solution.py:69
  26.3 55.2 %copy-start = (f32[1,256,8,256]{1,0,3,2:T(1,128)}, f32[1,256,8,256]{1,0,3,2:T(1,128)S(1)}, u32[]{:S(2)}) copy-start(f32[1,256,8,256]{1,0,3,2:T(1,128)S(1)} %broadcast_multiply_fusion) | copy-start | bytes 6291460
  27.2 24.0 %collective-permute-start = (f32[2,256,1,256]{1,0,3,2:T(2,128)S(1)}, f32[2,256,1,256]{1,0,3,2:T(2,128)S(1)}, u32[]{:S(2)}, u32[]{:S(2)}) collective-permute-start(f32[2,256,1,256]{1,0,3,2:T(2,128)S(1)} %get-tuple-element.44), channel_id=1, source_target_pairs={{0,1},{1,2},{2,3},{3,4},{4,5},{5,6},{6,7},{8,9},{9,10},{10,11},{11... | collective-permute-start | bytes 1572872 | tf_op jit(solution)/shard_map/ppermute | solution.py:16
  36.3 45.1 %collective-permute-start.1 = (f32[2,256,1,256]{1,0,3,2:T(2,128)S(1)}, f32[2,256,1,256]{1,0,3,2:T(2,128)S(1)}, u32[]{:S(2)}, u32[]{:S(2)}) collective-permute-start(f32[2,256,1,256]{1,0,3,2:T(2,128)S(1)} %get-tuple-element.45), channel_id=1, source_target_pairs={{1,0},{2,1},{3,2},{4,3},{5,4},{6,5},{7,6},{9,8},{10,9},{11,10},{12... | collective-permute-start | bytes 1572872 | tf_op jit(solution)/shard_map/ppermute | solution.py:17
  81.5 9.2 %collective-permute-start.2 = (f32[2,256,10,1]{1,0,3,2:T(2,128)S(1)}, f32[2,256,10,1]{1,0,3,2:T(2,128)S(1)}, u32[]{:S(2)}, u32[]{:S(2)}) collective-permute-start(f32[2,256,10,1]{1,0,3,2:T(2,128)S(1)} %get-tuple-element.40), channel_id=1, source_target_pairs={{0,8},{8,16},{16,24},{24,32},{32,40},{40,48},{48,56},{56,64},{64,7... | collective-permute-start | bytes 61448 | tf_op jit(solution)/shard_map/ppermute | solution.py:16
  81.6 9.2 %collective-permute-start.3 = (f32[2,256,10,1]{1,0,3,2:T(2,128)S(1)}, f32[2,256,10,1]{1,0,3,2:T(2,128)S(1)}, u32[]{:S(2)}, u32[]{:S(2)}) collective-permute-start(f32[2,256,10,1]{1,0,3,2:T(2,128)S(1)} %get-tuple-element.41), channel_id=1, source_target_pairs={{8,0},{16,8},{24,16},{32,24},{40,32},{48,40},{56,48},{64,56},{72,6... | collective-permute-start | bytes 61448 | tf_op jit(solution)/shard_map/ppermute | solution.py:17
  113.3 12.0 %copy-start.16 = (s32[1,1,256]{2,1,0:T(1,128)S(1)}, s32[1,1,256]{2,1,0:T(1,128)}, u32[]{:S(2)}) copy-start(s32[1,1,256]{2,1,0:T(1,128)} %param.8) | copy-start | bytes 3076
  113.9 29.0 %copy-start.2 = (f32[256,8,256]{0,2,1:T(8,128)}, f32[256,8,256]{0,2,1:T(8,128)S(1)}, u32[]{:S(2)}) copy-start(f32[256,8,256]{0,2,1:T(8,128)S(1)} %fusion.27) | copy-start | bytes 6291460
  114.0 22.0 %collective-permute-start.4 = (f32[1,256,1,256]{1,3,2,0:T(8,128)S(1)}, f32[1,256,1,256]{1,3,2,0:T(8,128)S(1)}, u32[]{:S(2)}, u32[]{:S(2)}) collective-permute-start(f32[1,256,1,256]{1,3,2,0:T(8,128)S(1)} %get-tuple-element.52), channel_id=1, source_target_pairs={{0,1},{1,2},{2,3},{3,4},{4,5},{5,6},{6,7},{8,9},{9,10},{10,11},{11... | collective-permute-start | bytes 786440 | tf_op jit(solution)/shard_map/ppermute | solution.py:16
  123.3 19.3 %collective-permute-start.5 = (f32[1,256,1,256]{1,3,2,0:T(8,128)S(1)}, f32[1,256,1,256]{1,3,2,0:T(8,128)S(1)}, u32[]{:S(2)}, u32[]{:S(2)}) collective-permute-start(f32[1,256,1,256]{1,3,2,0:T(8,128)S(1)} %get-tuple-element.53), channel_id=1, source_target_pairs={{1,0},{2,1},{3,2},{4,3},{5,4},{6,5},{7,6},{9,8},{10,9},{11,10},{12... | collective-permute-start | bytes 786440 | tf_op jit(solution)/shard_map/ppermute | solution.py:17
  144.4 12.4 %collective-permute-start.6 = (f32[1,256,10,1]{1,3,2,0:T(1,128)S(1)}, f32[1,256,10,1]{1,3,2,0:T(1,128)S(1)}, u32[]{:S(2)}, u32[]{:S(2)}) collective-permute-start(f32[1,256,10,1]{1,3,2,0:T(1,128)S(1)} %get-tuple-element.48), channel_id=1, source_target_pairs={{0,8},{8,16},{16,24},{24,32},{32,40},{40,48},{48,56},{56,64},{64,7... | collective-permute-start | bytes 30728 | tf_op jit(solution)/shard_map/ppermute | solution.py:16
  144.5 12.4 %collective-permute-start.7 = (f32[1,256,10,1]{1,3,2,0:T(1,128)S(1)}, f32[1,256,10,1]{1,3,2,0:T(1,128)S(1)}, u32[]{:S(2)}, u32[]{:S(2)}) collective-permute-start(f32[1,256,10,1]{1,3,2,0:T(1,128)S(1)} %get-tuple-element.49), channel_id=1, source_target_pairs={{8,0},{16,8},{24,16},{32,24},{40,32},{48,40},{56,48},{64,56},{72,6... | collective-permute-start | bytes 30728 | tf_op jit(solution)/shard_map/ppermute | solution.py:17
  150.3 9.3 %copy-start.18 = (f32[8]{0:T(128)}, f32[8]{0:T(128)S(1)}, u32[]{:S(2)}) copy-start(f32[8]{0:T(128)S(1)} %multiply_sine_fusion) | copy-start | bytes 100
  164.3 30.0 %copy-start.1 = (f32[1,256,8,256]{1,3,2,0:T(8,128)}, f32[1,256,8,256]{1,3,2,0:T(8,128)S(1)}, u32[]{:S(2)}) copy-start(f32[1,256,8,256]{1,3,2,0:T(8,128)S(1)} %get-tuple-element.27) | copy-start | bytes 6291460
  164.3 11.9 %copy-start.20 = (f32[1,1,256]{2,1,0:T(1,128)S(1)}, f32[1,1,256]{2,1,0:T(1,128)}, u32[]{:S(2)}) copy-start(f32[1,1,256]{2,1,0:T(1,128)} %param.11) | copy-start | bytes 3076
  164.4 29.9 %collective-permute-start.8 = (f32[2,256,1,256]{1,3,2,0:T(8,128)S(1)}, f32[2,256,1,256]{1,3,2,0:T(8,128)S(1)}, u32[]{:S(2)}, u32[]{:S(2)}) collective-permute-start(f32[2,256,1,256]{1,3,2,0:T(8,128)S(1)} %get-tuple-element.42), channel_id=1, source_target_pairs={{0,1},{1,2},{2,3},{3,4},{4,5},{5,6},{6,7},{8,9},{9,10},{10,11},{11... | collective-permute-start | bytes 1572872 | tf_op jit(solution)/shard_map/ppermute | solution.py:16
  170.8 23.5 %collective-permute-start.9 = (f32[2,256,1,256]{1,3,2,0:T(8,128)S(1)}, f32[2,256,1,256]{1,3,2,0:T(8,128)S(1)}, u32[]{:S(2)}, u32[]{:S(2)}) collective-permute-start(f32[2,256,1,256]{1,3,2,0:T(8,128)S(1)} %get-tuple-element.43), channel_id=1, source_target_pairs={{1,0},{2,1},{3,2},{4,3},{5,4},{6,5},{7,6},{9,8},{10,9},{11,10},{12... | collective-permute-start | bytes 1572872 | tf_op jit(solution)/shard_map/ppermute | solution.py:17
  194.4 21.6 %collective-permute-start.10 = (f32[2,256,10,1]{1,0,3,2:T(2,128)S(1)}, f32[2,256,10,1]{1,0,3,2:T(2,128)S(1)}, u32[]{:S(2)}, u32[]{:S(2)}) collective-permute-start(f32[2,256,10,1]{1,0,3,2:T(2,128)S(1)} %copy.49), channel_id=1, source_target_pairs={{0,8},{8,16},{16,24},{24,32},{32,40},{40,48},{48,56},{56,64},{64,7... | collective-permute-start | bytes 61448 | tf_op jit(solution)/shard_map/ppermute | solution.py:16
  194.5 21.5 %collective-permute-start.11 = (f32[2,256,10,1]{1,0,3,2:T(2,128)S(1)}, f32[2,256,10,1]{1,0,3,2:T(2,128)S(1)}, u32[]{:S(2)}, u32[]{:S(2)}) collective-permute-start(f32[2,256,10,1]{1,0,3,2:T(2,128)S(1)} %copy.50), channel_id=1, source_target_pairs={{8,0},{16,8},{24,16},{32,24},{40,32},{48,40},{56,48},{64,56},{72,6... | collective-permute-start | bytes 61448 | tf_op jit(solution)/shard_map/ppermute | solution.py:17
  224.2 298.6 %copy-start.22 = (s32[2]{0:T(128)S(1)}, s32[2]{0:T(128)}, u32[]{:S(2)}) copy-start(s32[2]{0:T(128)} %iota_multiply_fusion) | copy-start | bytes 28
  224.2 326.7 %collective-permute-start.12 = (f32[1,256,1,256]{1,3,2,0:T(8,128)}, f32[1,256,1,256]{1,3,2,0:T(8,128)S(1)}, u32[]{:S(2)}, u32[]{:S(2)}) collective-permute-start(f32[1,256,1,256]{1,3,2,0:T(8,128)} %get-tuple-element.50), channel_id=1, source_target_pairs={{0,1},{1,2},{2,3},{3,4},{4,5},{5,6},{6,7},{8,9},{9,10},{10,11},{11... | collective-permute-start | bytes 786440 | tf_op jit(solution)/shard_map/ppermute | solution.py:16
  231.5 319.4 %collective-permute-start.13 = (f32[1,256,1,256]{1,3,2,0:T(8,128)}, f32[1,256,1,256]{1,3,2,0:T(8,128)}, u32[]{:S(2)}, u32[]{:S(2)}) collective-permute-start(f32[1,256,1,256]{1,3,2,0:T(8,128)} %get-tuple-element.51), channel_id=1, source_target_pairs={{1,0},{2,1},{3,2},{4,3},{5,4},{6,5},{7,6},{9,8},{10,9},{11,10},{12... | collective-permute-start | bytes 786440 | tf_op jit(solution)/shard_map/ppermute | solution.py:17
  552.1 8.5 %collective-permute-start.14 = (f32[1,256,10,1]{1,3,2,0:T(1,128)S(1)}, f32[1,256,10,1]{1,3,2,0:T(1,128)S(1)}, u32[]{:S(2)}, u32[]{:S(2)}) collective-permute-start(f32[1,256,10,1]{1,3,2,0:T(1,128)S(1)} %get-tuple-element.46), channel_id=1, source_target_pairs={{0,8},{8,16},{16,24},{24,32},{32,40},{40,48},{48,56},{56,64},{64,7... | collective-permute-start | bytes 30728 | tf_op jit(solution)/shard_map/ppermute | solution.py:16
  552.2 8.4 %collective-permute-start.15 = (f32[1,256,10,1]{1,3,2,0:T(1,128)S(1)}, f32[1,256,10,1]{1,3,2,0:T(1,128)S(1)}, u32[]{:S(2)}, u32[]{:S(2)}) collective-permute-start(f32[1,256,10,1]{1,3,2,0:T(1,128)S(1)} %get-tuple-element.47), channel_id=1, source_target_pairs={{8,0},{16,8},{24,16},{32,24},{40,32},{48,40},{56,48},{64,56},{72,6... | collective-permute-start | bytes 30728 | tf_op jit(solution)/shard_map/ppermute | solution.py:17
  (16 other events, 30.3 us)
Sparse Core Ops, SparseCore 0:
  223.5 260.5 all-reduce.2
where the time goes:
time: 595 us; the launch traced here: 589 us
  waiting for transfers between devices  259 us (44%)
  other arithmetic  90.2 us (15%)
  blocking collectives  78.8 us (13%)
  starting transfers between devices  71.3 us (12%)
  local copies, waits for them, and re-layouts  61.1 us (10%)
  between operations  16.6 us (3%)
  matrix products  11.2 us (2%)
    psum x1, waiting for transfers between devices, shards(): gram, proj = lax.psum((gram, proj), ('lon', 'lat'))  168 us
    psum x1, blocking collectives, shards(): gram, proj = lax.psum((gram, proj), ('lon', 'lat'))  78.8 us
    ppermute x8, waiting for transfers between devices, with_halo(): before = lax.ppermute(last, axis, up)  54.7 us
    ppermute x8, starting transfers between devices, with_halo(): after = lax.ppermute(first, axis, down)  39 us
    ppermute x8, waiting for transfers between devices, with_halo(): after = lax.ppermute(first, axis, down)  37 us
    another operation x7, other arithmetic, shards(): lower = jnp.linalg.cholesky(gram + eye)  34.7 us
    ppermute x8, starting transfers between devices, with_halo(): before = lax.ppermute(last, axis, up)  32.3 us
    another operation x3, other arithmetic, shards(): inv_lower = jax.scipy.linalg.solve_triangular(lower, eye, lower=True)  21.3 us
  transfers between devices with their start and end apart: 17, of which 7 were waited for; matrix products, arithmetic and copies ran while one was open for 14% of the time, Pallas kernels for 0%

commit v1 on v0

v1 whole, which is shorter than its diff:
```python
import functools
import math

import jax
import jax.numpy as jnp
import numpy as np
from jax import lax
from jax.experimental import pallas as pl
from jax.experimental.pallas import tpu as pltpu
from jax.sharding import PartitionSpec as P

HI = lax.Precision.HIGHEST
CH = 8
PER = 8
ROWS = 8
COLS = 256
WIDE = 384
LANES = 128
EXT = 2 * COLS
BATH = EXT + 32
MSG = BATH + 8
VM = pltpu.VMEM


def roll(x, shift):
    return pltpu.roll(x, shift % x.shape[1], 1)


def ddx(x):
    return roll(x, -1) - roll(x, 1)


def lanes_of(shape):
    return lax.broadcasted_iota(jnp.int32, shape, 1)


def field_rows(lo, hi, c, q, i):
    rows = pl.ds(q * (CH * ROWS) + i, CH, stride=ROWS)
    return lo[c, rows, :], hi[c, rows, :]


def edges_kernel(lo, hi, bath, to_east, to_west, to_north, to_south):
    lane = lanes_of((CH, LANES))

    def chunk(q, carry):
        east = jnp.zeros((CH, LANES), jnp.float32)
        west = jnp.zeros((CH, LANES), jnp.float32)
        out = pl.ds(pl.multiple_of(q * CH, CH), CH)
        for c in range(4):
            for i in range(ROWS):
                if c < 3:
                    a, b = field_rows(lo, hi, c, q, i)
                else:
                    a = jnp.broadcast_to(bath[i : i + 1, :LANES], (CH, LANES))
                    b = jnp.broadcast_to(bath[i : i + 1, LANES:], (CH, LANES))
                spot = 4 * (c * ROWS + i)
                here = (lane >= spot) & (lane < spot + 4)
                west = jnp.where(here, roll(a, spot), west)
                east = jnp.where(here, roll(b, spot + 4), east)
        to_east[out, :] = east
        to_west[out, :] = west
        for i, ref in ((0, to_north), (ROWS - 1, to_south)):
            a, b = field_rows(lo, hi, 2, q, i)
            ref[out, :LANES] = a * bath[i : i + 1, :LANES]
            ref[out, LANES:] = b * bath[i : i + 1, LANES:]
        return carry

    lax.fori_loop(0, PER, chunk, 0)


def bath_rows(bath, from_east, from_west, wide_bath):
    lane = lanes_of((CH, LANES))
    e, w = from_east[0:CH, :], from_west[0:CH, :]
    for i in range(ROWS):
        spot = 4 * (3 * ROWS + i)
        tail = jnp.where(lane < 4, roll(e, -spot), roll(w, 124 - spot))
        wide_bath[i, :, :COLS] = jnp.broadcast_to(bath[i : i + 1, :], (CH, COLS))
        wide_bath[i, :, COLS:] = tail


def wide_rows(lo, hi, e, w, lane, q, c, i):
    a, b = field_rows(lo, hi, c, q, i)
    spot = 4 * (c * ROWS + i)
    tail = jnp.where(lane < 4, roll(e, -spot), roll(w, 124 - spot))
    return jnp.concatenate([a, b, tail], axis=1)


def border_kernel(nrows, lo, hi, bath, from_east, from_west, fcor, msg_n, msg_s, late_n, late_s, wide_bath):
    step = pl.program_id(0)
    base = lax.axis_index("lat") * nrows

    @pl.when(step == 0)
    def _():
        bath_rows(bath, from_east, from_west, wide_bath)
        for msg, r0, r1 in ((msg_n, 0, 1), (msg_s, ROWS - 1, ROWS - 2)):
            msg[EXT:MSG, :] = jnp.zeros((MSG - EXT, COLS), jnp.float32)
            msg[BATH : BATH + 1, :] = bath[r0 : r0 + 1, :]
            msg[BATH + 1 : BATH + 2, :] = bath[r1 : r1 + 1, :]
            msg[BATH + 2 : BATH + 3, :LANES] = wide_bath[r0, 0:1, COLS:]

    lane = lanes_of((CH, LANES))

    def chunk(q, carry):
        out = pl.ds(pl.multiple_of(q * CH, CH), CH)
        dst = pl.ds(pl.multiple_of(step * (CH * PER) + q * CH, CH), CH)
        dst_q = pl.ds(pl.multiple_of(COLS + step * (CH * PER) + q * CH, CH), CH)
        e, w = from_east[out, :], from_west[out, :]
        new = []
        for msg, late, first, sg, ext in (
            (msg_n, late_n, 0, 1, carry[0]),
            (msg_s, late_s, ROWS - 1, -1, carry[1]),
        ):
            rows = [first + sg * k for k in range(4)]
            H = [wide_bath[r] for r in rows]
            load = lambda c, k: wide_rows(lo, hi, e, w, lane, q, c, rows[k])
            h = [load(0, k) for k in range(3)]
            u = [load(1, k) for k in range(3)]
            v = [load(2, k) for k in range(4)]
            f0, f1 = fcor[base + rows[0]], fcor[base + rows[1]]
            fy = [H[k] * v[k] for k in range(4)]
            dfx = [ddx(H[k] * u[k]) for k in range(3)]
            h1a = h[1] - 0.25 * (dfx[1] + sg * (fy[2] - fy[0]))
            h1b = h[2] - 0.25 * (dfx[2] + sg * (fy[3] - fy[1]))
            part = h[0] - 0.25 * (dfx[0] + sg * fy[1])
            flux = H[0] * (v[0] - (0.5 * f0) * u[0] - (sg * 0.25) * h1a)
            uz = u[0] + (0.5 * f0) * v[0] - 0.25 * ddx(part)
            vz = v[1] - (0.5 * f1) * u[1] - (sg * 0.25) * (h1b - part)
            rest = part - 0.25 * (ddx(H[0] * uz) + sg * (H[1] * vz))
            msg[dst, :] = part[:, :COLS]
            msg[dst_q, :] = flux[:, :COLS]
            late[dst, :] = rest[:, :COLS]
            t = jnp.where(
                lane < 8,
                roll(fy[0][:, COLS:], 4),
                jnp.where(lane < 12, roll(part[:, COLS:], 10), roll(flux[:, COLS:], 14)),
            )
            t = pltpu.roll(t, q * 16, 1)
            new.append(jnp.where(lane // 16 == q, t, ext))
        return tuple(new)

    zero = jnp.zeros((CH, LANES), jnp.float32)
    exts = lax.fori_loop(0, PER, chunk, (zero, zero))
    for msg, ext in ((msg_n, exts[0]), (msg_s, exts[1])):
        msg[pl.ds(pl.multiple_of(EXT + step * CH, CH), CH), :LANES] = ext


def split(x, pieces):
    parts = []
    for k in range(pieces):
        p = x.astype(jnp.bfloat16)
        parts.append(p)
        if k + 1 < pieces:
            x = x - p.astype(jnp.float32)
    return parts


def dot(a, b, ca, cb):
    return lax.dot_general(
        a, b, (((ca,), (cb,)), ((), ())), precision=HI, preferred_element_type=jnp.float32
    )


def bdot(a, b):
    return jnp.dot(a, b, preferred_element_type=jnp.float32)


def forecast_kernel(
    nrows, ntiles, members, scale,
    lo, hi, bath, from_east, from_west, fcor, fy_n, fy_s, msg_n, msg_s, index, count, value, sd,
    out, sums, wide_bath, beyond, height,
):
    step = pl.program_id(0)
    tile = lax.axis_index("lat")
    base = tile * nrows
    has = (jnp.where(tile > 0, 1.0, 0.0), jnp.where(tile < ntiles - 1, 1.0, 0.0))

    @pl.when(step == 0)
    def _():
        bath_rows(bath, from_east, from_west, wide_bath)
        for k, msg in enumerate((msg_n, msg_s)):
            beyond[2 * k, :, :COLS] = jnp.broadcast_to(msg[BATH : BATH + 1, :], (CH, COLS))
            beyond[2 * k, :, COLS:] = jnp.broadcast_to(msg[BATH + 2 : BATH + 3, :LANES], (CH, LANES))
            beyond[2 * k + 1, :, :COLS] = jnp.broadcast_to(msg[BATH + 1 : BATH + 2, :], (CH, COLS))
            beyond[2 * k + 1, :, COLS:] = jnp.zeros((CH, LANES), jnp.float32)

    lane = lanes_of((CH, LANES))

    def chunk(q, carry):
        loc = pl.ds(pl.multiple_of(q * CH, CH), CH)
        dst = pl.ds(pl.multiple_of(step * (CH * PER) + q * CH, CH), CH)
        dst_q = pl.ds(pl.multiple_of(COLS + step * (CH * PER) + q * CH, CH), CH)
        e, w = from_east[loc, :], from_west[loc, :]
        load = lambda c, i: wide_rows(lo, hi, e, w, lane, q, c, i)
        H = [wide_bath[i] for i in range(ROWS)]
        f = [fcor[base + i] for i in range(ROWS)]
        h = [load(0, i) for i in range(ROWS)]
        u = [load(1, i) for i in range(ROWS)]
        v = [load(2, i) for i in range(ROWS)]
        ghost = []
        for msg, fy_msg in ((msg_n, fy_n), (msg_s, fy_s)):
            t = msg[pl.ds(pl.multiple_of(EXT + step * CH, CH), CH), :LANES]
            t = pltpu.roll(t, (LANES - q * 16) % LANES, 1)
            ghost.append((
                jnp.concatenate([fy_msg[loc, :], roll(t, -4)], axis=1),
                jnp.concatenate([msg[dst, :], roll(t, -10)], axis=1),
                jnp.concatenate([msg[dst_q, :], roll(t, -14)], axis=1),
            ))
        fy = [H[i] * v[i] for i in range(ROWS)]
        y = [ghost[0][0]] + fy + [ghost[1][0]]
        h1 = [h[i] - 0.25 * (ddx(H[i] * u[i]) + (y[i + 2] - y[i])) for i in range(ROWS)]
        eps = (-0.25 * fy[0], 0.25 * fy[-1])
        y = [has[0] * (ghost[0][1] + eps[0])] + h1 + [has[1] * (ghost[1][1] + eps[1])]
        u1 = [u[i] + (0.5 * f[i]) * v[i] - 0.25 * ddx(h1[i]) for i in range(ROWS)]
        v1 = [v[i] - (0.5 * f[i]) * u[i] - 0.25 * (y[i + 2] - y[i]) for i in range(ROWS)]
        fy = [H[i] * v1[i] for i in range(ROWS)]
        y = (
            [ghost[0][2] - 0.25 * (beyond[0] * h1[0])]
            + fy
            + [ghost[1][2] + 0.25 * (beyond[2] * h1[-1])]
        )
        h2 = [h1[i] - 0.25 * (ddx(H[i] * u1[i]) + (y[i + 2] - y[i])) for i in range(ROWS)]
        tail = []
        for k, sg, edge in ((0, -1, fy[0]), (1, 1, fy[-1])):
            bend = ddx(beyond[2 * k] * (-0.25 * ddx(eps[k])))
            tail.append(has[k] * (eps[k] - 0.25 * (bend - sg * edge + 0.25 * (beyond[2 * k + 1] * eps[k]))))
        y = [tail[0]] + h2 + [tail[1]]
        for i in range(ROWS):
            u2 = u1[i] + (0.5 * f[i]) * v1[i] - 0.25 * ddx(h2[i])
            v2 = v1[i] - (0.5 * f[i]) * u1[i] - 0.25 * (y[i + 2] - y[i])
            out[0, i, loc, :] = h2[i][:, :COLS]
            out[1, i, loc, :] = u2[:, :COLS]
            out[2, i, loc, :] = v2[:, :COLS]
            height[i, dst, :] = h2[i][:, :COLS]
        return carry

    lax.fori_loop(0, PER, chunk, 0)

    @pl.when(step == pl.num_programs(0) - 1)
    def _():
        slots = index.shape[1]
        sub = lax.broadcasted_iota(jnp.int32, (COLS, slots), 0)
        cell = jnp.broadcast_to(index[...], (COLS, slots))
        hx = jnp.zeros((members, slots), jnp.float32)
        for i in range(ROWS):
            pick = jnp.where(sub + i * COLS == cell, 1.0, 0.0).astype(jnp.bfloat16)
            for p in split(height[i], 3):
                hx = hx + bdot(p, pick)
        used = jnp.where(lanes_of((1, slots)) < count[0, 0], 1.0, 0.0)
        sigma = sd[...] * scale
        hmean = jnp.mean(hx, axis=0, keepdims=True)
        anom = (hx - hmean) * (used / (math.sqrt(members - 1) * sigma))
        innov = (value[...] - hmean) / sigma * used
        gram = dot(anom, anom, 1, 1)
        proj = dot(jnp.broadcast_to(innov, (8, slots)), anom, 1, 1)
        n = LANES
        ln, sb = lanes_of((n, n)), lax.broadcasted_iota(jnp.int32, (n, n), 0)
        last = gram[n:, n:]
        sums[0:n, :] = jnp.where(ln >= sb, gram[:n, :n], last)
        sums[n : 2 * n, :] = gram[:n, n:]
        sums[2 * n :, :] = jnp.zeros((16, n), jnp.float32)
        sums[2 * n : 2 * n + 1, :] = jnp.sum(jnp.where(ln == sb, last, 0.0), axis=0, keepdims=True)
        sums[2 * n + 1 : 2 * n + 2, :] = proj[0:1, :n]
        sums[2 * n + 2 : 2 * n + 3, :] = proj[0:1, n:]


def elim(a, dst, base):
    n = LANES
    groups = n // 8
    lane = lanes_of((8, n))
    sub = lax.broadcasted_iota(jnp.int32, (8, n), 0)
    A = [a[8 * g : 8 * g + 8, :] for g in range(groups)]
    X = [(lane == sub + 8 * g).astype(jnp.float32) for g in range(groups)]

    def body(it, carry):
        A, X = list(carry[:groups]), list(carry[groups:])
        for k in range(8):
            d = jnp.broadcast_to(A[0][k : k + 1, k : k + 1], (1, n))
            inv = 1.0 / d
            ra = A[0][k : k + 1, :] * inv
            rx = X[0][k : k + 1, :] * inv
            for g in range(groups):
                col = jnp.broadcast_to(A[g][:, k : k + 1], (8, n))
                if g == 0:
                    below = sub > k
                    scaled = jnp.where(sub == k, X[0] * lax.rsqrt(d), X[0])
                    A[0] = jnp.where(below, A[0] - col * ra, A[0])
                    X[0] = jnp.where(below, X[0] - col * rx, scaled)
                else:
                    A[g] = A[g] - col * ra
                    X[g] = X[g] - col * rx
        dst[pl.ds(pl.multiple_of(base + it * 8, 8), 8), :] = X[0]
        z = jnp.zeros((8, n), jnp.float32)
        A = [roll(A[g], -8) for g in range(1, groups)] + [z]
        return tuple(A) + tuple(X[1:]) + (z,)

    lax.fori_loop(0, groups, body, tuple(A) + tuple(X))


def factor_kernel(members, g_ref, mix, inverse):
    n = LANES
    lane, sub = lanes_of((n, n)), lax.broadcasted_iota(jnp.int32, (n, n), 0)
    both = g_ref[0:n, :]
    g12 = g_ref[n : 2 * n, :]
    tail = g_ref[2 * n : 2 * n + 8, :]
    eye = (lane == sub).astype(jnp.float32)
    up = jnp.where(lane >= sub, both, 0.0)
    low = jnp.where(lane < sub, both, 0.0)
    g11 = up + jnp.where(lane > sub, up, 0.0).T + eye
    g22 = low + low.T + jnp.where(lane == sub, jnp.broadcast_to(tail[0:1, :], (n, n)), 0.0) + eye
    elim(g11, inverse, 0)
    x11 = inverse[0:n, :]
    y12 = dot(x11, g12, 1, 0)
    elim(g22 - dot(y12, y12, 0, 0), inverse, n)
    x22 = inverse[n : 2 * n, :]
    x21 = -dot(x22, dot(y12, x11, 0, 0), 1, 0)
    p1 = jnp.broadcast_to(tail[1:2, :], (8, n))
    p2 = jnp.broadcast_to(tail[2:3, :], (8, n))
    q1 = dot(p1, x11, 1, 1)
    q2 = dot(p1, x21, 1, 1) + dot(p2, x22, 1, 1)
    c = 1.0 / math.sqrt(members - 1)
    w1 = (dot(q1, x11, 1, 0) + dot(q2, x21, 1, 0))[0:1, :] * c
    w2 = dot(q2, x22, 1, 0)[0:1, :] * c
    ws = jnp.sum(w1, axis=1, keepdims=True) + jnp.sum(w2, axis=1, keepdims=True)
    r = 1.0 / members
    s1 = (1.0 - ws - jnp.sum(x11, axis=1, keepdims=True)) * r
    s2 = (1.0 - ws - jnp.sum(x21, axis=1, keepdims=True) - jnp.sum(x22, axis=1, keepdims=True)) * r
    mix[0:n, 0:n] = x11 + (w1 + s1)
    mix[0:n, n:] = w2 + s1
    mix[n:, 0:n] = x21 + (w1 + s2)
    mix[n:, n:] = x22 + (w2 + s2)


def apply_kernel(mix, fields, late_n, late_s, out):
    high, low = split(mix[...], 2)
    wind = jnp.where(pl.program_id(0) == 2, 0.25, 0.0)
    for i in range(ROWS):
        x = fields[0, i]
        if i == 0:
            x = x + wind * late_n[...]
        if i == ROWS - 1:
            x = x - wind * late_s[...]
        a, b = split(x, 2)
        res = bdot(high, a) + (bdot(high, b) + bdot(low, a))
        out[0, pl.ds(i, x.shape[0], stride=ROWS), :] = res


def whole(shape):
    return pl.BlockSpec(shape, lambda *_: (0,) * len(shape))


def f32(*shape):
    return jax.ShapeDtypeStruct(shape, jnp.float32)


def flips(n, bit):
    return [(i, i ^ bit) for i in range(n)]


def bits(n):
    return [1 << k for k in range(n.bit_length() - 1)]


def total(x):
    nlon, nlat = lax.axis_size("lon"), lax.axis_size("lat")
    half = x.reshape(2, x.shape[0] // 2, x.shape[1])
    core = lax.axis_index("lon") % 2
    mine = lax.dynamic_index_in_dim(half, core, 0, keepdims=False)
    theirs = lax.dynamic_index_in_dim(half, 1 - core, 0, keepdims=False)
    y = mine + lax.ppermute(theirs, "lon", flips(nlon, 1))
    stages = []
    for axis, n, todo in (("lon", nlon, bits(nlon)[1:]), ("lat", nlat, bits(nlat)[1:] + bits(nlat)[:1])):
        for k in range(0, len(todo), 2):
            stages.append((axis, n, todo[k : k + 2]))
    for axis, n, todo in stages:
        hops = todo if len(todo) == 1 else [todo[0], todo[1], todo[0] | todo[1]]
        parts = [lax.ppermute(y, axis, flips(n, b)) for b in hops]
        for p in parts:
            y = y + p
    other = lax.ppermute(y, "lon", flips(nlon, 1))
    lo = jnp.where(core == 0, y, other)
    hi = jnp.where(core == 0, other, y)
    return jnp.concatenate([lo, hi], axis=0)


def shards(state, bathymetry, obs_index, obs_count, obs_value, obs_sd):
    members = state.shape[1]
    nlat, nlon = lax.axis_size("lat"), lax.axis_size("lon")
    slots = obs_index.shape[2]
    total_rows = ROWS * nlat
    fcor = np.sin(math.pi / 3.0 * ((np.arange(total_rows) + 0.5) / total_rows - 0.5)).astype(np.float32)
    flat = state.reshape(3, members * ROWS, COLS)
    blk = CH * PER
    grid = (members // blk,)
    state_specs = [
        pl.BlockSpec((3, blk * ROWS, LANES), lambda s: (0, s, 0)),
        pl.BlockSpec((3, blk * ROWS, LANES), lambda s: (0, s, 1)),
    ]
    thin = pl.BlockSpec((blk, LANES), lambda s: (s, 0))
    row = pl.BlockSpec((blk, COLS), lambda s: (s, 0))
    bath_spec = whole((ROWS, COLS))
    smem = pl.BlockSpec(memory_space=pltpu.SMEM)

    to_east, to_west, to_north, to_south = pl.pallas_call(
        edges_kernel,
        grid=grid,
        in_specs=state_specs + [bath_spec],
        out_specs=[thin, thin, row, row],
        out_shape=[f32(members, LANES)] * 2 + [f32(members, COLS)] * 2,
        name="edges",
    )(flat, flat, bathymetry)

    east = [(i, (i + 1) % nlon) for i in range(nlon)]
    west = [(j, i) for i, j in east]
    south = [(i, i + 1) for i in range(nlat - 1)]
    north = [(j, i) for i, j in south]
    from_west = lax.ppermute(to_east, "lon", east)
    from_east = lax.ppermute(to_west, "lon", west)
    fy_n = lax.ppermute(to_south, "lat", south)
    fy_s = lax.ppermute(to_north, "lat", north)

    msg_n, msg_s, late_n, late_s = pl.pallas_call(
        functools.partial(border_kernel, ROWS),
        grid=grid,
        in_specs=state_specs + [bath_spec, thin, thin, smem],
        out_specs=[whole((MSG, COLS))] * 2 + [whole((members, COLS))] * 2,
        out_shape=[f32(MSG, COLS)] * 2 + [f32(members, COLS)] * 2,
        scratch_shapes=[VM((ROWS, CH, WIDE), jnp.float32)],
        name="border",
    )(flat, flat, bathymetry, from_east, from_west, fcor)
    got_n = lax.ppermute(msg_s, "lat", south)
    got_s = lax.ppermute(msg_n, "lat", north)

    one = lambda x: x.reshape(1, slots)
    obs = whole((1, slots))
    fields, sums = pl.pallas_call(
        functools.partial(forecast_kernel, ROWS, nlat, members, math.sqrt(slots * nlat * nlon) / 16.0),
        grid=grid,
        in_specs=state_specs
        + [bath_spec, thin, thin, smem, row, row, whole((MSG, COLS)), whole((MSG, COLS))]
        + [obs, smem, obs, obs],
        out_specs=[pl.BlockSpec((3, ROWS, blk, COLS), lambda s: (0, 0, s, 0)), whole((272, LANES))],
        out_shape=[f32(3, ROWS, members, COLS), f32(272, LANES)],
        scratch_shapes=[
            VM((ROWS, CH, WIDE), jnp.float32),
            VM((4, CH, WIDE), jnp.float32),
            VM((ROWS, members, COLS), jnp.float32),
        ],
        name="forecast",
    )(
        flat, flat, bathymetry, from_east, from_west, fcor, fy_n, fy_s, got_n, got_s,
        one(obs_index), obs_count, one(obs_value), one(obs_sd),
    )

    sums, late_n, late_s = lax.optimization_barrier((sums, late_n, late_s))
    late_from_n = lax.ppermute(late_s, "lat", south)
    late_from_s = lax.ppermute(late_n, "lat", north)
    sums = total(sums)

    mix = pl.pallas_call(
        functools.partial(factor_kernel, members),
        out_shape=f32(members, members),
        in_specs=[pl.BlockSpec(memory_space=VM)],
        out_specs=pl.BlockSpec(memory_space=VM),
        scratch_shapes=[VM((members, LANES), jnp.float32)],
        name="factor",
    )(sums)

    half = pl.BlockSpec((members, LANES), lambda c, j: (0, j))
    analysis = pl.pallas_call(
        apply_kernel,
        grid=(3, COLS // LANES),
        in_specs=[
            whole((members, members)),
            pl.BlockSpec((1, ROWS, members, LANES), lambda c, j: (c, 0, 0, j)),
            half,
            half,
        ],
        out_specs=pl.BlockSpec((1, members * ROWS, LANES), lambda c, j: (c, 0, j)),
        out_shape=f32(3, members * ROWS, COLS),
        name="mix",
    )(mix, fields, late_from_n, late_from_s)
    return analysis.reshape(state.shape)


def solution(mesh):
    return jax.shard_map(
        shards,
        mesh=mesh,
        in_specs=(
            P(None, None, "lat", "lon"),
            P("lat", "lon"),
            P("lat", "lon", None),
            P("lat", "lon"),
            P("lat", "lon", None),
            P("lat", "lon", None),
        ),
        out_specs=P(None, None, "lat", "lon"),
        check_vma=False,
    )
```

time: 595 us -> 217 us (0.36)
  waiting for transfers between devices: 259 us -> 75.1 us
  other arithmetic: 90.2 us -> 1.66 us
  blocking collectives: 78.8 us -> 0 us
  Pallas kernels: 0 us -> 77.9 us
  local copies, waits for them, and re-layouts: 61.1 us -> 3.38 us
  between operations: 16.6 us -> 0.84 us
  starting transfers between devices: 71.3 us -> 57.1 us
  matrix products: 11.2 us -> 0 us
    psum x1 -> x0, waiting for transfers between devices: 168 us -> none  [shards(): gram, proj = lax.psum((gram, proj), ('lon', 'lat'))]
    psum x1 -> x0, blocking collectives: 78.8 us -> none  [shards(): gram, proj = lax.psum((gram, proj), ('lon', 'lat'))]
    pallas_call x0 -> x5, Pallas kernels: none -> 77.9 us  [the longest x1 27.5 us: shards(): pl.pallas_call(functools.partial(factor_kernel, members), out_shape=f32(m...]
    another operation x12 -> x0, other arithmetic: 59.9 us -> none  [the longest x7 34.7 us: shards(): lower = jnp.linalg.cholesky(gram + eye)]
    unnamed x52 -> x24, local copies, waits for them, and re-layouts: 20.5 us -> 2.49 us
    concatenate x6 -> x1, other arithmetic: 18.5 us -> 0.67 us  [total(): return jnp.concatenate([lo, hi], axis=0)]
    slice x8 -> x0, local copies, waits for them, and re-layouts: 17 us -> none  [the longest x1 10.4 us: new_height(): flux[0][:, 1:-1, 2:] - flux[0][:, 1:-1, :-2] + flux[1][:, 2:, 1:-1]]
    ppermute x16 -> x20, waiting for transfers between devices: 91.6 us -> 75.1 us  [the longest x1 42.9 us: shards(): fy_n = lax.ppermute(to_south, 'lat', south)]
  transfers between devices with their start and end apart: 17 -> 20, of which waited for: 7 -> 12; matrix products, arithmetic and copies ran while one was open for 14% -> 0% of each run, Pallas kernels for 0% -> 13%
where the time goes in v1:
time: 217 us; the launch traced here: 216 us
  Pallas kernels  77.9 us (36%)
  waiting for transfers between devices  75.1 us (35%)
  starting transfers between devices  57.1 us (26%)
  local copies, waits for them, and re-layouts  3.38 us (2%)
    ppermute x1, waiting for transfers between devices, shards(): fy_n = lax.ppermute(to_south, 'lat', south)  42.9 us
    pallas_call x1, Pallas kernels, shards(): pl.pallas_call(functools.partial(factor_kernel, members), out_shape=f32(m...  27.5 us
    pallas_call x1, Pallas kernels, shards(): pl.pallas_call(functools.partial(forecast_kernel, ROWS, nlat, members, ma...  20.9 us
    ppermute x10, starting transfers between devices, total(): parts = [lax.ppermute(y, axis, flips(n, b)) for b in hops]  18.6 us
    ppermute x10, waiting for transfers between devices, total(): parts = [lax.ppermute(y, axis, flips(n, b)) for b in hops]  14.3 us
    pallas_call x1, Pallas kernels, shards(): pl.pallas_call(functools.partial(border_kernel, ROWS), grid=grid, in_spec...  12.6 us
    pallas_call x1, Pallas kernels, shards(): pl.pallas_call(apply_kernel, grid=(3, COLS // LANES), in_specs=[whole((me...  9.91 us
    ppermute x1, waiting for transfers between devices, shards(): fy_s = lax.ppermute(to_north, 'lat', north)  8.17 us
  transfers between devices with their start and end apart: 20, of which 12 were waited for; matrix products, arithmetic and copies ran while one was open for 0% of the time, Pallas kernels for 13%

profile of v1, /device:TPU:8, one launch (start us, length us, event | category | flops | bytes accessed | tf_op | source)
XLA Modules:
  0.0 216.0 jit_solution(3247520950823367198)
XLA Ops:
  0.0 7.0 %edges.1 = (f32[256,128]{1,0:T(8,128)}, f32[256,128]{1,0:T(8,128)}, f32[256,256]{1,0:T(8,128)}, f32[256,256]{1,0:T(8,128)}) custom-call(f32[3,2048,256]{2,1,0:T(8,128)} %bitcast.10, f32[3,2048,256]{2,1,0:T(8,128)} %bitcast.11, f32[8,256]{1,0:T(8,128)} %bath.5), custom_call_target="tpu_custom_call" | custom-call | tf_op jit(solution)/shard_map/edges/pallas_call | solution.py:403
  7.0 6.3 %collective-permute-start = (f32[256,128]{1,0:T(8,128)}, f32[256,128]{1,0:T(8,128)S(1)}, u32[]{:S(2)}, u32[]{:S(2)}) collective-permute-start(f32[256,128]{1,0:T(8,128)} %get-tuple-element.18), channel_id=1, source_target_pairs={{8,0},{16,8},{24,16},{32,24},{40,32},{48,40},{56,48},{64,56},{72,6... | collective-permute-start | bytes 393224 | tf_op jit(solution)/shard_map/ppermute | solution.py:417
  13.3 2.8 %collective-permute-done.from_east = f32[256,128]{1,0:T(8,128)S(1)} collective-permute-done((f32[256,128]{1,0:T(8,128)}, f32[256,128]{1,0:T(8,128)S(1)}, u32[]{:S(2)}, u32[]{:S(2)}) %collective-permute-start) | collective-permute-done | bytes 131104 | tf_op jit(solution)/shard_map/ppermute | solution.py:417
  16.1 5.7 %collective-permute-done.1.from_west = f32[256,128]{1,0:T(8,128)S(1)} collective-permute-done((f32[256,128]{1,0:T(8,128)}, f32[256,128]{1,0:T(8,128)S(1)}, u32[]{:S(2)}, u32[]{:S(2)}) %collective-permute-start.1) | collective-permute-done | bytes 131104 | tf_op jit(solution)/shard_map/ppermute | solution.py:416
  22.4 12.6 %border.1 = (f32[552,256]{1,0:T(8,128)}, f32[552,256]{1,0:T(8,128)}, f32[256,256]{1,0:T(8,128)}, f32[256,256]{1,0:T(8,128)}) custom-call(f32[3,2048,256]{2,1,0:T(8,128)} %bitcast.12, f32[3,2048,256]{2,1,0:T(8,128)} %bitcast.13, f32[8,256]{1,0:T(8,128)} %bath.5, f32[256,128]{1,0:T(8,128)} %copy-done.2, f32[256,128]{1,0:T(8,128)} %copy-done.3, ...), custom_call_target="tpu_custom_call" | custom-call | tf_op jit(solution)/shard_map/border/pallas_call | solution.py:421
  35.0 6.4 %collective-permute-start.4 = (f32[552,256]{1,0:T(8,128)}, f32[552,256]{1,0:T(8,128)S(1)}, u32[]{:S(2)}, u32[]{:S(2)}) collective-permute-start(f32[552,256]{1,0:T(8,128)} %get-tuple-element.22), channel_id=1, source_target_pairs={{0,1},{1,2},{2,3},{3,4},{4,5},{5,6},{6,7},{8,9},{9,10},{10,11},{11... | collective-permute-start | bytes 1695752 | tf_op jit(solution)/shard_map/ppermute | solution.py:430
  41.4 4.2 %collective-permute-start.5 = (f32[552,256]{1,0:T(8,128)}, f32[552,256]{1,0:T(8,128)S(1)}, u32[]{:S(2)}, u32[]{:S(2)}) collective-permute-start(f32[552,256]{1,0:T(8,128)} %get-tuple-element.23), channel_id=1, source_target_pairs={{1,0},{2,1},{3,2},{4,3},{5,4},{6,5},{7,6},{9,8},{10,9},{11,10},{12... | collective-permute-start | bytes 1695752 | tf_op jit(solution)/shard_map/ppermute | solution.py:431
  45.7 5.5 %collective-permute-start.2 = (f32[256,256]{1,0:T(8,128)S(1)}, f32[256,256]{1,0:T(8,128)S(1)}, u32[]{:S(2)}, u32[]{:S(2)}) collective-permute-start(f32[256,256]{1,0:T(8,128)S(1)} %copy-done.11), channel_id=1, source_target_pairs={{0,1},{1,2},{2,3},{3,4},{4,5},{5,6},{6,7},{8,9},{9,10},{10,11},{11... | collective-permute-start | bytes 786440 | tf_op jit(solution)/shard_map/ppermute | solution.py:418
  51.2 5.1 %collective-permute-start.3 = (f32[256,256]{1,0:T(8,128)S(1)}, f32[256,256]{1,0:T(8,128)S(1)}, u32[]{:S(2)}, u32[]{:S(2)}) collective-permute-start(f32[256,256]{1,0:T(8,128)S(1)} %copy-done.10), channel_id=1, source_target_pairs={{1,0},{2,1},{3,2},{4,3},{5,4},{6,5},{7,6},{9,8},{10,9},{11,10},{12... | collective-permute-start | bytes 786440 | tf_op jit(solution)/shard_map/ppermute | solution.py:419
  57.0 42.9 %collective-permute-done.2.fy_n = f32[256,256]{1,0:T(8,128)S(1)} collective-permute-done((f32[256,256]{1,0:T(8,128)S(1)}, f32[256,256]{1,0:T(8,128)S(1)}, u32[]{:S(2)}, u32[]{:S(2)}) %collective-permute-start.2) | collective-permute-done | bytes 262176 | tf_op jit(solution)/shard_map/ppermute | solution.py:418
  99.9 8.2 %collective-permute-done.3.fy_s = f32[256,256]{1,0:T(8,128)S(1)} collective-permute-done((f32[256,256]{1,0:T(8,128)S(1)}, f32[256,256]{1,0:T(8,128)S(1)}, u32[]{:S(2)}, u32[]{:S(2)}) %collective-permute-start.3) | collective-permute-done | bytes 262176 | tf_op jit(solution)/shard_map/ppermute | solution.py:419
  109.1 20.9 %forecast.1 = (f32[3,8,256,256]{3,2,1,0:T(8,128)}, f32[272,128]{1,0:T(8,128)}) custom-call(f32[3,2048,256]{2,1,0:T(8,128)} %bitcast.14, f32[3,2048,256]{2,1,0:T(8,128)} %bitcast.15, f32[8,256]{1,0:T(8,128)} %bath.5, f32[256,128]{1,0:T(8,128)} %copy-done.2, f32[256,128]{1,0:T(8,128)} %copy-done.3, f32[64]{0:T(128)} %constant.31.clone.fcor, ...), custom_call_target="tpu_custom_call" | custom-call | tf_op jit(solution)/shard_map/forecast/pallas_call | solution.py:435
  133.1 2.7 %collective-permute-start.9 = (f32[136,128]{1,0:T(8,128)S(1)}, f32[136,128]{1,0:T(8,128)S(1)}, u32[]{:S(2)}, u32[]{:S(2)}) collective-permute-start(f32[136,128]{1,0:T(8,128)S(1)} %bitcast_add_fusion), channel_id=1, source_target_pairs={{0,48},{8,56},{16,32},{24,40},{32,16},{40,24},{48,0},{56,8},{64,11... | collective-permute-start | bytes 208904 | tf_op jit(solution)/shard_map/ppermute | solution.py:376
  137.6 2.5 %collective-permute-done.9 = f32[136,128]{1,0:T(8,128)S(1)} collective-permute-done((f32[136,128]{1,0:T(8,128)S(1)}, f32[136,128]{1,0:T(8,128)S(1)}, u32[]{:S(2)}, u32[]{:S(2)}) %collective-permute-start.9) | collective-permute-done | bytes 69664 | tf_op jit(solution)/shard_map/ppermute | solution.py:376
  142.3 2.2 %collective-permute-start.12 = (f32[136,128]{1,0:T(8,128)S(1)}, f32[136,128]{1,0:T(8,128)S(1)}, u32[]{:S(2)}, u32[]{:S(2)}) collective-permute-start(f32[136,128]{1,0:T(8,128)S(1)} %add_add_fusion.2), channel_id=1, source_target_pairs={{0,192},{8,200},{16,208},{24,216},{32,224},{40,232},{48,240},{56,2... | collective-permute-start | bytes 208904 | tf_op jit(solution)/shard_map/ppermute | solution.py:376
  147.9 2.4 %collective-permute-done.11 = f32[136,128]{1,0:T(8,128)S(1)} collective-permute-done((f32[136,128]{1,0:T(8,128)S(1)}, f32[136,128]{1,0:T(8,128)S(1)}, u32[]{:S(2)}, u32[]{:S(2)}) %collective-permute-start.11) | collective-permute-done | bytes 69664 | tf_op jit(solution)/shard_map/ppermute | solution.py:376
  151.9 2.6 %collective-permute-start.13 = (f32[136,128]{1,0:T(8,128)S(1)}, f32[136,128]{1,0:T(8,128)S(1)}, u32[]{:S(2)}, u32[]{:S(2)}) collective-permute-start(f32[136,128]{1,0:T(8,128)S(1)} %add_add_fusion.1), channel_id=1, source_target_pairs={{0,2},{1,3},{2,0},{3,1},{4,6},{5,7},{6,4},{7,5},{8,10},{9,11},{10,... | collective-permute-start | bytes 208904 | tf_op jit(solution)/shard_map/ppermute | solution.py:376
  155.5 2.3 %collective-permute-done.14 = f32[136,128]{1,0:T(8,128)S(1)} collective-permute-done((f32[136,128]{1,0:T(8,128)S(1)}, f32[136,128]{1,0:T(8,128)S(1)}, u32[]{:S(2)}, u32[]{:S(2)}) %collective-permute-start.14) | collective-permute-done | bytes 69664 | tf_op jit(solution)/shard_map/ppermute | solution.py:376
  157.8 5.7 %collective-permute-start.16 = (f32[136,128]{1,0:T(8,128)S(1)}, f32[136,128]{1,0:T(8,128)S(1)}, u32[]{:S(2)}, u32[]{:S(2)}) collective-permute-start(f32[136,128]{1,0:T(8,128)S(1)} %add_add_fusion), channel_id=1, source_target_pairs={{0,1},{1,0},{2,3},{3,2},{4,5},{5,4},{6,7},{7,6},{8,9},{9,8},{10,11... | collective-permute-start | bytes 208904 | tf_op jit(solution)/shard_map/ppermute | solution.py:376
  163.5 2.6 %collective-permute-done.16 = f32[136,128]{1,0:T(8,128)S(1)} collective-permute-done((f32[136,128]{1,0:T(8,128)S(1)}, f32[136,128]{1,0:T(8,128)S(1)}, u32[]{:S(2)}, u32[]{:S(2)}) %collective-permute-start.16) | collective-permute-done | bytes 69664 | tf_op jit(solution)/shard_map/ppermute | solution.py:376
  166.3 7.5 %collective-permute-start.18 = (f32[256,256]{1,0:T(8,128)S(1)}, f32[256,256]{1,0:T(8,128)S(1)}, u32[]{:S(2)}, u32[]{:S(2)}) collective-permute-start(f32[256,256]{1,0:T(8,128)S(1)} %copy-done.9), channel_id=1, source_target_pairs={{0,1},{1,2},{2,3},{3,4},{4,5},{5,6},{6,7},{8,9},{9,10},{10,11},{11... | collective-permute-start | bytes 786440 | tf_op jit(solution)/shard_map/ppermute | solution.py:455
  173.8 3.3 %collective-permute-start.19 = (f32[256,256]{1,0:T(8,128)S(1)}, f32[256,256]{1,0:T(8,128)S(1)}, u32[]{:S(2)}, u32[]{:S(2)}) collective-permute-start(f32[256,256]{1,0:T(8,128)S(1)} %copy-done.8), channel_id=1, source_target_pairs={{1,0},{2,1},{3,2},{4,3},{5,4},{6,5},{7,6},{9,8},{10,9},{11,10},{12... | collective-permute-start | bytes 786440 | tf_op jit(solution)/shard_map/ppermute | solution.py:456
  177.8 27.5 %factor.1.mix = f32[256,256]{1,0:T(8,128)} custom-call(f32[272,128]{1,0:T(8,128)} %pad_maximum_fusion.g_ref), custom_call_target="tpu_custom_call" | custom-call | tf_op jit(solution)/shard_map/factor/pallas_call | solution.py:459
  206.1 9.9 %mix.1 = f32[3,2048,256]{2,1,0:T(8,128)} custom-call(f32[256,256]{1,0:T(8,128)} %factor.1.mix, f32[3,8,256,256]{3,2,1,0:T(8,128)} %get-tuple-element.28.fields, f32[256,256]{1,0:T(8,128)} %copy-done.6, f32[256,256]{1,0:T(8,128)} %copy-done.7), custom_call_target="tpu_custom_call" | custom-call | tf_op jit(solution)/shard_map/mix/pallas_call | solution.py:469
  (53 shorter events, 16.3 us)
Async XLA Ops:
  7.0 9.1 %collective-permute-start = (f32[256,128]{1,0:T(8,128)}, f32[256,128]{1,0:T(8,128)S(1)}, u32[]{:S(2)}, u32[]{:S(2)}) collective-permute-start(f32[256,128]{1,0:T(8,128)} %get-tuple-element.18), channel_id=1, source_target_pairs={{8,0},{16,8},{24,16},{32,24},{40,32},{48,40},{56,48},{64,56},{72,6... | collective-permute-start | bytes 393224 | tf_op jit(solution)/shard_map/ppermute | solution.py:417
  13.3 32.4 %copy-start.11 = (f32[256,256]{1,0:T(8,128)S(1)}, f32[256,256]{1,0:T(8,128)}, u32[]{:S(2)}) copy-start(f32[256,256]{1,0:T(8,128)} %get-tuple-element.20) | copy-start | bytes 786436
  13.3 37.9 %copy-start.10 = (f32[256,256]{1,0:T(8,128)S(1)}, f32[256,256]{1,0:T(8,128)}, u32[]{:S(2)}) copy-start(f32[256,256]{1,0:T(8,128)} %get-tuple-element.21) | copy-start | bytes 786436
  13.3 8.5 %collective-permute-start.1 = (f32[256,128]{1,0:T(8,128)}, f32[256,128]{1,0:T(8,128)S(1)}, u32[]{:S(2)}, u32[]{:S(2)}) collective-permute-start(f32[256,128]{1,0:T(8,128)} %get-tuple-element.19), channel_id=1, source_target_pairs={{0,8},{8,16},{16,24},{24,32},{32,40},{40,48},{48,56},{56,64},{64,7... | collective-permute-start | bytes 393224 | tf_op jit(solution)/shard_map/ppermute | solution.py:416
  35.0 73.0 %collective-permute-start.4 = (f32[552,256]{1,0:T(8,128)}, f32[552,256]{1,0:T(8,128)S(1)}, u32[]{:S(2)}, u32[]{:S(2)}) collective-permute-start(f32[552,256]{1,0:T(8,128)} %get-tuple-element.22), channel_id=1, source_target_pairs={{0,1},{1,2},{2,3},{3,4},{4,5},{5,6},{6,7},{8,9},{9,10},{10,11},{11... | collective-permute-start | bytes 1695752 | tf_op jit(solution)/shard_map/ppermute | solution.py:430
  41.4 66.6 %collective-permute-start.5 = (f32[552,256]{1,0:T(8,128)}, f32[552,256]{1,0:T(8,128)S(1)}, u32[]{:S(2)}, u32[]{:S(2)}) collective-permute-start(f32[552,256]{1,0:T(8,128)} %get-tuple-element.23), channel_id=1, source_target_pairs={{1,0},{2,1},{3,2},{4,3},{5,4},{6,5},{7,6},{9,8},{10,9},{11,10},{12... | collective-permute-start | bytes 1695752 | tf_op jit(solution)/shard_map/ppermute | solution.py:431
  45.7 54.2 %collective-permute-start.2 = (f32[256,256]{1,0:T(8,128)S(1)}, f32[256,256]{1,0:T(8,128)S(1)}, u32[]{:S(2)}, u32[]{:S(2)}) collective-permute-start(f32[256,256]{1,0:T(8,128)S(1)} %copy-done.11), channel_id=1, source_target_pairs={{0,1},{1,2},{2,3},{3,4},{4,5},{5,6},{6,7},{8,9},{9,10},{10,11},{11... | collective-permute-start | bytes 786440 | tf_op jit(solution)/shard_map/ppermute | solution.py:418
  51.2 56.9 %collective-permute-start.3 = (f32[256,256]{1,0:T(8,128)S(1)}, f32[256,256]{1,0:T(8,128)S(1)}, u32[]{:S(2)}, u32[]{:S(2)}) collective-permute-start(f32[256,256]{1,0:T(8,128)S(1)} %copy-done.10), channel_id=1, source_target_pairs={{1,0},{2,1},{3,2},{4,3},{5,4},{6,5},{7,6},{9,8},{10,9},{11,10},{12... | collective-permute-start | bytes 786440 | tf_op jit(solution)/shard_map/ppermute | solution.py:419
  109.1 57.1 %copy-start.9 = (f32[256,256]{1,0:T(8,128)S(1)}, f32[256,256]{1,0:T(8,128)}, u32[]{:S(2)}) copy-start(f32[256,256]{1,0:T(8,128)} %get-tuple-element.29) | copy-start | bytes 786436
  109.1 64.7 %copy-start.8 = (f32[256,256]{1,0:T(8,128)S(1)}, f32[256,256]{1,0:T(8,128)}, u32[]{:S(2)}) copy-start(f32[256,256]{1,0:T(8,128)} %get-tuple-element.30) | copy-start | bytes 786436
  131.0 1.3 collective-permute-start.6
  133.1 6.9 %collective-permute-start.9 = (f32[136,128]{1,0:T(8,128)S(1)}, f32[136,128]{1,0:T(8,128)S(1)}, u32[]{:S(2)}, u32[]{:S(2)}) collective-permute-start(f32[136,128]{1,0:T(8,128)S(1)} %bitcast_add_fusion), channel_id=1, source_target_pairs={{0,48},{8,56},{16,32},{24,40},{32,16},{40,24},{48,0},{56,8},{64,11... | collective-permute-start | bytes 208904 | tf_op jit(solution)/shard_map/ppermute | solution.py:376
  135.8 6.4 %collective-permute-start.8 = (f32[136,128]{1,0:T(8,128)S(1)}, f32[136,128]{1,0:T(8,128)S(1)}, u32[]{:S(2)}, u32[]{:S(2)}) collective-permute-start(f32[136,128]{1,0:T(8,128)S(1)} %bitcast_add_fusion), channel_id=1, source_target_pairs={{0,32},{8,40},{16,48},{24,56},{32,0},{40,8},{48,16},{56,24},{64,96... | collective-permute-start | bytes 208904 | tf_op jit(solution)/shard_map/ppermute | solution.py:376
  135.8 6.4 %collective-permute-start.7 = (f32[136,128]{1,0:T(8,128)S(1)}, f32[136,128]{1,0:T(8,128)S(1)}, u32[]{:S(2)}, u32[]{:S(2)}) collective-permute-start(f32[136,128]{1,0:T(8,128)S(1)} %bitcast_add_fusion), channel_id=1, source_target_pairs={{0,16},{8,24},{16,0},{24,8},{32,48},{40,56},{48,32},{56,40},{64,80... | collective-permute-start | bytes 208904 | tf_op jit(solution)/shard_map/ppermute | solution.py:376
  142.3 5.6 %collective-permute-start.12 = (f32[136,128]{1,0:T(8,128)S(1)}, f32[136,128]{1,0:T(8,128)S(1)}, u32[]{:S(2)}, u32[]{:S(2)}) collective-permute-start(f32[136,128]{1,0:T(8,128)S(1)} %add_add_fusion.2), channel_id=1, source_target_pairs={{0,192},{8,200},{16,208},{24,216},{32,224},{40,232},{48,240},{56,2... | collective-permute-start | bytes 208904 | tf_op jit(solution)/shard_map/ppermute | solution.py:376
  144.5 5.8 %collective-permute-start.11 = (f32[136,128]{1,0:T(8,128)S(1)}, f32[136,128]{1,0:T(8,128)S(1)}, u32[]{:S(2)}, u32[]{:S(2)}) collective-permute-start(f32[136,128]{1,0:T(8,128)S(1)} %add_add_fusion.2), channel_id=1, source_target_pairs={{0,128},{8,136},{16,144},{24,152},{32,160},{40,168},{48,176},{56,1... | collective-permute-start | bytes 208904 | tf_op jit(solution)/shard_map/ppermute | solution.py:376
  145.3 5.0 %collective-permute-start.10 = (f32[136,128]{1,0:T(8,128)S(1)}, f32[136,128]{1,0:T(8,128)S(1)}, u32[]{:S(2)}, u32[]{:S(2)}) collective-permute-start(f32[136,128]{1,0:T(8,128)S(1)} %add_add_fusion.2), channel_id=1, source_target_pairs={{0,64},{8,72},{16,80},{24,88},{32,96},{40,104},{48,112},{56,120},{... | collective-permute-start | bytes 208904 | tf_op jit(solution)/shard_map/ppermute | solution.py:376
  150.3 5.1 %collective-permute-start.15 = (f32[136,128]{1,0:T(8,128)S(1)}, f32[136,128]{1,0:T(8,128)S(1)}, u32[]{:S(2)}, u32[]{:S(2)}) collective-permute-start(f32[136,128]{1,0:T(8,128)S(1)} %add_add_fusion.1), channel_id=1, source_target_pairs={{0,6},{1,7},{2,4},{3,5},{4,2},{5,3},{6,0},{7,1},{8,14},{9,15},{10,... | collective-permute-start | bytes 208904 | tf_op jit(solution)/shard_map/ppermute | solution.py:376
  151.9 5.8 %collective-permute-start.14 = (f32[136,128]{1,0:T(8,128)S(1)}, f32[136,128]{1,0:T(8,128)S(1)}, u32[]{:S(2)}, u32[]{:S(2)}) collective-permute-start(f32[136,128]{1,0:T(8,128)S(1)} %add_add_fusion.1), channel_id=1, source_target_pairs={{0,4},{1,5},{2,6},{3,7},{4,0},{5,1},{6,2},{7,3},{8,12},{9,13},{10,... | collective-permute-start | bytes 208904 | tf_op jit(solution)/shard_map/ppermute | solution.py:376
  151.9 5.8 %collective-permute-start.13 = (f32[136,128]{1,0:T(8,128)S(1)}, f32[136,128]{1,0:T(8,128)S(1)}, u32[]{:S(2)}, u32[]{:S(2)}) collective-permute-start(f32[136,128]{1,0:T(8,128)S(1)} %add_add_fusion.1), channel_id=1, source_target_pairs={{0,2},{1,3},{2,0},{3,1},{4,6},{5,7},{6,4},{7,5},{8,10},{9,11},{10,... | collective-permute-start | bytes 208904 | tf_op jit(solution)/shard_map/ppermute | solution.py:376
  157.8 8.3 %collective-permute-start.16 = (f32[136,128]{1,0:T(8,128)S(1)}, f32[136,128]{1,0:T(8,128)S(1)}, u32[]{:S(2)}, u32[]{:S(2)}) collective-permute-start(f32[136,128]{1,0:T(8,128)S(1)} %add_add_fusion), channel_id=1, source_target_pairs={{0,1},{1,0},{2,3},{3,2},{4,5},{5,4},{6,7},{7,6},{8,9},{9,8},{10,11... | collective-permute-start | bytes 208904 | tf_op jit(solution)/shard_map/ppermute | solution.py:376
  166.1 11.0 %collective-permute-start.17 = (f32[136,128]{1,0:T(8,128)S(1)}, f32[136,128]{1,0:T(8,128)S(1)}, u32[]{:S(2)}, u32[]{:S(2)}) collective-permute-start(f32[136,128]{1,0:T(8,128)S(1)} %add.58), channel_id=1, source_target_pairs={{0,8},{8,0},{16,24},{24,16},{32,40},{40,32},{48,56},{56,48},{64,72... | collective-permute-start | bytes 208904 | tf_op jit(solution)/shard_map/ppermute | solution.py:379
  166.3 39.1 %collective-permute-start.18 = (f32[256,256]{1,0:T(8,128)S(1)}, f32[256,256]{1,0:T(8,128)S(1)}, u32[]{:S(2)}, u32[]{:S(2)}) collective-permute-start(f32[256,256]{1,0:T(8,128)S(1)} %copy-done.9), channel_id=1, source_target_pairs={{0,1},{1,2},{2,3},{3,4},{4,5},{5,6},{6,7},{8,9},{9,10},{10,11},{11... | collective-permute-start | bytes 786440 | tf_op jit(solution)/shard_map/ppermute | solution.py:455
  173.8 31.5 %collective-permute-start.19 = (f32[256,256]{1,0:T(8,128)S(1)}, f32[256,256]{1,0:T(8,128)S(1)}, u32[]{:S(2)}, u32[]{:S(2)}) collective-permute-start(f32[256,256]{1,0:T(8,128)S(1)} %copy-done.8), channel_id=1, source_target_pairs={{1,0},{2,1},{3,2},{4,3},{5,4},{6,5},{7,6},{9,8},{10,9},{11,10},{12... | collective-permute-start | bytes 786440 | tf_op jit(solution)/shard_map/ppermute | solution.py:456
  (8 other events, 18.8 us)

commit v2 on v1

--- a/solution.py
+++ b/solution.py
@@ -8,6 +8,7 @@
 from jax.experimental import pallas as pl
 from jax.experimental.pallas import tpu as pltpu
 from jax.sharding import PartitionSpec as P
+
 
 HI = lax.Precision.HIGHEST
 CH = 8
@@ -65,7 +66,7 @@
             ref[out, LANES:] = b * bath[i : i + 1, LANES:]
         return carry
 
-    lax.fori_loop(0, PER, chunk, 0)
+    each(PER, chunk, 2)(0)
 
 
 def bath_rows(bath, from_east, from_west, wide_bath):
@@ -139,7 +140,7 @@
         return tuple(new)
 
     zero = jnp.zeros((CH, LANES), jnp.float32)
-    exts = lax.fori_loop(0, PER, chunk, (zero, zero))
+    exts = each(PER, chunk, 4)((zero, zero))
     for msg, ext in ((msg_n, exts[0]), (msg_s, exts[1])):
         msg[pl.ds(pl.multiple_of(EXT + step * CH, CH), CH), :LANES] = ext
 
@@ -164,31 +165,33 @@
     return jnp.dot(a, b, preferred_element_type=jnp.float32)
 
 
-def forecast_kernel(
-    nrows, ntiles, members, scale,
-    lo, hi, bath, from_east, from_west, fcor, fy_n, fy_s, msg_n, msg_s, index, count, value, sd,
-    out, sums, wide_bath, beyond, height,
+def clip(limit):
+    return pltpu.CompilerParams(vmem_limit_bytes=limit << 20)
+
+
+def local_kernel(
+    nrows, lo, hi, bath, from_east, from_west, fcor, index,
+    out, flux_edge, height_edge, wind_edge, seen, wide_bath, height,
 ):
     step = pl.program_id(0)
-    tile = lax.axis_index("lat")
-    base = tile * nrows
-    has = (jnp.where(tile > 0, 1.0, 0.0), jnp.where(tile < ntiles - 1, 1.0, 0.0))
+    base = lax.axis_index("lat") * nrows
 
     @pl.when(step == 0)
     def _():
         bath_rows(bath, from_east, from_west, wide_bath)
-        for k, msg in enumerate((msg_n, msg_s)):
-            beyond[2 * k, :, :COLS] = jnp.broadcast_to(msg[BATH : BATH + 1, :], (CH, COLS))
-            beyond[2 * k, :, COLS:] = jnp.broadcast_to(msg[BATH + 2 : BATH + 3, :LANES], (CH, LANES))
-            beyond[2 * k + 1, :, :COLS] = jnp.broadcast_to(msg[BATH + 1 : BATH + 2, :], (CH, COLS))
-            beyond[2 * k + 1, :, COLS:] = jnp.zeros((CH, LANES), jnp.float32)
 
     lane = lanes_of((CH, LANES))
+
+    def across(y, i):
+        if i == 0:
+            return y[1]
+        if i == ROWS - 1:
+            return -y[i - 1]
+        return y[i + 1] - y[i - 1]
 
     def chunk(q, carry):
         loc = pl.ds(pl.multiple_of(q * CH, CH), CH)
         dst = pl.ds(pl.multiple_of(step * (CH * PER) + q * CH, CH), CH)
-        dst_q = pl.ds(pl.multiple_of(COLS + step * (CH * PER) + q * CH, CH), CH)
         e, w = from_east[loc, :], from_west[loc, :]
         load = lambda c, i: wide_rows(lo, hi, e, w, lane, q, c, i)
         H = [wide_bath[i] for i in range(ROWS)]
@@ -196,37 +199,19 @@
         h = [load(0, i) for i in range(ROWS)]
         u = [load(1, i) for i in range(ROWS)]
         v = [load(2, i) for i in range(ROWS)]
-        ghost = []
-        for msg, fy_msg in ((msg_n, fy_n), (msg_s, fy_s)):
-            t = msg[pl.ds(pl.multiple_of(EXT + step * CH, CH), CH), :LANES]
-            t = pltpu.roll(t, (LANES - q * 16) % LANES, 1)
-            ghost.append((
-                jnp.concatenate([fy_msg[loc, :], roll(t, -4)], axis=1),
-                jnp.concatenate([msg[dst, :], roll(t, -10)], axis=1),
-                jnp.concatenate([msg[dst_q, :], roll(t, -14)], axis=1),
-            ))
         fy = [H[i] * v[i] for i in range(ROWS)]
-        y = [ghost[0][0]] + fy + [ghost[1][0]]
-        h1 = [h[i] - 0.25 * (ddx(H[i] * u[i]) + (y[i + 2] - y[i])) for i in range(ROWS)]
-        eps = (-0.25 * fy[0], 0.25 * fy[-1])
-        y = [has[0] * (ghost[0][1] + eps[0])] + h1 + [has[1] * (ghost[1][1] + eps[1])]
+        h1 = [h[i] - 0.25 * (ddx(H[i] * u[i]) + across(fy, i)) for i in range(ROWS)]
         u1 = [u[i] + (0.5 * f[i]) * v[i] - 0.25 * ddx(h1[i]) for i in range(ROWS)]
-        v1 = [v[i] - (0.5 * f[i]) * u[i] - 0.25 * (y[i + 2] - y[i]) for i in range(ROWS)]
+        v1 = [v[i] - (0.5 * f[i]) * u[i] - 0.25 * across(h1, i) for i in range(ROWS)]
+        for k, i in ((0, 0), (1, ROWS - 1)):
+            flux_edge[k, loc, :] = fy[i]
+            height_edge[k, loc, :] = h1[i]
+            wind_edge[k, loc, :] = v1[i][:, :COLS]
         fy = [H[i] * v1[i] for i in range(ROWS)]
-        y = (
-            [ghost[0][2] - 0.25 * (beyond[0] * h1[0])]
-            + fy
-            + [ghost[1][2] + 0.25 * (beyond[2] * h1[-1])]
-        )
-        h2 = [h1[i] - 0.25 * (ddx(H[i] * u1[i]) + (y[i + 2] - y[i])) for i in range(ROWS)]
-        tail = []
-        for k, sg, edge in ((0, -1, fy[0]), (1, 1, fy[-1])):
-            bend = ddx(beyond[2 * k] * (-0.25 * ddx(eps[k])))
-            tail.append(has[k] * (eps[k] - 0.25 * (bend - sg * edge + 0.25 * (beyond[2 * k + 1] * eps[k]))))
-        y = [tail[0]] + h2 + [tail[1]]
+        h2 = [h1[i] - 0.25 * (ddx(H[i] * u1[i]) + across(fy, i)) for i in range(ROWS)]
         for i in range(ROWS):
             u2 = u1[i] + (0.5 * f[i]) * v1[i] - 0.25 * ddx(h2[i])
-            v2 = v1[i] - (0.5 * f[i]) * u1[i] - 0.25 * (y[i + 2] - y[i])
+            v2 = v1[i] - (0.5 * f[i]) * u1[i] - 0.25 * across(h2, i)
             out[0, i, loc, :] = h2[i][:, :COLS]
             out[1, i, loc, :] = u2[:, :COLS]
             out[2, i, loc, :] = v2[:, :COLS]
@@ -237,30 +222,142 @@
 
     @pl.when(step == pl.num_programs(0) - 1)
     def _():
-        slots = index.shape[1]
-        sub = lax.broadcasted_iota(jnp.int32, (COLS, slots), 0)
-        cell = jnp.broadcast_to(index[...], (COLS, slots))
-        hx = jnp.zeros((members, slots), jnp.float32)
-        for i in range(ROWS):
-            pick = jnp.where(sub + i * COLS == cell, 1.0, 0.0).astype(jnp.bfloat16)
-            for p in split(height[i], 3):
-                hx = hx + bdot(p, pick)
-        used = jnp.where(lanes_of((1, slots)) < count[0, 0], 1.0, 0.0)
-        sigma = sd[...] * scale
-        hmean = jnp.mean(hx, axis=0, keepdims=True)
-        anom = (hx - hmean) * (used / (math.sqrt(members - 1) * sigma))
-        innov = (value[...] - hmean) / sigma * used
-        gram = dot(anom, anom, 1, 1)
-        proj = dot(jnp.broadcast_to(innov, (8, slots)), anom, 1, 1)
-        n = LANES
-        ln, sb = lanes_of((n, n)), lax.broadcasted_iota(jnp.int32, (n, n), 0)
-        last = gram[n:, n:]
-        sums[0:n, :] = jnp.where(ln >= sb, gram[:n, :n], last)
-        sums[n : 2 * n, :] = gram[:n, n:]
-        sums[2 * n :, :] = jnp.zeros((16, n), jnp.float32)
-        sums[2 * n : 2 * n + 1, :] = jnp.sum(jnp.where(ln == sb, last, 0.0), axis=0, keepdims=True)
-        sums[2 * n + 1 : 2 * n + 2, :] = proj[0:1, :n]
-        sums[2 * n + 2 : 2 * n + 3, :] = proj[0:1, n:]
+        seen[...] = observe(index, [(i, height[i]) for i in range(ROWS)])
+
+
+def observe(index, planes):
+    slots = index.shape[1]
+    sub = lax.broadcasted_iota(jnp.int32, (COLS, slots), 0)
+    cell = jnp.broadcast_to(index[...], (COLS, slots))
+    hx = jnp.zeros((planes[0][1].shape[0], slots), jnp.float32)
+    for i, plane in planes:
+        pick = jnp.where(sub + i * COLS == cell, 1.0, 0.0).astype(jnp.bfloat16)
+        for p in split(plane, 3):
+            hx = hx + bdot(p, pick)
+    return hx
+
+
+def beyond_rows(msgs, beyond):
+    for k, msg in enumerate(msgs):
+        beyond[2 * k, :, :COLS] = jnp.broadcast_to(msg[BATH : BATH + 1, :], (CH, COLS))
+        beyond[2 * k, :, COLS:] = jnp.broadcast_to(msg[BATH + 2 : BATH + 3, :LANES], (CH, LANES))
+        beyond[2 * k + 1, :, :COLS] = jnp.broadcast_to(msg[BATH + 1 : BATH + 2, :], (CH, COLS))
+        beyond[2 * k + 1, :, COLS:] = jnp.zeros((CH, LANES), jnp.float32)
+
+
+def edge_change(k, has, q, fy_msg, msg, flux_edge, height_edge, wide_bath, beyond):
+    sg, e, n = ((-1, 0, 1), (1, ROWS - 1, ROWS - 2))[k]
+    chunk = q % PER
+    rows = pl.ds(pl.multiple_of(q * CH, CH), CH)
+    rows_q = pl.ds(pl.multiple_of(COLS + q * CH, CH), CH)
+    t = msg[pl.ds(pl.multiple_of(EXT + (q // PER) * CH, CH), CH), :LANES]
+    t = pltpu.roll(t, (LANES - chunk * 16) % LANES, 1)
+    g0 = jnp.concatenate([fy_msg[rows, :], roll(t, -4)], axis=1)
+    part = jnp.concatenate([msg[rows, :], roll(t, -10)], axis=1)
+    flux = jnp.concatenate([msg[rows_q, :], roll(t, -14)], axis=1)
+    c = sg * 0.25
+    eps = c * flux_edge[k, rows, :]
+    dh1 = -c * g0
+    du1 = -0.25 * ddx(dh1)
+    dv_e = -c * (has * (part + eps))
+    dv_n = -c * dh1
+    h1 = height_edge[k, rows, :] + dh1
+    g2 = flux + c * (beyond[2 * k] * h1)
+    He, Hn = wide_bath[e], wide_bath[n]
+    flow_n = Hn * dv_n
+    a = dh1 - 0.25 * (ddx(He * du1) - sg * flow_n + sg * g2)
+    b = -c * (He * dv_e)
+    d = -c * flow_n
+    return eps, du1, dv_e, dv_n, a, b, d
+
+
+def sums_kernel(
+    ntiles, members, scale,
+    bath, from_east, from_west, fy_n, fy_s, msg_n, msg_s, flux_edge, height_edge, seen, index, count, value, sd,
+    sums, wide_bath, beyond, change,
+):
+    tile = lax.axis_index("lat")
+    has = (jnp.where(tile > 0, 1.0, 0.0), jnp.where(tile < ntiles - 1, 1.0, 0.0))
+    bath_rows(bath, from_east, from_west, wide_bath)
+    beyond_rows((msg_n, msg_s), beyond)
+    slots = index.shape[1]
+
+    def chunk(q, carry):
+        dst = pl.ds(pl.multiple_of(q * CH, CH), CH)
+        for k, fy, msg in ((0, fy_n, msg_n), (1, fy_s, msg_s)):
+            new = edge_change(k, has[k], q, fy, msg, flux_edge, height_edge, wide_bath, beyond)
+            for j in range(3):
+                change[3 * k + j, dst, :] = new[4 + j][:, :COLS]
+        return carry
+
+    each(members // CH, chunk, 4)(0)
+    rows = (0, 1, 2, ROWS - 1, ROWS - 2, ROWS - 3)
+    hx = seen[...] + observe(index, [(r, change[j]) for j, r in enumerate(rows)])
+    used = jnp.where(lanes_of((1, slots)) < count[0, 0], 1.0, 0.0)
+    sigma = sd[...] * scale
+    hmean = jnp.mean(hx, axis=0, keepdims=True)
+    anom = (hx - hmean) * (used / (math.sqrt(members - 1) * sigma))
+    innov = (value[...] - hmean) / sigma * used
+    gram = dot(anom, anom, 1, 1)
+    proj = dot(jnp.broadcast_to(innov, (8, slots)), anom, 1, 1)
+    n = LANES
+    ln, sb = lanes_of((n, n)), lax.broadcasted_iota(jnp.int32, (n, n), 0)
+    last = gram[n:, n:]
+    sums[0:n, :] = jnp.where(ln >= sb, gram[:n, :n], last)
+    sums[n : 2 * n, :] = gram[:n, n:]
+    sums[2 * n :, :] = jnp.zeros((16, n), jnp.float32)
+    sums[2 * n : 2 * n + 1, :] = jnp.sum(jnp.where(ln == sb, last, 0.0), axis=0, keepdims=True)
+    sums[2 * n + 1 : 2 * n + 2, :] = proj[0:1, :n]
+    sums[2 * n + 2 : 2 * n + 3, :] = proj[0:1, n:]
+
+
+def complete_kernel(
+    nrows, ntiles, block,
+    bath, from_east, from_west, fcor, fy_n, fy_s, msg_n, msg_s, flux_edge, height_edge, wind_edge, fields,
+    out, wide_bath, beyond,
+):
+    tile = lax.axis_index("lat")
+    base = tile * nrows
+    has = (jnp.where(tile > 0, 1.0, 0.0), jnp.where(tile < ntiles - 1, 1.0, 0.0))
+    bath_rows(bath, from_east, from_west, wide_bath)
+    beyond_rows((msg_n, msg_s), beyond)
+
+    def chunk(q, carry):
+        loc = pl.ds(pl.multiple_of(q * CH, CH), CH)
+        full = block * PER + q
+        rows = pl.ds(pl.multiple_of(full * CH, CH), CH)
+        for k, sg, e, fy, msg in ((0, -1, 0, fy_n, msg_n), (1, 1, ROWS - 1, fy_s, msg_s)):
+            eps, du1, dv_e, dv_n, a, b, d = edge_change(
+                k, has[k], full, fy, msg, flux_edge, height_edge, wide_bath, beyond
+            )
+            c = sg * 0.25
+            flow = wide_bath[e] * dv_e
+            flow = flow[:, :COLS] + wide_bath[e][:, :COLS] * wind_edge[k, rows, :]
+            bend = ddx(beyond[2 * k] * (-0.25 * ddx(eps))) + 0.25 * (beyond[2 * k + 1] * eps)
+            g3 = has[k] * (eps[:, :COLS] - 0.25 * (bend[:, :COLS] - sg * flow))
+            cut = lambda x: x[:, :COLS]
+            f0, f1 = 0.5 * fcor[base + e], 0.5 * fcor[base + e - sg]
+            r = [e - sg * j for j in range(4)]
+            upd = (
+                (0, r[0], cut(a)),
+                (0, r[1], cut(b)),
+                (0, r[2], cut(d)),
+                (1, r[0], cut(du1 + f0 * dv_e - 0.25 * ddx(a))),
+                (1, r[1], cut(f1 * dv_n - 0.25 * ddx(b))),
+                (1, r[2], cut(-0.25 * ddx(d))),
+                (2, r[0], cut(dv_e - f0 * du1) - c * (g3 - cut(b))),
+                (2, r[1], cut(dv_n - c * (a - d))),
+                (2, r[2], cut(-c * b)),
+                (2, r[3], cut(-c * d)),
+            )
+            for i, j, x in upd:
+                out[i, j, loc, :] = fields[i, j, loc, :] + x
+        return carry
+
+    for i in range(2):
+        for j in (3, 4):
+            out[i, j] = fields[i, j]
+    each(PER, chunk, 4)(0)
 
 
 def elim(a, dst, base):
@@ -271,29 +368,38 @@
     A = [a[8 * g : 8 * g + 8, :] for g in range(groups)]
     X = [(lane == sub + 8 * g).astype(jnp.float32) for g in range(groups)]
 
-    def body(it, carry):
-        A, X = list(carry[:groups]), list(carry[groups:])
+    def body(live, it, carry):
+        A, X = list(carry[:live]), list(carry[live:])
+        cols = [[jnp.broadcast_to(A[g][:, k : k + 1], (8, n)) for k in range(8)] for g in range(live)]
+        C, P, Z = cols[0], A[0], X[0]
+        rows = Z
         for k in range(8):
-            d = jnp.broadcast_to(A[0][k : k + 1, k : k + 1], (1, n))
+            pick = lambda x: jnp.broadcast_to(x[k : k + 1, :], (8, n))
+            here = sub == k
+            d = pick(C[k])
             inv = 1.0 / d
-            ra = A[0][k : k + 1, :] * inv
-            rx = X[0][k : k + 1, :] * inv
-            for g in range(groups):
-                col = jnp.broadcast_to(A[g][:, k : k + 1], (8, n))
-                if g == 0:
-                    below = sub > k
-                    scaled = jnp.where(sub == k, X[0] * lax.rsqrt(d), X[0])
-                    A[0] = jnp.where(below, A[0] - col * ra, A[0])
-                    X[0] = jnp.where(below, X[0] - col * rx, scaled)
-                else:
-                    A[g] = A[g] - col * ra
-                    X[g] = X[g] - col * rx
-        dst[pl.ds(pl.multiple_of(base + it * 8, 8), 8), :] = X[0]
+            rows = jnp.where(here, Z * lax.rsqrt(d), rows)
+            ra, rx = pick(P) * inv, pick(Z) * inv
+            for j in range(k + 1, 8):
+                rc = pick(C[j]) * inv
+                C[j] = jnp.where(here, rc, C[j] - C[k] * rc)
+            P = jnp.where(here, ra, P - C[k] * ra)
+            Z = jnp.where(here, rx, Z - C[k] * rx)
+        dst[pl.ds(pl.multiple_of(base + it * 8, 8), 8), :] = rows
+        for k in range(8):
+            rp, rz = (jnp.broadcast_to(x[k : k + 1, :], (8, n)) for x in (P, Z))
+            for g in range(1, live):
+                A[g] = A[g] - cols[g][k] * rp
+                X[g] = X[g] - cols[g][k] * rz
         z = jnp.zeros((8, n), jnp.float32)
-        A = [roll(A[g], -8) for g in range(1, groups)] + [z]
+        A = [roll(A[g], -8) for g in range(1, live)] + [z]
         return tuple(A) + tuple(X[1:]) + (z,)
 
-    lax.fori_loop(0, groups, body, tuple(A) + tuple(X))
+    seg = 4
+    for first in range(0, groups, seg):
+        live = groups - first
+        out = lax.fori_loop(first, first + seg, functools.partial(body, live), tuple(A) + tuple(X))
+        A, X = list(out[: live - seg]), list(out[live : 2 * live - seg])
 
 
 def factor_kernel(members, g_ref, mix, inverse):
@@ -344,6 +450,15 @@
         out[0, pl.ds(i, x.shape[0], stride=ROWS), :] = res
 
 
+def each(trips, fn, together):
+    def turn(t, carry):
+        for j in range(together):
+            carry = fn(t * together + j, carry)
+        return carry
+
+    return lambda init: lax.fori_loop(0, trips // together, turn, init)
+
+
 def whole(shape):
     return pl.BlockSpec(shape, lambda *_: (0,) * len(shape))
 
@@ -382,13 +497,13 @@
     return jnp.concatenate([lo, hi], axis=0)
 
 
-def shards(state, bathymetry, obs_index, obs_count, obs_value, obs_sd):
+def body(state, bathymetry, obs_index, obs_count, obs_value, obs_sd):
     members = state.shape[1]
     nlat, nlon = lax.axis_size("lat"), lax.axis_size("lon")
     slots = obs_index.shape[2]
     total_rows = ROWS * nlat
     fcor = np.sin(math.pi / 3.0 * ((np.arange(total_rows) + 0.5) / total_rows - 0.5)).astype(np.float32)
-    flat = state.reshape(3, members * ROWS, COLS)
+    flat = pltpu.with_memory_space_constraint(state.reshape(3, members * ROWS, COLS), pltpu.HBM)
     blk = CH * PER
     grid = (members // blk,)
     state_specs = [
@@ -406,6 +521,7 @@
         in_specs=state_specs + [bath_spec],
         out_specs=[thin, thin, row, row],
         out_shape=[f32(members, LANES)] * 2 + [f32(members, COLS)] * 2,
+        compiler_params=clip(24),
         name="edges",
     )(flat, flat, bathymetry)
 
@@ -425,6 +541,7 @@
         out_specs=[whole((MSG, COLS))] * 2 + [whole((members, COLS))] * 2,
         out_shape=[f32(MSG, COLS)] * 2 + [f32(members, COLS)] * 2,
         scratch_shapes=[VM((ROWS, CH, WIDE), jnp.float32)],
+        compiler_params=clip(24),
         name="border",
     )(flat, flat, bathymetry, from_east, from_west, fcor)
     got_n = lax.ppermute(msg_s, "lat", south)
@@ -432,29 +549,64 @@
 
     one = lambda x: x.reshape(1, slots)
     obs = whole((1, slots))
-    fields, sums = pl.pallas_call(
-        functools.partial(forecast_kernel, ROWS, nlat, members, math.sqrt(slots * nlat * nlon) / 16.0),
+    edge = whole((2, members, WIDE))
+    blocks = members // blk
+    wide_scratch = VM((ROWS, CH, WIDE), jnp.float32)
+    beyond_scratch = VM((4, CH, WIDE), jnp.float32)
+    fields, flux_edge, height_edge, wind_edge, seen = pl.pallas_call(
+        functools.partial(local_kernel, ROWS),
         grid=grid,
-        in_specs=state_specs
-        + [bath_spec, thin, thin, smem, row, row, whole((MSG, COLS)), whole((MSG, COLS))]
-        + [obs, smem, obs, obs],
-        out_specs=[pl.BlockSpec((3, ROWS, blk, COLS), lambda s: (0, 0, s, 0)), whole((272, LANES))],
-        out_shape=[f32(3, ROWS, members, COLS), f32(272, LANES)],
-        scratch_shapes=[
-            VM((ROWS, CH, WIDE), jnp.float32),
-            VM((4, CH, WIDE), jnp.float32),
-            VM((ROWS, members, COLS), jnp.float32),
+        in_specs=state_specs + [bath_spec, thin, thin, smem, obs],
+        out_specs=[
+            pl.BlockSpec((3, ROWS, blk, COLS), lambda s: (0, 0, s, 0)),
+            pl.BlockSpec((2, blk, WIDE), lambda s: (0, s, 0)),
+            pl.BlockSpec((2, blk, WIDE), lambda s: (0, s, 0)),
+            pl.BlockSpec((2, blk, COLS), lambda s: (0, s, 0)),
+            whole((members, slots)),
         ],
-        name="forecast",
+        out_shape=[
+            pltpu.HBM((3, ROWS, members, COLS), jnp.float32), f32(2, members, WIDE), f32(2, members, WIDE),
+            f32(2, members, COLS), f32(members, slots),
+        ],
+        scratch_shapes=[wide_scratch, VM((ROWS, members, COLS), jnp.float32)],
+        compiler_params=clip(24),
+        name="local",
+    )(flat, flat, bathymetry, from_east, from_west, fcor, one(obs_index))
+
+    head = whole((CH, LANES))
+    got = (fy_n, fy_s, got_n, got_s, flux_edge, height_edge)
+    got_specs = [whole((members, COLS))] * 2 + [whole((MSG, COLS))] * 2 + [edge, edge]
+    sums = pl.pallas_call(
+        functools.partial(sums_kernel, nlat, members, math.sqrt(slots * nlat * nlon) / 16.0),
+        grid=(1,),
+        in_specs=[bath_spec, head, head] + got_specs + [whole((members, slots)), obs, smem, obs, obs],
+        out_specs=whole((272, LANES)),
+        out_shape=f32(272, LANES),
+        scratch_shapes=[wide_scratch, beyond_scratch, VM((6, members, COLS), jnp.float32)],
+        compiler_params=clip(24),
+        name="sums",
     )(
-        flat, flat, bathymetry, from_east, from_west, fcor, fy_n, fy_s, got_n, got_s,
+        bathymetry, from_east, from_west, *got, seen,
         one(obs_index), obs_count, one(obs_value), one(obs_sd),
     )
 
-    sums, late_n, late_s = lax.optimization_barrier((sums, late_n, late_s))
+    for k in range(blocks):
+        part = pl.BlockSpec((3, ROWS, blk, COLS), lambda s, k=k: (0, 0, k, 0))
+        fields = pl.pallas_call(
+            functools.partial(complete_kernel, ROWS, nlat, k),
+            grid=(1,),
+            in_specs=[bath_spec, head, head, smem] + got_specs + [whole((2, members, COLS)), part],
+            out_specs=part,
+            out_shape=pltpu.HBM((3, ROWS, members, COLS), jnp.float32),
+            scratch_shapes=[wide_scratch, beyond_scratch],
+            input_output_aliases={11: 0},
+            compiler_params=clip(24),
+            name="complete",
+        )(bathymetry, from_east, from_west, fcor, *got, wind_edge, fields)
+
+    sums, late_n, late_s = lax.optimization_barrier((total(sums), late_n, late_s))
     late_from_n = lax.ppermute(late_s, "lat", south)
     late_from_s = lax.ppermute(late_n, "lat", north)
-    sums = total(sums)
 
     mix = pl.pallas_call(
         functools.partial(factor_kernel, members),
@@ -462,6 +614,7 @@
         in_specs=[pl.BlockSpec(memory_space=VM)],
         out_specs=pl.BlockSpec(memory_space=VM),
         scratch_shapes=[VM((members, LANES), jnp.float32)],
+        compiler_params=clip(8),
         name="factor",
     )(sums)
 
@@ -477,6 +630,7 @@
         ],
         out_specs=pl.BlockSpec((1, members * ROWS, LANES), lambda c, j: (c, 0, j)),
         out_shape=f32(3, members * ROWS, COLS),
+        compiler_params=clip(24),
         name="mix",
     )(mix, fields, late_from_n, late_from_s)
     return analysis.reshape(state.shape)
@@ -484,7 +638,7 @@
 
 def solution(mesh):
     return jax.shard_map(
-        shards,
+        body,
         mesh=mesh,
         in_specs=(
             P(None, None, "lat", "lon"),

time: 217 us -> 209 us (0.963)
  waiting for transfers between devices: 75.1 us -> 59 us
  local copies, waits for them, and re-layouts: 3.38 us -> 9.82 us
  Pallas kernels: 77.9 us -> 81 us
    ppermute x8, waiting for transfers between devices: 59.5 us -> 40.4 us  [the longest x1 26.1 us: body(): fy_n = lax.ppermute(to_south, 'lat', south)]
    unnamed x24 -> x32, local copies, waits for them, and re-layouts: 2.49 us -> 9.2 us
    pallas_call x5 -> x10, Pallas kernels: 77.9 us -> 81 us  [the longest x4 19.8 us: body(): pl.pallas_call(functools.partial(complete_kernel, ROWS, nlat, k), grid=(1...]
  transfers between devices with their start and end apart: 20 -> 20, of which waited for: 12 -> 14; matrix products, arithmetic and copies ran while one was open for 0% -> 0% of each run, Pallas kernels for 13% -> 24%
where the time goes in v2:
time: 209 us
  Pallas kernels  81 us (39%)
  waiting for transfers between devices  59 us (28%)
  starting transfers between devices  55.3 us (26%)
  local copies, waits for them, and re-layouts  9.82 us (5%)
  other arithmetic  2.57 us (1%)
    ppermute x1, waiting for transfers between devices, body(): fy_n = lax.ppermute(to_south, 'lat', south)  26.1 us
    pallas_call x4, Pallas kernels, body(): pl.pallas_call(functools.partial(complete_kernel, ROWS, nlat, k), grid=(1...  19.8 us
    pallas_call x1, Pallas kernels, body(): pl.pallas_call(functools.partial(local_kernel, ROWS), grid=grid, in_specs...  18 us
    ppermute x10, starting transfers between devices, total(): parts = [lax.ppermute(y, axis, flips(n, b)) for b in hops]  17.1 us
    ppermute x10, waiting for transfers between devices, total(): parts = [lax.ppermute(y, axis, flips(n, b)) for b in hops]  15.3 us
    pallas_call x1, Pallas kernels, body(): pl.pallas_call(functools.partial(factor_kernel, members), out_shape=f32(m...  12.7 us
    pallas_call x1, Pallas kernels, body(): pl.pallas_call(functools.partial(border_kernel, ROWS), grid=grid, in_spec...  11 us
    unnamed x32, local copies, waits for them, and re-layouts  9.2 us
  transfers between devices with their start and end apart: 20, of which 14 were waited for; matrix products, arithmetic and copies ran while one was open for 0% of the time, Pallas kernels for 24%

profile of v2, /device:TPU:8, one launch (start us, length us, event | category | flops | bytes accessed | tf_op | source)
XLA Modules:
  0.0 208.5 jit_solution(16341739429398644211)
XLA Ops:
  0.7 6.1 %edges.1 = (f32[256,128]{1,0:T(8,128)S(1)}, f32[256,128]{1,0:T(8,128)S(1)}, f32[256,256]{1,0:T(8,128)}, f32[256,256]{1,0:T(8,128)}) custom-call(f32[3,2048,256]{2,1,0:T(8,128)} %bitcast.16, f32[3,2048,256]{2,1,0:T(8,128)} %bitcast.17, f32[8,256]{1,0:T(8,128)S(1)} %copy-done.8), custom_call_target="tpu_custom_call" | custom-call | tf_op jit(solution)/shard_map/edges/pallas_call | solution.py:518
  6.8 6.3 %collective-permute-start = (f32[256,128]{1,0:T(8,128)S(1)}, f32[256,128]{1,0:T(8,128)S(1)}, u32[]{:S(2)}, u32[]{:S(2)}) collective-permute-start(f32[256,128]{1,0:T(8,128)S(1)} %get-tuple-element.21), channel_id=1, source_target_pairs={{8,0},{16,8},{24,16},{32,24},{40,32},{48,40},{56,48},{64,56},{72,6... | collective-permute-start | bytes 393224 | tf_op jit(solution)/shard_map/ppermute | solution.py:533
  15.6 5.8 %collective-permute-done.1.from_west = f32[256,128]{1,0:T(8,128)S(1)} collective-permute-done((f32[256,128]{1,0:T(8,128)S(1)}, f32[256,128]{1,0:T(8,128)S(1)}, u32[]{:S(2)}, u32[]{:S(2)}) %collective-permute-start.1) | collective-permute-done | bytes 131104 | tf_op jit(solution)/shard_map/ppermute | solution.py:532
  21.4 11.0 %border.1 = (f32[552,256]{1,0:T(8,128)}, f32[552,256]{1,0:T(8,128)}, f32[256,256]{1,0:T(8,128)S(1)}, f32[256,256]{1,0:T(8,128)S(1)}) custom-call(f32[3,2048,256]{2,1,0:T(8,128)} %bitcast.18, f32[3,2048,256]{2,1,0:T(8,128)} %bitcast.19, f32[8,256]{1,0:T(8,128)S(1)} %copy-done.8, f32[256,128]{1,0:T(8,128)S(1)} %collective-permute-done.from_east, ...), custom_call_target="tpu_custom_call" | custom-call | tf_op jit(solution)/shard_map/border/pallas_call | solution.py:537
  33.8 6.4 %collective-permute-start.4 = (f32[552,256]{1,0:T(8,128)}, f32[552,256]{1,0:T(8,128)S(1)}, u32[]{:S(2)}, u32[]{:S(2)}) collective-permute-start(f32[552,256]{1,0:T(8,128)} %get-tuple-element.25), channel_id=1, source_target_pairs={{0,1},{1,2},{2,3},{3,4},{4,5},{5,6},{6,7},{8,9},{9,10},{10,11},{11... | collective-permute-start | bytes 1695752 | tf_op jit(solution)/shard_map/ppermute | solution.py:547
  40.2 4.2 %collective-permute-start.5 = (f32[552,256]{1,0:T(8,128)}, f32[552,256]{1,0:T(8,128)S(1)}, u32[]{:S(2)}, u32[]{:S(2)}) collective-permute-start(f32[552,256]{1,0:T(8,128)} %get-tuple-element.26), channel_id=1, source_target_pairs={{1,0},{2,1},{3,2},{4,3},{5,4},{6,5},{7,6},{9,8},{10,9},{11,10},{12... | collective-permute-start | bytes 1695752 | tf_op jit(solution)/shard_map/ppermute | solution.py:548
  44.4 5.5 %collective-permute-start.2 = (f32[256,256]{1,0:T(8,128)}, f32[256,256]{1,0:T(8,128)S(1)}, u32[]{:S(2)}, u32[]{:S(2)}) collective-permute-start(f32[256,256]{1,0:T(8,128)} %get-tuple-element.23), channel_id=1, source_target_pairs={{0,1},{1,2},{2,3},{3,4},{4,5},{5,6},{6,7},{8,9},{9,10},{10,11},{11... | collective-permute-start | bytes 786440 | tf_op jit(solution)/shard_map/ppermute | solution.py:534
  49.9 5.1 %collective-permute-start.3 = (f32[256,256]{1,0:T(8,128)}, f32[256,256]{1,0:T(8,128)}, u32[]{:S(2)}, u32[]{:S(2)}) collective-permute-start(f32[256,256]{1,0:T(8,128)} %get-tuple-element.24), channel_id=1, source_target_pairs={{1,0},{2,1},{3,2},{4,3},{5,4},{6,5},{7,6},{9,8},{10,9},{11,10},{12... | collective-permute-start | bytes 786440 | tf_op jit(solution)/shard_map/ppermute | solution.py:535
  57.6 18.0 %local.1 = (f32[3,8,256,256]{3,2,1,0:T(8,128)}, f32[2,256,384]{2,1,0:T(8,128)S(1)}, f32[2,256,384]{2,1,0:T(8,128)S(1)}, f32[2,256,256]{2,1,0:T(8,128)S(1)}, f32[256,256]{1,0:T(8,128)S(1)}) custom-call(f32[3,2048,256]{2,1,0:T(8,128)} %bitcast.20, f32[3,2048,256]{2,1,0:T(8,128)} %bitcast.21, f32[8,256]{1,0:T(8,128)S(1)} %copy-done.9, ...), custom_call_target="tpu_custom_call" | custom-call | tf_op jit(solution)/shard_map/local/pallas_call | solution.py:556
  75.6 26.1 %collective-permute-done.2.fy_n = f32[256,256]{1,0:T(8,128)S(1)} collective-permute-done((f32[256,256]{1,0:T(8,128)}, f32[256,256]{1,0:T(8,128)S(1)}, u32[]{:S(2)}, u32[]{:S(2)}) %collective-permute-start.2) | collective-permute-done | bytes 262176 | tf_op jit(solution)/shard_map/ppermute | solution.py:534
  101.7 6.0 %collective-permute-done.3.fy_s = f32[256,256]{1,0:T(8,128)} collective-permute-done((f32[256,256]{1,0:T(8,128)}, f32[256,256]{1,0:T(8,128)}, u32[]{:S(2)}, u32[]{:S(2)}) %collective-permute-start.3) | collective-permute-done | bytes 262176 | tf_op jit(solution)/shard_map/ppermute | solution.py:535
  107.8 5.8 %sums.1 = f32[272,128]{1,0:T(8,128)S(1)} custom-call(f32[8,256]{1,0:T(8,128)S(1)} %copy-done.9, f32[256,128]{1,0:T(8,128)S(1)} %copy-done.2, f32[256,128]{1,0:T(8,128)S(1)} %copy-done.5, f32[256,256]{1,0:T(8,128)S(1)} %collective-permute-done.2.fy_n, f32[256,256]{1,0:T(8,128)} %collective-permute-done.3.fy_s, f32[552,256]{1,0:T(8,128)S(1)} %collective-permute-done.4.msg_n, ...), custom_call_target="tpu_custom_call" | custom-call | tf_op jit(solution)/shard_map/sums/pallas_call | solution.py:579
  135.6 2.6 %collective-permute-start.13 = (f32[136,128]{1,0:T(8,128)S(1)}, f32[136,128]{1,0:T(8,128)S(1)}, u32[]{:S(2)}, u32[]{:S(2)}) collective-permute-start(f32[136,128]{1,0:T(8,128)S(1)} %add_add_fusion.1), channel_id=1, source_target_pairs={{0,2},{1,3},{2,0},{3,1},{4,6},{5,7},{6,4},{7,5},{8,10},{9,11},{10,... | collective-permute-start | bytes 208904 | tf_op jit(solution)/shard_map/ppermute | solution.py:491
  141.5 4.3 %collective-permute-start.16 = (f32[136,128]{1,0:T(8,128)S(1)}, f32[136,128]{1,0:T(8,128)S(1)}, u32[]{:S(2)}, u32[]{:S(2)}) collective-permute-start(f32[136,128]{1,0:T(8,128)S(1)} %add_add_fusion), channel_id=1, source_target_pairs={{0,1},{1,0},{2,3},{3,2},{4,5},{5,4},{6,7},{7,6},{8,9},{9,8},{10,11... | collective-permute-start | bytes 208904 | tf_op jit(solution)/shard_map/ppermute | solution.py:491
  145.8 4.2 %collective-permute-done.16 = f32[136,128]{1,0:T(8,128)S(1)} collective-permute-done((f32[136,128]{1,0:T(8,128)S(1)}, f32[136,128]{1,0:T(8,128)S(1)}, u32[]{:S(2)}, u32[]{:S(2)}) %collective-permute-start.16) | collective-permute-done | bytes 69664 | tf_op jit(solution)/shard_map/ppermute | solution.py:491
  153.2 6.7 %collective-permute-start.18 = (f32[256,256]{1,0:T(8,128)}, f32[256,256]{1,0:T(8,128)S(1)}, u32[]{:S(2)}, u32[]{:S(2)}) collective-permute-start(f32[256,256]{1,0:T(8,128)} %copy-done.15), channel_id=1, source_target_pairs={{0,1},{1,2},{2,3},{3,4},{4,5},{5,6},{6,7},{8,9},{9,10},{10,11},{11... | collective-permute-start | bytes 786440 | tf_op jit(solution)/shard_map/ppermute | solution.py:608
  159.8 4.0 %collective-permute-start.19 = (f32[256,256]{1,0:T(8,128)}, f32[256,256]{1,0:T(8,128)S(1)}, u32[]{:S(2)}, u32[]{:S(2)}) collective-permute-start(f32[256,256]{1,0:T(8,128)} %copy-done.14), channel_id=1, source_target_pairs={{1,0},{2,1},{3,2},{4,3},{5,4},{6,5},{7,6},{9,8},{10,9},{11,10},{12... | collective-permute-start | bytes 786440 | tf_op jit(solution)/shard_map/ppermute | solution.py:609
  165.6 5.0 %complete.4.fields = f32[3,8,256,256]{3,2,1,0:T(8,128)} custom-call(f32[8,256]{1,0:T(8,128)S(1)} %copy-done.9, f32[256,128]{1,0:T(8,128)S(1)} %copy-done.3, f32[256,128]{1,0:T(8,128)S(1)} %copy-done.6, f32[64]{0:T(128)S(1)} %copy-done.10, f32[256,256]{1,0:T(8,128)S(1)} %collective-permute-done.2.fy_n, ...), custom_call_target="tpu_custom_call", output_to_operand_aliasing={{}: (11, {})} | custom-call | tf_op jit(solution)/shard_map/complete/pallas_call | solution.py:595
  170.6 5.0 %complete.5.fields = f32[3,8,256,256]{3,2,1,0:T(8,128)} custom-call(f32[8,256]{1,0:T(8,128)S(1)} %copy-done.9, f32[256,128]{1,0:T(8,128)S(1)} %copy-done.3, f32[256,128]{1,0:T(8,128)S(1)} %copy-done.6, f32[64]{0:T(128)S(1)} %copy-done.10, f32[256,256]{1,0:T(8,128)S(1)} %collective-permute-done.2.fy_n, ...), custom_call_target="tpu_custom_call", output_to_operand_aliasing={{}: (11, {})} | custom-call | tf_op jit(solution)/shard_map/complete/pallas_call | solution.py:595
  175.5 5.0 %complete.6.fields = f32[3,8,256,256]{3,2,1,0:T(8,128)} custom-call(f32[8,256]{1,0:T(8,128)S(1)} %copy-done.9, f32[256,128]{1,0:T(8,128)S(1)} %copy-done.3, f32[256,128]{1,0:T(8,128)S(1)} %copy-done.6, f32[64]{0:T(128)S(1)} %copy-done.10, f32[256,256]{1,0:T(8,128)S(1)} %collective-permute-done.2.fy_n, ...), custom_call_target="tpu_custom_call", output_to_operand_aliasing={{}: (11, {})} | custom-call | tf_op jit(solution)/shard_map/complete/pallas_call | solution.py:595
  180.5 5.0 %complete.7.fields = f32[3,8,256,256]{3,2,1,0:T(8,128)} custom-call(f32[8,256]{1,0:T(8,128)S(1)} %copy-done.9, f32[256,128]{1,0:T(8,128)S(1)} %copy-done.3, f32[256,128]{1,0:T(8,128)S(1)} %copy-done.6, f32[64]{0:T(128)S(1)} %copy-done.10, f32[256,256]{1,0:T(8,128)S(1)} %collective-permute-done.2.fy_n, ...), custom_call_target="tpu_custom_call", output_to_operand_aliasing={{}: (11, {})} | custom-call | tf_op jit(solution)/shard_map/complete/pallas_call | solution.py:595
  185.5 12.7 %factor.1.mix = f32[256,256]{1,0:T(8,128)S(1)} custom-call(f32[272,128]{1,0:T(8,128)S(1)} %pad_maximum_fusion.g_ref), custom_call_target="tpu_custom_call" | custom-call | tf_op jit(solution)/shard_map/factor/pallas_call | solution.py:611
  198.2 2.8 %copy-done = f32[3,8,256,256]{3,2,1,0:T(8,128)S(1)} copy-done((f32[3,8,256,256]{3,2,1,0:T(8,128)S(1)}, f32[3,8,256,256]{3,2,1,0:T(8,128)}, u32[]{:S(2)}) %copy-start) | copy-done | bytes 6291480
  201.0 7.6 %mix.1 = f32[3,2048,256]{2,1,0:T(8,128)} custom-call(f32[256,256]{1,0:T(8,128)S(1)} %factor.1.mix, f32[3,8,256,256]{3,2,1,0:T(8,128)S(1)} %copy-done, f32[256,256]{1,0:T(8,128)S(1)} %collective-permute-done.18.late_n, f32[256,256]{1,0:T(8,128)S(1)} %collective-permute-done.19.late_s), custom_call_target="tpu_custom_call" | custom-call | tf_op jit(solution)/shard_map/mix/pallas_call | solution.py:622
  (66 shorter events, 36.7 us)
Async XLA Ops:
  6.8 8.8 %collective-permute-start = (f32[256,128]{1,0:T(8,128)S(1)}, f32[256,128]{1,0:T(8,128)S(1)}, u32[]{:S(2)}, u32[]{:S(2)}) collective-permute-start(f32[256,128]{1,0:T(8,128)S(1)} %get-tuple-element.21), channel_id=1, source_target_pairs={{8,0},{16,8},{24,16},{32,24},{40,32},{48,40},{56,48},{64,56},{72,6... | collective-permute-start | bytes 393224 | tf_op jit(solution)/shard_map/ppermute | solution.py:533
  13.1 42.7 %copy-start.9 = (f32[8,256]{1,0:T(8,128)S(1)}, f32[8,256]{1,0:T(8,128)}, u32[]{:S(2)}) copy-start(f32[8,256]{1,0:T(8,128)} %bath.15) | copy-start | bytes 24580
  13.1 42.7 %copy-start.11 = (s32[1,1,256]{2,1,0:T(1,128)S(1)}, s32[1,1,256]{2,1,0:T(1,128)}, u32[]{:S(2)}) copy-start(s32[1,1,256]{2,1,0:T(1,128)} %param.9) | copy-start | bytes 3076
  13.1 8.3 %collective-permute-start.1 = (f32[256,128]{1,0:T(8,128)S(1)}, f32[256,128]{1,0:T(8,128)S(1)}, u32[]{:S(2)}, u32[]{:S(2)}) collective-permute-start(f32[256,128]{1,0:T(8,128)S(1)} %get-tuple-element.22), channel_id=1, source_target_pairs={{0,8},{8,16},{16,24},{24,32},{32,40},{40,48},{48,56},{56,64},{64,7... | collective-permute-start | bytes 393224 | tf_op jit(solution)/shard_map/ppermute | solution.py:532
  33.8 74.0 %collective-permute-start.4 = (f32[552,256]{1,0:T(8,128)}, f32[552,256]{1,0:T(8,128)S(1)}, u32[]{:S(2)}, u32[]{:S(2)}) collective-permute-start(f32[552,256]{1,0:T(8,128)} %get-tuple-element.25), channel_id=1, source_target_pairs={{0,1},{1,2},{2,3},{3,4},{4,5},{5,6},{6,7},{8,9},{9,10},{10,11},{11... | collective-permute-start | bytes 1695752 | tf_op jit(solution)/shard_map/ppermute | solution.py:547
  40.2 67.6 %collective-permute-start.5 = (f32[552,256]{1,0:T(8,128)}, f32[552,256]{1,0:T(8,128)S(1)}, u32[]{:S(2)}, u32[]{:S(2)}) collective-permute-start(f32[552,256]{1,0:T(8,128)} %get-tuple-element.26), channel_id=1, source_target_pairs={{1,0},{2,1},{3,2},{4,3},{5,4},{6,5},{7,6},{9,8},{10,9},{11,10},{12... | collective-permute-start | bytes 1695752 | tf_op jit(solution)/shard_map/ppermute | solution.py:548
  44.4 57.3 %collective-permute-start.2 = (f32[256,256]{1,0:T(8,128)}, f32[256,256]{1,0:T(8,128)S(1)}, u32[]{:S(2)}, u32[]{:S(2)}) collective-permute-start(f32[256,256]{1,0:T(8,128)} %get-tuple-element.23), channel_id=1, source_target_pairs={{0,1},{1,2},{2,3},{3,4},{4,5},{5,6},{6,7},{8,9},{9,10},{10,11},{11... | collective-permute-start | bytes 786440 | tf_op jit(solution)/shard_map/ppermute | solution.py:534
  49.9 57.8 %collective-permute-start.3 = (f32[256,256]{1,0:T(8,128)}, f32[256,256]{1,0:T(8,128)}, u32[]{:S(2)}, u32[]{:S(2)}) collective-permute-start(f32[256,256]{1,0:T(8,128)} %get-tuple-element.24), channel_id=1, source_target_pairs={{1,0},{2,1},{3,2},{4,3},{5,4},{6,5},{7,6},{9,8},{10,9},{11,10},{12... | collective-permute-start | bytes 786440 | tf_op jit(solution)/shard_map/ppermute | solution.py:535
  57.6 50.1 %copy-start.12 = (f32[1,1,256]{2,1,0:T(1,128)S(1)}, f32[1,1,256]{2,1,0:T(1,128)}, u32[]{:S(2)}) copy-start(f32[1,1,256]{2,1,0:T(1,128)} %param.11) | copy-start | bytes 3076
  57.6 50.1 %copy-start.13 = (f32[1,1,256]{2,1,0:T(1,128)S(1)}, f32[1,1,256]{2,1,0:T(1,128)}, u32[]{:S(2)}) copy-start(f32[1,1,256]{2,1,0:T(1,128)} %param.12) | copy-start | bytes 3076
  114.9 1.6 collective-permute-start.6
  117.4 7.0 %collective-permute-start.9 = (f32[136,128]{1,0:T(8,128)S(1)}, f32[136,128]{1,0:T(8,128)S(1)}, u32[]{:S(2)}, u32[]{:S(2)}) collective-permute-start(f32[136,128]{1,0:T(8,128)S(1)} %bitcast_add_fusion), channel_id=1, source_target_pairs={{0,48},{8,56},{16,32},{24,40},{32,16},{40,24},{48,0},{56,8},{64,11... | collective-permute-start | bytes 208904 | tf_op jit(solution)/shard_map/ppermute | solution.py:491
  119.4 7.2 %collective-permute-start.8 = (f32[136,128]{1,0:T(8,128)S(1)}, f32[136,128]{1,0:T(8,128)S(1)}, u32[]{:S(2)}, u32[]{:S(2)}) collective-permute-start(f32[136,128]{1,0:T(8,128)S(1)} %bitcast_add_fusion), channel_id=1, source_target_pairs={{0,32},{8,40},{16,48},{24,56},{32,0},{40,8},{48,16},{56,24},{64,96... | collective-permute-start | bytes 208904 | tf_op jit(solution)/shard_map/ppermute | solution.py:491
  119.4 7.2 %collective-permute-start.7 = (f32[136,128]{1,0:T(8,128)S(1)}, f32[136,128]{1,0:T(8,128)S(1)}, u32[]{:S(2)}, u32[]{:S(2)}) collective-permute-start(f32[136,128]{1,0:T(8,128)S(1)} %bitcast_add_fusion), channel_id=1, source_target_pairs={{0,16},{8,24},{16,0},{24,8},{32,48},{40,56},{48,32},{56,40},{64,80... | collective-permute-start | bytes 208904 | tf_op jit(solution)/shard_map/ppermute | solution.py:491
  126.6 6.4 %collective-permute-start.12 = (f32[136,128]{1,0:T(8,128)S(1)}, f32[136,128]{1,0:T(8,128)S(1)}, u32[]{:S(2)}, u32[]{:S(2)}) collective-permute-start(f32[136,128]{1,0:T(8,128)S(1)} %add_add_fusion.2), channel_id=1, source_target_pairs={{0,192},{8,200},{16,208},{24,216},{32,224},{40,232},{48,240},{56,2... | collective-permute-start | bytes 208904 | tf_op jit(solution)/shard_map/ppermute | solution.py:491
  128.1 5.8 %collective-permute-start.11 = (f32[136,128]{1,0:T(8,128)S(1)}, f32[136,128]{1,0:T(8,128)S(1)}, u32[]{:S(2)}, u32[]{:S(2)}) collective-permute-start(f32[136,128]{1,0:T(8,128)S(1)} %add_add_fusion.2), channel_id=1, source_target_pairs={{0,128},{8,136},{16,144},{24,152},{32,160},{40,168},{48,176},{56,1... | collective-permute-start | bytes 208904 | tf_op jit(solution)/shard_map/ppermute | solution.py:491
  128.9 5.2 %collective-permute-start.10 = (f32[136,128]{1,0:T(8,128)S(1)}, f32[136,128]{1,0:T(8,128)S(1)}, u32[]{:S(2)}, u32[]{:S(2)}) collective-permute-start(f32[136,128]{1,0:T(8,128)S(1)} %add_add_fusion.2), channel_id=1, source_target_pairs={{0,64},{8,72},{16,80},{24,88},{32,96},{40,104},{48,112},{56,120},{... | collective-permute-start | bytes 208904 | tf_op jit(solution)/shard_map/ppermute | solution.py:491
  134.1 5.1 %collective-permute-start.15 = (f32[136,128]{1,0:T(8,128)S(1)}, f32[136,128]{1,0:T(8,128)S(1)}, u32[]{:S(2)}, u32[]{:S(2)}) collective-permute-start(f32[136,128]{1,0:T(8,128)S(1)} %add_add_fusion.1), channel_id=1, source_target_pairs={{0,6},{1,7},{2,4},{3,5},{4,2},{5,3},{6,0},{7,1},{8,14},{9,15},{10,... | collective-permute-start | bytes 208904 | tf_op jit(solution)/shard_map/ppermute | solution.py:491
  135.6 5.8 %collective-permute-start.14 = (f32[136,128]{1,0:T(8,128)S(1)}, f32[136,128]{1,0:T(8,128)S(1)}, u32[]{:S(2)}, u32[]{:S(2)}) collective-permute-start(f32[136,128]{1,0:T(8,128)S(1)} %add_add_fusion.1), channel_id=1, source_target_pairs={{0,4},{1,5},{2,6},{3,7},{4,0},{5,1},{6,2},{7,3},{8,12},{9,13},{10,... | collective-permute-start | bytes 208904 | tf_op jit(solution)/shard_map/ppermute | solution.py:491
  135.6 5.8 %collective-permute-start.13 = (f32[136,128]{1,0:T(8,128)S(1)}, f32[136,128]{1,0:T(8,128)S(1)}, u32[]{:S(2)}, u32[]{:S(2)}) collective-permute-start(f32[136,128]{1,0:T(8,128)S(1)} %add_add_fusion.1), channel_id=1, source_target_pairs={{0,2},{1,3},{2,0},{3,1},{4,6},{5,7},{6,4},{7,5},{8,10},{9,11},{10,... | collective-permute-start | bytes 208904 | tf_op jit(solution)/shard_map/ppermute | solution.py:491
  141.5 8.5 %collective-permute-start.16 = (f32[136,128]{1,0:T(8,128)S(1)}, f32[136,128]{1,0:T(8,128)S(1)}, u32[]{:S(2)}, u32[]{:S(2)}) collective-permute-start(f32[136,128]{1,0:T(8,128)S(1)} %add_add_fusion), channel_id=1, source_target_pairs={{0,1},{1,0},{2,3},{3,2},{4,5},{5,4},{6,7},{7,6},{8,9},{9,8},{10,11... | collective-permute-start | bytes 208904 | tf_op jit(solution)/shard_map/ppermute | solution.py:491
  150.6 1.6 collective-permute-start.17
  153.2 45.0 %collective-permute-start.18 = (f32[256,256]{1,0:T(8,128)}, f32[256,256]{1,0:T(8,128)S(1)}, u32[]{:S(2)}, u32[]{:S(2)}) collective-permute-start(f32[256,256]{1,0:T(8,128)} %copy-done.15), channel_id=1, source_target_pairs={{0,1},{1,2},{2,3},{3,4},{4,5},{5,6},{6,7},{8,9},{9,10},{10,11},{11... | collective-permute-start | bytes 786440 | tf_op jit(solution)/shard_map/ppermute | solution.py:608
  159.8 38.3 %collective-permute-start.19 = (f32[256,256]{1,0:T(8,128)}, f32[256,256]{1,0:T(8,128)S(1)}, u32[]{:S(2)}, u32[]{:S(2)}) collective-permute-start(f32[256,256]{1,0:T(8,128)} %copy-done.14), channel_id=1, source_target_pairs={{1,0},{2,1},{3,2},{4,3},{5,4},{6,5},{7,6},{9,8},{10,9},{11,10},{12... | collective-permute-start | bytes 786440 | tf_op jit(solution)/shard_map/ppermute | solution.py:609
  (12 other events, 57.7 us)

commit v3 on v2

--- a/solution.py
+++ b/solution.py
@@ -23,6 +23,15 @@
 VM = pltpu.VMEM
 
 
+def each(trips, fn, together):
+    def turn(t, carry):
+        for j in range(together):
+            carry = fn(t * together + j, carry)
+        return carry
+
+    return lambda init: lax.fori_loop(0, trips // together, turn, init)
+
+
 def roll(x, shift):
     return pltpu.roll(x, shift % x.shape[1], 1)
 
@@ -40,30 +49,41 @@
     return lo[c, rows, :], hi[c, rows, :]
 
 
-def edges_kernel(lo, hi, bath, to_east, to_west, to_north, to_south):
+def flux_kernel(lo, hi, bath, to_north, to_south):
+    def chunk(q, carry):
+        out = pl.ds(pl.multiple_of(q * CH, CH), CH)
+        for i, ref in ((0, to_north), (ROWS - 1, to_south)):
+            a, b = field_rows(lo, hi, 0, q, i)
+            ref[out, :LANES] = a * bath[i : i + 1, :LANES]
+            ref[out, LANES:] = b * bath[i : i + 1, LANES:]
+        return carry
+
+    each(PER, chunk, 4)(0)
+
+
+def edges_kernel(lo, hi, bath, to_east, to_west):
     lane = lanes_of((CH, LANES))
+    first = jnp.zeros((CH, LANES), jnp.float32)
+    last = jnp.zeros((CH, LANES), jnp.float32)
+    place = lambda spot: (lane >= spot) & (lane < spot + 4)
+    for i in range(ROWS):
+        spot = 4 * (3 * ROWS + i)
+        a = jnp.broadcast_to(bath[i : i + 1, :LANES], (CH, LANES))
+        b = jnp.broadcast_to(bath[i : i + 1, LANES:], (CH, LANES))
+        first = jnp.where(place(spot), roll(a, spot), first)
+        last = jnp.where(place(spot), roll(b, spot + 4), last)
 
     def chunk(q, carry):
-        east = jnp.zeros((CH, LANES), jnp.float32)
-        west = jnp.zeros((CH, LANES), jnp.float32)
+        west, east = first, last
         out = pl.ds(pl.multiple_of(q * CH, CH), CH)
-        for c in range(4):
+        for c in range(3):
             for i in range(ROWS):
-                if c < 3:
-                    a, b = field_rows(lo, hi, c, q, i)
-                else:
-                    a = jnp.broadcast_to(bath[i : i + 1, :LANES], (CH, LANES))
-                    b = jnp.broadcast_to(bath[i : i + 1, LANES:], (CH, LANES))
+                a, b = field_rows(lo, hi, c, q, i)
                 spot = 4 * (c * ROWS + i)
-                here = (lane >= spot) & (lane < spot + 4)
-                west = jnp.where(here, roll(a, spot), west)
-                east = jnp.where(here, roll(b, spot + 4), east)
+                west = jnp.where(place(spot), roll(a, spot), west)
+                east = jnp.where(place(spot), roll(b, spot + 4), east)
         to_east[out, :] = east
         to_west[out, :] = west
-        for i, ref in ((0, to_north), (ROWS - 1, to_south)):
-            a, b = field_rows(lo, hi, 2, q, i)
-            ref[out, :LANES] = a * bath[i : i + 1, :LANES]
-            ref[out, LANES:] = b * bath[i : i + 1, LANES:]
         return carry
 
     each(PER, chunk, 2)(0)
@@ -86,7 +106,7 @@
     return jnp.concatenate([a, b, tail], axis=1)
 
 
-def border_kernel(nrows, lo, hi, bath, from_east, from_west, fcor, msg_n, msg_s, late_n, late_s, wide_bath):
+def border_kernel(nrows, lo, hi, bath, from_east, from_west, fcor, msg_n, msg_s, wide_bath):
     step = pl.program_id(0)
     base = lax.axis_index("lat") * nrows
 
@@ -107,29 +127,21 @@
         dst_q = pl.ds(pl.multiple_of(COLS + step * (CH * PER) + q * CH, CH), CH)
         e, w = from_east[out, :], from_west[out, :]
         new = []
-        for msg, late, first, sg, ext in (
-            (msg_n, late_n, 0, 1, carry[0]),
-            (msg_s, late_s, ROWS - 1, -1, carry[1]),
-        ):
-            rows = [first + sg * k for k in range(4)]
+        for msg, first, sg, ext in ((msg_n, 0, 1, carry[0]), (msg_s, ROWS - 1, -1, carry[1])):
+            rows = [first + sg * k for k in range(3)]
             H = [wide_bath[r] for r in rows]
             load = lambda c, k: wide_rows(lo, hi, e, w, lane, q, c, rows[k])
-            h = [load(0, k) for k in range(3)]
-            u = [load(1, k) for k in range(3)]
-            v = [load(2, k) for k in range(4)]
-            f0, f1 = fcor[base + rows[0]], fcor[base + rows[1]]
-            fy = [H[k] * v[k] for k in range(4)]
-            dfx = [ddx(H[k] * u[k]) for k in range(3)]
+            h = [load(0, k) for k in range(2)]
+            u = [load(1, k) for k in range(2)]
+            v = [load(2, k) for k in range(3)]
+            f0 = fcor[base + rows[0]]
+            fy = [H[k] * v[k] for k in range(3)]
+            dfx = [ddx(H[k] * u[k]) for k in range(2)]
             h1a = h[1] - 0.25 * (dfx[1] + sg * (fy[2] - fy[0]))
-            h1b = h[2] - 0.25 * (dfx[2] + sg * (fy[3] - fy[1]))
             part = h[0] - 0.25 * (dfx[0] + sg * fy[1])
             flux = H[0] * (v[0] - (0.5 * f0) * u[0] - (sg * 0.25) * h1a)
-            uz = u[0] + (0.5 * f0) * v[0] - 0.25 * ddx(part)
-            vz = v[1] - (0.5 * f1) * u[1] - (sg * 0.25) * (h1b - part)
-            rest = part - 0.25 * (ddx(H[0] * uz) + sg * (H[1] * vz))
             msg[dst, :] = part[:, :COLS]
             msg[dst_q, :] = flux[:, :COLS]
-            late[dst, :] = rest[:, :COLS]
             t = jnp.where(
                 lane < 8,
                 roll(fy[0][:, COLS:], 4),
@@ -170,16 +182,11 @@
 
 
 def local_kernel(
-    nrows, lo, hi, bath, from_east, from_west, fcor, index,
-    out, flux_edge, height_edge, wind_edge, seen, wide_bath, height,
+    nrows, lo, hi, wide_bath, from_east, from_west, fcor, index,
+    out, flux_edge, height_edge, wind_edge, seen, late_n, late_s, height,
 ):
     step = pl.program_id(0)
     base = lax.axis_index("lat") * nrows
-
-    @pl.when(step == 0)
-    def _():
-        bath_rows(bath, from_east, from_west, wide_bath)
-
     lane = lanes_of((CH, LANES))
 
     def across(y, i):
@@ -216,6 +223,8 @@
             out[1, i, loc, :] = u2[:, :COLS]
             out[2, i, loc, :] = v2[:, :COLS]
             height[i, dst, :] = h2[i][:, :COLS]
+        late_n[loc, :] = h2[0][:, :COLS]
+        late_s[loc, :] = h2[-1][:, :COLS]
         return carry
 
     lax.fori_loop(0, PER, chunk, 0)
@@ -245,16 +254,13 @@
         beyond[2 * k + 1, :, COLS:] = jnp.zeros((CH, LANES), jnp.float32)
 
 
-def edge_change(k, has, q, fy_msg, msg, flux_edge, height_edge, wide_bath, beyond):
+def edge_change(k, has, q, chunk, fy_row, part_row, flux_row, ext, flux_edge, height_edge, wide_bath, beyond):
     sg, e, n = ((-1, 0, 1), (1, ROWS - 1, ROWS - 2))[k]
-    chunk = q % PER
     rows = pl.ds(pl.multiple_of(q * CH, CH), CH)
-    rows_q = pl.ds(pl.multiple_of(COLS + q * CH, CH), CH)
-    t = msg[pl.ds(pl.multiple_of(EXT + (q // PER) * CH, CH), CH), :LANES]
-    t = pltpu.roll(t, (LANES - chunk * 16) % LANES, 1)
-    g0 = jnp.concatenate([fy_msg[rows, :], roll(t, -4)], axis=1)
-    part = jnp.concatenate([msg[rows, :], roll(t, -10)], axis=1)
-    flux = jnp.concatenate([msg[rows_q, :], roll(t, -14)], axis=1)
+    t = pltpu.roll(ext, (LANES - chunk * 16) % LANES, 1)
+    g0 = jnp.concatenate([fy_row, roll(t, -4)], axis=1)
+    part = jnp.concatenate([part_row, roll(t, -10)], axis=1)
+    flux = jnp.concatenate([flux_row, roll(t, -14)], axis=1)
     c = sg * 0.25
     eps = c * flux_edge[k, rows, :]
     dh1 = -c * g0
@@ -273,19 +279,23 @@
 
 def sums_kernel(
     ntiles, members, scale,
-    bath, from_east, from_west, fy_n, fy_s, msg_n, msg_s, flux_edge, height_edge, seen, index, count, value, sd,
-    sums, wide_bath, beyond, change,
+    wide_bath, fy_n, fy_s, msg_n, msg_s, flux_edge, height_edge, seen, index, count, value, sd,
+    mine, theirs, beyond, change, sums,
 ):
     tile = lax.axis_index("lat")
     has = (jnp.where(tile > 0, 1.0, 0.0), jnp.where(tile < ntiles - 1, 1.0, 0.0))
-    bath_rows(bath, from_east, from_west, wide_bath)
     beyond_rows((msg_n, msg_s), beyond)
     slots = index.shape[1]
 
     def chunk(q, carry):
         dst = pl.ds(pl.multiple_of(q * CH, CH), CH)
         for k, fy, msg in ((0, fy_n, msg_n), (1, fy_s, msg_s)):
-            new = edge_change(k, has[k], q, fy, msg, flux_edge, height_edge, wide_bath, beyond)
+            far = pl.ds(pl.multiple_of(COLS + q * CH, CH), CH)
+            ext = msg[pl.ds(pl.multiple_of(EXT + (q // PER) * CH, CH), CH), :LANES]
+            new = edge_change(
+                k, has[k], q, q % PER, fy[dst, :], msg[dst, :], msg[far, :], ext,
+                flux_edge, height_edge, wide_bath, beyond,
+            )
             for j in range(3):
                 change[3 * k + j, dst, :] = new[4 + j][:, :COLS]
         return carry
@@ -309,26 +319,31 @@
     sums[2 * n : 2 * n + 1, :] = jnp.sum(jnp.where(ln == sb, last, 0.0), axis=0, keepdims=True)
     sums[2 * n + 1 : 2 * n + 2, :] = proj[0:1, :n]
     sums[2 * n + 2 : 2 * n + 3, :] = proj[0:1, n:]
+    part = mine.shape[0]
+    core = lax.axis_index("lon") % 2
+    mine[...] = sums[pl.ds(pl.multiple_of(core * part, 8), part), :]
+    theirs[...] = sums[pl.ds(pl.multiple_of((1 - core) * part, 8), part), :]
 
 
 def complete_kernel(
-    nrows, ntiles, block,
-    bath, from_east, from_west, fcor, fy_n, fy_s, msg_n, msg_s, flux_edge, height_edge, wind_edge, fields,
-    out, wide_bath, beyond,
+    nrows, ntiles, first, wide_bath, beyond, fcor, fy_n, fy_s,
+    part_n, flux_n, ext_n, part_s, flux_s, ext_s, flux_edge, height_edge, wind_edge, fields, out,
 ):
     tile = lax.axis_index("lat")
     base = tile * nrows
     has = (jnp.where(tile > 0, 1.0, 0.0), jnp.where(tile < ntiles - 1, 1.0, 0.0))
-    bath_rows(bath, from_east, from_west, wide_bath)
-    beyond_rows((msg_n, msg_s), beyond)
 
     def chunk(q, carry):
         loc = pl.ds(pl.multiple_of(q * CH, CH), CH)
-        full = block * PER + q
-        rows = pl.ds(pl.multiple_of(full * CH, CH), CH)
-        for k, sg, e, fy, msg in ((0, -1, 0, fy_n, msg_n), (1, 1, ROWS - 1, fy_s, msg_s)):
+        rows = loc
+        there = pl.ds(pl.multiple_of(first + q * CH, CH), CH)
+        for k, sg, e, fy, part, flux, ext in (
+            (0, -1, 0, fy_n, part_n, flux_n, ext_n),
+            (1, 1, ROWS - 1, fy_s, part_s, flux_s, ext_s),
+        ):
             eps, du1, dv_e, dv_n, a, b, d = edge_change(
-                k, has[k], full, fy, msg, flux_edge, height_edge, wide_bath, beyond
+                k, has[k], q, q, fy[loc, :], part[loc, :], flux[loc, :], ext[:, :LANES],
+                flux_edge, height_edge, wide_bath, beyond,
             )
             c = sg * 0.25
             flow = wide_bath[e] * dv_e
@@ -351,12 +366,9 @@
                 (2, r[3], cut(-c * d)),
             )
             for i, j, x in upd:
-                out[i, j, loc, :] = fields[i, j, loc, :] + x
+                out[i, j, there, :] = fields[i, j, there, :] + x
         return carry
 
-    for i in range(2):
-        for j in (3, 4):
-            out[i, j] = fields[i, j]
     each(PER, chunk, 4)(0)
 
 
@@ -402,8 +414,12 @@
         A, X = list(out[: live - seg]), list(out[live : 2 * live - seg])
 
 
-def factor_kernel(members, g_ref, mix, inverse):
+def factor_kernel(members, mine, other, mix, inverse, g_ref):
     n = LANES
+    part = mine.shape[0]
+    core = lax.axis_index("lon") % 2
+    g_ref[pl.ds(pl.multiple_of(core * part, 8), part), :] = mine[...]
+    g_ref[pl.ds(pl.multiple_of((1 - core) * part, 8), part), :] = other[...]
     lane, sub = lanes_of((n, n)), lax.broadcasted_iota(jnp.int32, (n, n), 0)
     both = g_ref[0:n, :]
     g12 = g_ref[n : 2 * n, :]
@@ -450,15 +466,6 @@
         out[0, pl.ds(i, x.shape[0], stride=ROWS), :] = res
 
 
-def each(trips, fn, together):
-    def turn(t, carry):
-        for j in range(together):
-            carry = fn(t * together + j, carry)
-        return carry
-
-    return lambda init: lax.fori_loop(0, trips // together, turn, init)
-
-
 def whole(shape):
     return pl.BlockSpec(shape, lambda *_: (0,) * len(shape))
 
@@ -475,26 +482,25 @@
     return [1 << k for k in range(n.bit_length() - 1)]
 
 
-def total(x):
+def total(mine, theirs, late_n, late_s, south, north):
     nlon, nlat = lax.axis_size("lon"), lax.axis_size("lat")
-    half = x.reshape(2, x.shape[0] // 2, x.shape[1])
-    core = lax.axis_index("lon") % 2
-    mine = lax.dynamic_index_in_dim(half, core, 0, keepdims=False)
-    theirs = lax.dynamic_index_in_dim(half, 1 - core, 0, keepdims=False)
     y = mine + lax.ppermute(theirs, "lon", flips(nlon, 1))
-    stages = []
-    for axis, n, todo in (("lon", nlon, bits(nlon)[1:]), ("lat", nlat, bits(nlat)[1:] + bits(nlat)[:1])):
-        for k in range(0, len(todo), 2):
-            stages.append((axis, n, todo[k : k + 2]))
-    for axis, n, todo in stages:
+    lon, lat = bits(nlon), bits(nlat)
+    stages = [("lat", nlat, lat[:1]), ("lon", nlon, lon[1:3]), ("lon", nlon, lon[3:]), ("lat", nlat, lat[1:])]
+    late = []
+    for k, (axis, n, todo) in enumerate(stages):
         hops = todo if len(todo) == 1 else [todo[0], todo[1], todo[0] | todo[1]]
+        if k == 2:
+            y, late_s = lax.optimization_barrier((y, late_s))
+            late.append(lax.ppermute(late_s, "lat", south))
+        if k == 3:
+            y, late_n = lax.optimization_barrier((y, late_n))
+            late.append(lax.ppermute(late_n, "lat", north))
         parts = [lax.ppermute(y, axis, flips(n, b)) for b in hops]
         for p in parts:
             y = y + p
     other = lax.ppermute(y, "lon", flips(nlon, 1))
-    lo = jnp.where(core == 0, y, other)
-    hi = jnp.where(core == 0, other, y)
-    return jnp.concatenate([lo, hi], axis=0)
+    return y, other, late
 
 
 def body(state, bathymetry, obs_index, obs_count, obs_value, obs_sd):
@@ -515,32 +521,46 @@
     bath_spec = whole((ROWS, COLS))
     smem = pl.BlockSpec(memory_space=pltpu.SMEM)
 
-    to_east, to_west, to_north, to_south = pl.pallas_call(
-        edges_kernel,
-        grid=grid,
-        in_specs=state_specs + [bath_spec],
-        out_specs=[thin, thin, row, row],
-        out_shape=[f32(members, LANES)] * 2 + [f32(members, COLS)] * 2,
-        compiler_params=clip(24),
-        name="edges",
-    )(flat, flat, bathymetry)
-
+    wide_bath_shape = (ROWS, CH, WIDE)
     east = [(i, (i + 1) % nlon) for i in range(nlon)]
     west = [(j, i) for i, j in east]
     south = [(i, i + 1) for i in range(nlat - 1)]
     north = [(j, i) for i, j in south]
+
+    to_east, to_west = pl.pallas_call(
+        edges_kernel,
+        grid=grid,
+        in_specs=state_specs + [bath_spec],
+        out_specs=[thin, thin],
+        out_shape=[f32(members, LANES)] * 2,
+        compiler_params=clip(24),
+        name="edges",
+    )(flat, flat, bathymetry)
     from_west = lax.ppermute(to_east, "lon", east)
     from_east = lax.ppermute(to_west, "lon", west)
+
+    wind_specs = [
+        pl.BlockSpec((1, blk * ROWS, LANES), lambda s: (2, s, 0)),
+        pl.BlockSpec((1, blk * ROWS, LANES), lambda s: (2, s, 1)),
+    ]
+    to_north, to_south = pl.pallas_call(
+        flux_kernel,
+        grid=grid,
+        in_specs=wind_specs + [bath_spec],
+        out_specs=[row, row],
+        out_shape=[f32(members, COLS)] * 2,
+        compiler_params=clip(24),
+        name="flux",
+    )(flat, flat, bathymetry)
     fy_n = lax.ppermute(to_south, "lat", south)
     fy_s = lax.ppermute(to_north, "lat", north)
 
-    msg_n, msg_s, late_n, late_s = pl.pallas_call(
+    msg_n, msg_s, wide_bath = pl.pallas_call(
         functools.partial(border_kernel, ROWS),
         grid=grid,
         in_specs=state_specs + [bath_spec, thin, thin, smem],
-        out_specs=[whole((MSG, COLS))] * 2 + [whole((members, COLS))] * 2,
-        out_shape=[f32(MSG, COLS)] * 2 + [f32(members, COLS)] * 2,
-        scratch_shapes=[VM((ROWS, CH, WIDE), jnp.float32)],
+        out_specs=[whole((MSG, COLS))] * 2 + [whole(wide_bath_shape)],
+        out_shape=[f32(MSG, COLS)] * 2 + [f32(*wide_bath_shape)],
         compiler_params=clip(24),
         name="border",
     )(flat, flat, bathymetry, from_east, from_west, fcor)
@@ -551,72 +571,82 @@
     obs = whole((1, slots))
     edge = whole((2, members, WIDE))
     blocks = members // blk
-    wide_scratch = VM((ROWS, CH, WIDE), jnp.float32)
-    beyond_scratch = VM((4, CH, WIDE), jnp.float32)
-    fields, flux_edge, height_edge, wind_edge, seen = pl.pallas_call(
+    wb_spec, bey_spec = whole(wide_bath_shape), whole((4, CH, WIDE))
+    fields_shape = VM((3, ROWS, members, COLS), jnp.float32)
+    fields, flux_edge, height_edge, wind_edge, seen, late_n, late_s = pl.pallas_call(
         functools.partial(local_kernel, ROWS),
         grid=grid,
-        in_specs=state_specs + [bath_spec, thin, thin, smem, obs],
+        in_specs=state_specs + [wb_spec, thin, thin, smem, obs],
         out_specs=[
             pl.BlockSpec((3, ROWS, blk, COLS), lambda s: (0, 0, s, 0)),
             pl.BlockSpec((2, blk, WIDE), lambda s: (0, s, 0)),
             pl.BlockSpec((2, blk, WIDE), lambda s: (0, s, 0)),
             pl.BlockSpec((2, blk, COLS), lambda s: (0, s, 0)),
             whole((members, slots)),
+            row,
+            row,
         ],
         out_shape=[
-            pltpu.HBM((3, ROWS, members, COLS), jnp.float32), f32(2, members, WIDE), f32(2, members, WIDE),
-            f32(2, members, COLS), f32(members, slots),
+            fields_shape, f32(2, members, WIDE), f32(2, members, WIDE),
+            f32(2, members, COLS), f32(members, slots), f32(members, COLS), f32(members, COLS),
         ],
-        scratch_shapes=[wide_scratch, VM((ROWS, members, COLS), jnp.float32)],
+        scratch_shapes=[VM((ROWS, members, COLS), jnp.float32)],
         compiler_params=clip(24),
         name="local",
-    )(flat, flat, bathymetry, from_east, from_west, fcor, one(obs_index))
-
-    head = whole((CH, LANES))
-    got = (fy_n, fy_s, got_n, got_s, flux_edge, height_edge)
-    got_specs = [whole((members, COLS))] * 2 + [whole((MSG, COLS))] * 2 + [edge, edge]
-    sums = pl.pallas_call(
+    )(flat, flat, wide_bath, from_east, from_west, fcor, one(obs_index))
+
+    part = f32(136, LANES)
+    mine, theirs, beyond = pl.pallas_call(
         functools.partial(sums_kernel, nlat, members, math.sqrt(slots * nlat * nlon) / 16.0),
         grid=(1,),
-        in_specs=[bath_spec, head, head] + got_specs + [whole((members, slots)), obs, smem, obs, obs],
-        out_specs=whole((272, LANES)),
-        out_shape=f32(272, LANES),
-        scratch_shapes=[wide_scratch, beyond_scratch, VM((6, members, COLS), jnp.float32)],
+        in_specs=[wb_spec]
+        + [whole((members, COLS))] * 2
+        + [whole((MSG, COLS))] * 2
+        + [edge, edge, whole((members, slots)), obs, smem, obs, obs],
+        out_specs=[whole(part.shape), whole(part.shape), bey_spec],
+        out_shape=[part, part, f32(4, CH, WIDE)],
+        scratch_shapes=[VM((6, members, COLS), jnp.float32), VM((272, LANES), jnp.float32)],
         compiler_params=clip(24),
         name="sums",
     )(
-        bathymetry, from_east, from_west, *got, seen,
+        wide_bath, fy_n, fy_s, got_n, got_s, flux_edge, height_edge, seen,
         one(obs_index), obs_count, one(obs_value), one(obs_sd),
     )
 
     for k in range(blocks):
-        part = pl.BlockSpec((3, ROWS, blk, COLS), lambda s, k=k: (0, 0, k, 0))
+        at = lambda rows, j: pl.BlockSpec((rows, COLS), lambda s: (j, 0))
+        msg_specs = [at(blk, k), at(blk, COLS // blk + k), at(CH, EXT // CH + k)]
+        edge_k = pl.BlockSpec((2, blk, WIDE), lambda s, k=k: (0, k, 0))
+        wind_k = pl.BlockSpec((2, blk, COLS), lambda s, k=k: (0, k, 0))
+        here = pl.BlockSpec(memory_space=VM)
         fields = pl.pallas_call(
-            functools.partial(complete_kernel, ROWS, nlat, k),
+            functools.partial(complete_kernel, ROWS, nlat, k * blk),
             grid=(1,),
-            in_specs=[bath_spec, head, head, smem] + got_specs + [whole((2, members, COLS)), part],
-            out_specs=part,
-            out_shape=pltpu.HBM((3, ROWS, members, COLS), jnp.float32),
-            scratch_shapes=[wide_scratch, beyond_scratch],
-            input_output_aliases={11: 0},
+            in_specs=[wb_spec, bey_spec, smem, at(blk, k), at(blk, k)]
+            + msg_specs * 2
+            + [edge_k, edge_k, wind_k, here],
+            out_specs=here,
+            out_shape=fields_shape,
+            input_output_aliases={14: 0},
             compiler_params=clip(24),
             name="complete",
-        )(bathymetry, from_east, from_west, fcor, *got, wind_edge, fields)
-
-    sums, late_n, late_s = lax.optimization_barrier((total(sums), late_n, late_s))
-    late_from_n = lax.ppermute(late_s, "lat", south)
-    late_from_s = lax.ppermute(late_n, "lat", north)
+        )(
+            wide_bath, beyond, fcor, fy_n, fy_s, got_n, got_n, got_n, got_s, got_s, got_s,
+            flux_edge, height_edge, wind_edge, fields,
+        )
+
+    sum_mine, sum_other, late = total(mine, theirs, late_n, late_s, south, north)
+    fields = pltpu.with_memory_space_constraint(fields, pltpu.VMEM)
 
     mix = pl.pallas_call(
         functools.partial(factor_kernel, members),
         out_shape=f32(members, members),
-        in_specs=[pl.BlockSpec(memory_space=VM)],
+        in_specs=[pl.BlockSpec(memory_space=VM)] * 2,
         out_specs=pl.BlockSpec(memory_space=VM),
-        scratch_shapes=[VM((members, LANES), jnp.float32)],
+        scratch_shapes=[VM((members, LANES), jnp.float32), VM((272, LANES), jnp.float32)],
         compiler_params=clip(8),
         name="factor",
-    )(sums)
+    )(sum_mine, sum_other)
 
     half = pl.BlockSpec((members, LANES), lambda c, j: (0, j))
     analysis = pl.pallas_call(
@@ -632,7 +662,7 @@
         out_shape=f32(3, members * ROWS, COLS),
         compiler_params=clip(24),
         name="mix",
-    )(mix, fields, late_from_n, late_from_s)
+    )(mix, fields, *late)
     return analysis.reshape(state.shape)
 
 

time: 209 us -> 179 us (0.86)
  Pallas kernels: 81 us -> 67.4 us
  local copies, waits for them, and re-layouts: 9.82 us -> 0.72 us
  waiting for transfers between devices: 59 us -> 53.4 us
  other arithmetic: 2.57 us -> 0.09 us
    unnamed x32 -> x10, local copies, waits for them, and re-layouts: 9.2 us -> 0.72 us
    pallas_call x4 -> x5, Pallas kernels: 19.8 us -> 13.6 us  [the longest x4 11.2 us: body(): pl.pallas_call(functools.partial(complete_kernel, ROWS, nlat, k * blk), g...]
    pallas_call x1, Pallas kernels: 11 us -> 6.09 us  [body(): pl.pallas_call(functools.partial(border_kernel, ROWS), grid=grid, in_spec...]
    ppermute x10, waiting for transfers between devices: 15.3 us -> 11.8 us  [total(): parts = [lax.ppermute(y, axis, flips(n, b)) for b in hops]]
  transfers between devices with their start and end apart: 20 -> 20, of which waited for: 14 -> 10; matrix products, arithmetic and copies ran while one was open for 0% -> 0% of each run, Pallas kernels for 24% -> 25%
where the time goes in v3:
time: 179 us; the launch traced here: 178 us
  Pallas kernels  67.4 us (38%)
  starting transfers between devices  55.5 us (31%)
  waiting for transfers between devices  53.4 us (30%)
    ppermute x1, waiting for transfers between devices, body(): fy_n = lax.ppermute(to_south, 'lat', south)  26 us
    pallas_call x1, Pallas kernels, body(): pl.pallas_call(functools.partial(local_kernel, ROWS), grid=grid, in_specs...  17.4 us
    ppermute x10, starting transfers between devices, total(): parts = [lax.ppermute(y, axis, flips(n, b)) for b in hops]  17.2 us
    pallas_call x1, Pallas kernels, body(): pl.pallas_call(functools.partial(factor_kernel, members), out_shape=f32(m...  12.7 us
    ppermute x10, waiting for transfers between devices, total(): parts = [lax.ppermute(y, axis, flips(n, b)) for b in hops]  11.8 us
    pallas_call x4, Pallas kernels, body(): pl.pallas_call(functools.partial(complete_kernel, ROWS, nlat, k * blk), g...  11.2 us
    pallas_call x1, Pallas kernels, body(): pl.pallas_call(apply_kernel, grid=(3, COLS // LANES), in_specs=[whole((me...  7.58 us
    ppermute x1, starting transfers between devices, body(): got_n = lax.ppermute(msg_s, 'lat', south)  6.4 us
  transfers between devices with their start and end apart: 20, of which 10 were waited for; matrix products, arithmetic and copies ran while one was open for 0% of the time, Pallas kernels for 25%

profile of v3, /device:TPU:8, one launch (start us, length us, event | category | flops | bytes accessed | tf_op | source)
XLA Modules:
  0.0 178.0 jit_solution(17776887204482923264)
XLA Ops:
  0.7 5.3 %edges.1 = (f32[256,128]{1,0:T(8,128)S(1)}, f32[256,128]{1,0:T(8,128)S(1)}) custom-call(f32[3,2048,256]{2,1,0:T(8,128)} %bitcast.9, f32[3,2048,256]{2,1,0:T(8,128)} %bitcast.10, f32[8,256]{1,0:T(8,128)S(1)} %copy-done), custom_call_target="tpu_custom_call" | custom-call | tf_op jit(solution)/shard_map/edges/pallas_call | solution.py:530
  6.0 6.3 %collective-permute-start = (f32[256,128]{1,0:T(8,128)S(1)}, f32[256,128]{1,0:T(8,128)S(1)}, u32[]{:S(2)}, u32[]{:S(2)}) collective-permute-start(f32[256,128]{1,0:T(8,128)S(1)} %get-tuple-element.26), channel_id=1, source_target_pairs={{8,0},{16,8},{24,16},{32,24},{40,32},{48,40},{56,48},{64,56},{72,6... | collective-permute-start | bytes 393224 | tf_op jit(solution)/shard_map/ppermute | solution.py:540
  12.3 2.5 %collective-permute-done.from_east = f32[256,128]{1,0:T(8,128)S(1)} collective-permute-done((f32[256,128]{1,0:T(8,128)S(1)}, f32[256,128]{1,0:T(8,128)S(1)}, u32[]{:S(2)}, u32[]{:S(2)}) %collective-permute-start) | collective-permute-done | bytes 131104 | tf_op jit(solution)/shard_map/ppermute | solution.py:540
  14.8 5.8 %collective-permute-done.1.from_west = f32[256,128]{1,0:T(8,128)S(1)} collective-permute-done((f32[256,128]{1,0:T(8,128)S(1)}, f32[256,128]{1,0:T(8,128)S(1)}, u32[]{:S(2)}, u32[]{:S(2)}) %collective-permute-start.1) | collective-permute-done | bytes 131104 | tf_op jit(solution)/shard_map/ppermute | solution.py:539
  20.6 6.1 %border.1 = (f32[552,256]{1,0:T(8,128)S(1)}, f32[552,256]{1,0:T(8,128)S(1)}, f32[8,8,384]{2,1,0:T(8,128)S(1)}) custom-call(f32[3,2048,256]{2,1,0:T(8,128)} %bitcast.11, f32[3,2048,256]{2,1,0:T(8,128)} %bitcast.12, f32[8,256]{1,0:T(8,128)S(1)} %copy-done, f32[256,128]{1,0:T(8,128)S(1)} %collective-permute-done.from_east, ...), custom_call_target="tpu_custom_call" | custom-call | tf_op jit(solution)/shard_map/border/pallas_call | solution.py:558
  26.7 6.4 %collective-permute-start.4 = (f32[552,256]{1,0:T(8,128)S(1)}, f32[552,256]{1,0:T(8,128)S(1)}, u32[]{:S(2)}, u32[]{:S(2)}) collective-permute-start(f32[552,256]{1,0:T(8,128)S(1)} %get-tuple-element.31), channel_id=1, source_target_pairs={{0,1},{1,2},{2,3},{3,4},{4,5},{5,6},{6,7},{8,9},{9,10},{10,11},{11... | collective-permute-start | bytes 1695752 | tf_op jit(solution)/shard_map/ppermute | solution.py:567
  33.1 4.2 %collective-permute-start.5 = (f32[552,256]{1,0:T(8,128)S(1)}, f32[552,256]{1,0:T(8,128)S(1)}, u32[]{:S(2)}, u32[]{:S(2)}) collective-permute-start(f32[552,256]{1,0:T(8,128)S(1)} %get-tuple-element.32), channel_id=1, source_target_pairs={{1,0},{2,1},{3,2},{4,3},{5,4},{6,5},{7,6},{9,8},{10,9},{11,10},{12... | collective-permute-start | bytes 1695752 | tf_op jit(solution)/shard_map/ppermute | solution.py:568
  39.7 5.5 %collective-permute-start.2 = (f32[256,256]{1,0:T(8,128)S(1)}, f32[256,256]{1,0:T(8,128)S(1)}, u32[]{:S(2)}, u32[]{:S(2)}) collective-permute-start(f32[256,256]{1,0:T(8,128)S(1)} %get-tuple-element.29), channel_id=1, source_target_pairs={{0,1},{1,2},{2,3},{3,4},{4,5},{5,6},{6,7},{8,9},{9,10},{10,11},{11... | collective-permute-start | bytes 786440 | tf_op jit(solution)/shard_map/ppermute | solution.py:555
  45.3 5.1 %collective-permute-start.3 = (f32[256,256]{1,0:T(8,128)S(1)}, f32[256,256]{1,0:T(8,128)S(1)}, u32[]{:S(2)}, u32[]{:S(2)}) collective-permute-start(f32[256,256]{1,0:T(8,128)S(1)} %get-tuple-element.30), channel_id=1, source_target_pairs={{1,0},{2,1},{3,2},{4,3},{5,4},{6,5},{7,6},{9,8},{10,9},{11,10},{12... | collective-permute-start | bytes 786440 | tf_op jit(solution)/shard_map/ppermute | solution.py:556
  51.1 17.4 %local.1 = (f32[3,8,256,256]{3,2,1,0:T(8,128)S(1)}, f32[2,256,384]{2,1,0:T(8,128)S(1)}, f32[2,256,384]{2,1,0:T(8,128)S(1)}, f32[2,256,256]{2,1,0:T(8,128)S(1)}, ...) custom-call(f32[3,2048,256]{2,1,0:T(8,128)} %bitcast.15, f32[3,2048,256]{2,1,0:T(8,128)} %bitcast.16, ...), custom_call_target="tpu_custom_call" | custom-call | tf_op jit(solution)/shard_map/local/pallas_call | solution.py:576
  68.5 26.0 %collective-permute-done.2.fy_n = f32[256,256]{1,0:T(8,128)S(1)} collective-permute-done((f32[256,256]{1,0:T(8,128)S(1)}, f32[256,256]{1,0:T(8,128)S(1)}, u32[]{:S(2)}, u32[]{:S(2)}) %collective-permute-start.2) | collective-permute-done | bytes 262176 | tf_op jit(solution)/shard_map/ppermute | solution.py:555
  94.4 6.0 %collective-permute-done.3.fy_s = f32[256,256]{1,0:T(8,128)S(1)} collective-permute-done((f32[256,256]{1,0:T(8,128)S(1)}, f32[256,256]{1,0:T(8,128)S(1)}, u32[]{:S(2)}, u32[]{:S(2)}) %collective-permute-start.3) | collective-permute-done | bytes 262176 | tf_op jit(solution)/shard_map/ppermute | solution.py:556
  100.5 4.8 %sums.1 = (f32[136,128]{1,0:T(8,128)S(1)}, f32[136,128]{1,0:T(8,128)S(1)}, f32[4,8,384]{2,1,0:T(8,128)S(1)}) custom-call(f32[8,8,384]{2,1,0:T(8,128)S(1)} %get-tuple-element.28.wide_bath, f32[256,256]{1,0:T(8,128)S(1)} %collective-permute-done.2.fy_n, f32[256,256]{1,0:T(8,128)S(1)} %collective-permute-done.3.fy_s, ...), custom_call_target="tpu_custom_call" | custom-call | tf_op jit(solution)/shard_map/sums/pallas_call | solution.py:599
  106.6 4.3 %collective-permute-start.7 = (f32[136,128]{1,0:T(8,128)S(1)}, f32[136,128]{1,0:T(8,128)S(1)}, u32[]{:S(2)}, u32[]{:S(2)}) collective-permute-start(f32[136,128]{1,0:T(8,128)S(1)} %add.33), channel_id=1, source_target_pairs={{0,1},{1,0},{2,3},{3,2},{4,5},{5,4},{6,7},{7,6},{8,9},{9,8},{10,11... | collective-permute-start | bytes 208904 | tf_op jit(solution)/shard_map/ppermute | solution.py:499
  110.9 4.0 %collective-permute-done.7 = f32[136,128]{1,0:T(8,128)S(1)} collective-permute-done((f32[136,128]{1,0:T(8,128)S(1)}, f32[136,128]{1,0:T(8,128)S(1)}, u32[]{:S(2)}, u32[]{:S(2)}) %collective-permute-start.7) | collective-permute-done | bytes 69664 | tf_op jit(solution)/shard_map/ppermute | solution.py:499
  122.9 2.6 %collective-permute-start.13 = (f32[136,128]{1,0:T(8,128)S(1)}, f32[136,128]{1,0:T(8,128)S(1)}, u32[]{:S(2)}, u32[]{:S(2)}) collective-permute-start(f32[136,128]{1,0:T(8,128)S(1)} %add_add_fusion.2), channel_id=1, source_target_pairs={{0,192},{8,200},{16,208},{24,216},{32,224},{40,232},{48,240},{56,2... | collective-permute-start | bytes 208904 | tf_op jit(solution)/shard_map/ppermute | solution.py:499
  135.6 6.0 %collective-permute-start.18 = (f32[256,256]{1,0:T(8,128)S(1)}, f32[256,256]{1,0:T(8,128)S(1)}, u32[]{:S(2)}, u32[]{:S(2)}) collective-permute-start(f32[256,256]{1,0:T(8,128)S(1)} %get-tuple-element.45), channel_id=1, source_target_pairs={{0,1},{1,2},{2,3},{3,4},{4,5},{5,6},{6,7},{8,9},{9,10},{10,11},{11... | collective-permute-start | bytes 786440 | tf_op jit(solution)/shard_map/ppermute | solution.py:495
  141.6 4.6 %collective-permute-start.19 = (f32[256,256]{1,0:T(8,128)S(1)}, f32[256,256]{1,0:T(8,128)S(1)}, u32[]{:S(2)}, u32[]{:S(2)}) collective-permute-start(f32[256,256]{1,0:T(8,128)S(1)} %get-tuple-element.46), channel_id=1, source_target_pairs={{1,0},{2,1},{3,2},{4,3},{5,4},{6,5},{7,6},{9,8},{10,9},{11,10},{12... | collective-permute-start | bytes 786440 | tf_op jit(solution)/shard_map/ppermute | solution.py:498
  146.4 2.8 %complete.4.fields = f32[3,8,256,256]{3,2,1,0:T(8,128)S(1)} custom-call(f32[8,8,384]{2,1,0:T(8,128)S(1)} %get-tuple-element.28.wide_bath, f32[4,8,384]{2,1,0:T(8,128)S(1)} %get-tuple-element.42.beyond, f32[64]{0:T(128)S(1)} %copy-done.1, f32[256,256]{1,0:T(8,128)S(1)} %collective-permute-done.2.fy_n, ...), custom_call_target="tpu_custom_call", output_to_operand_aliasing={{}: (14, {})} | custom-call | tf_op jit(solution)/shard_map/complete/pallas_call | solution.py:622
  149.2 2.8 %complete.5.fields = f32[3,8,256,256]{3,2,1,0:T(8,128)S(1)} custom-call(f32[8,8,384]{2,1,0:T(8,128)S(1)} %get-tuple-element.28.wide_bath, f32[4,8,384]{2,1,0:T(8,128)S(1)} %get-tuple-element.42.beyond, f32[64]{0:T(128)S(1)} %copy-done.1, f32[256,256]{1,0:T(8,128)S(1)} %collective-permute-done.2.fy_n, ...), custom_call_target="tpu_custom_call", output_to_operand_aliasing={{}: (14, {})} | custom-call | tf_op jit(solution)/shard_map/complete/pallas_call | solution.py:622
  152.0 2.8 %complete.6.fields = f32[3,8,256,256]{3,2,1,0:T(8,128)S(1)} custom-call(f32[8,8,384]{2,1,0:T(8,128)S(1)} %get-tuple-element.28.wide_bath, f32[4,8,384]{2,1,0:T(8,128)S(1)} %get-tuple-element.42.beyond, f32[64]{0:T(128)S(1)} %copy-done.1, f32[256,256]{1,0:T(8,128)S(1)} %collective-permute-done.2.fy_n, ...), custom_call_target="tpu_custom_call", output_to_operand_aliasing={{}: (14, {})} | custom-call | tf_op jit(solution)/shard_map/complete/pallas_call | solution.py:622
  154.8 2.8 %complete.7.fields = f32[3,8,256,256]{3,2,1,0:T(8,128)S(1)} custom-call(f32[8,8,384]{2,1,0:T(8,128)S(1)} %get-tuple-element.28.wide_bath, f32[4,8,384]{2,1,0:T(8,128)S(1)} %get-tuple-element.42.beyond, f32[64]{0:T(128)S(1)} %copy-done.1, f32[256,256]{1,0:T(8,128)S(1)} %collective-permute-done.2.fy_n, ...), custom_call_target="tpu_custom_call", output_to_operand_aliasing={{}: (14, {})} | custom-call | tf_op jit(solution)/shard_map/complete/pallas_call | solution.py:622
  157.7 12.7 %factor.1.mix = f32[256,256]{1,0:T(8,128)S(1)} custom-call(f32[136,128]{1,0:T(8,128)S(1)} %add_add_fusion.mine, f32[136,128]{1,0:T(8,128)S(1)} %collective-permute-done.17.other), custom_call_target="tpu_custom_call" | custom-call | tf_op jit(solution)/shard_map/factor/pallas_call | solution.py:641
  170.4 7.6 %mix.1 = f32[3,2048,256]{2,1,0:T(8,128)} custom-call(f32[256,256]{1,0:T(8,128)S(1)} %factor.1.mix, f32[3,8,256,256]{3,2,1,0:T(8,128)S(1)} %complete.7.fields, f32[256,256]{1,0:T(8,128)S(1)} %collective-permute-done.18.late_n, f32[256,256]{1,0:T(8,128)S(1)} %collective-permute-done.19.late_s), custom_call_target="tpu_custom_call" | custom-call | tf_op jit(solution)/shard_map/mix/pallas_call | solution.py:652
  (42 shorter events, 22.5 us)
Async XLA Ops:
  0.7 19.9 %copy-start.1 = (f32[64]{0:T(128)S(1)}, f32[64]{0:T(128)}, u32[]{:S(2)}) copy-start(f32[64]{0:T(128)} %constant.2.clone.fcor) | copy-start | bytes 772
  6.0 8.9 %collective-permute-start = (f32[256,128]{1,0:T(8,128)S(1)}, f32[256,128]{1,0:T(8,128)S(1)}, u32[]{:S(2)}, u32[]{:S(2)}) collective-permute-start(f32[256,128]{1,0:T(8,128)S(1)} %get-tuple-element.26), channel_id=1, source_target_pairs={{8,0},{16,8},{24,16},{32,24},{40,32},{48,40},{56,48},{64,56},{72,6... | collective-permute-start | bytes 393224 | tf_op jit(solution)/shard_map/ppermute | solution.py:540
  12.3 8.3 %collective-permute-start.1 = (f32[256,128]{1,0:T(8,128)S(1)}, f32[256,128]{1,0:T(8,128)S(1)}, u32[]{:S(2)}, u32[]{:S(2)}) collective-permute-start(f32[256,128]{1,0:T(8,128)S(1)} %get-tuple-element.27), channel_id=1, source_target_pairs={{0,8},{8,16},{16,24},{24,32},{32,40},{40,48},{48,56},{56,64},{64,7... | collective-permute-start | bytes 393224 | tf_op jit(solution)/shard_map/ppermute | solution.py:539
  26.7 73.7 %collective-permute-start.4 = (f32[552,256]{1,0:T(8,128)S(1)}, f32[552,256]{1,0:T(8,128)S(1)}, u32[]{:S(2)}, u32[]{:S(2)}) collective-permute-start(f32[552,256]{1,0:T(8,128)S(1)} %get-tuple-element.31), channel_id=1, source_target_pairs={{0,1},{1,2},{2,3},{3,4},{4,5},{5,6},{6,7},{8,9},{9,10},{10,11},{11... | collective-permute-start | bytes 1695752 | tf_op jit(solution)/shard_map/ppermute | solution.py:567
  33.1 17.9 %copy-start.2 = (s32[1,1,256]{2,1,0:T(1,128)S(1)}, s32[1,1,256]{2,1,0:T(1,128)}, u32[]{:S(2)}) copy-start(s32[1,1,256]{2,1,0:T(1,128)} %param.9) | copy-start | bytes 3076
  33.1 67.3 %collective-permute-start.5 = (f32[552,256]{1,0:T(8,128)S(1)}, f32[552,256]{1,0:T(8,128)S(1)}, u32[]{:S(2)}, u32[]{:S(2)}) collective-permute-start(f32[552,256]{1,0:T(8,128)S(1)} %get-tuple-element.32), channel_id=1, source_target_pairs={{1,0},{2,1},{3,2},{4,3},{5,4},{6,5},{7,6},{9,8},{10,9},{11,10},{12... | collective-permute-start | bytes 1695752 | tf_op jit(solution)/shard_map/ppermute | solution.py:568
  39.7 54.7 %collective-permute-start.2 = (f32[256,256]{1,0:T(8,128)S(1)}, f32[256,256]{1,0:T(8,128)S(1)}, u32[]{:S(2)}, u32[]{:S(2)}) collective-permute-start(f32[256,256]{1,0:T(8,128)S(1)} %get-tuple-element.29), channel_id=1, source_target_pairs={{0,1},{1,2},{2,3},{3,4},{4,5},{5,6},{6,7},{8,9},{9,10},{10,11},{11... | collective-permute-start | bytes 786440 | tf_op jit(solution)/shard_map/ppermute | solution.py:555
  45.3 55.2 %collective-permute-start.3 = (f32[256,256]{1,0:T(8,128)S(1)}, f32[256,256]{1,0:T(8,128)S(1)}, u32[]{:S(2)}, u32[]{:S(2)}) collective-permute-start(f32[256,256]{1,0:T(8,128)S(1)} %get-tuple-element.30), channel_id=1, source_target_pairs={{1,0},{2,1},{3,2},{4,3},{5,4},{6,5},{7,6},{9,8},{10,9},{11,10},{12... | collective-permute-start | bytes 786440 | tf_op jit(solution)/shard_map/ppermute | solution.py:556
  51.1 49.4 %copy-start.3 = (f32[1,1,256]{2,1,0:T(1,128)S(1)}, f32[1,1,256]{2,1,0:T(1,128)}, u32[]{:S(2)}) copy-start(f32[1,1,256]{2,1,0:T(1,128)} %param.11) | copy-start | bytes 3076
  51.1 49.4 %copy-start.4 = (f32[1,1,256]{2,1,0:T(1,128)S(1)}, f32[1,1,256]{2,1,0:T(1,128)}, u32[]{:S(2)}) copy-start(f32[1,1,256]{2,1,0:T(1,128)} %param.12) | copy-start | bytes 3076
  105.3 1.3 collective-permute-start.6
  106.6 8.3 %collective-permute-start.7 = (f32[136,128]{1,0:T(8,128)S(1)}, f32[136,128]{1,0:T(8,128)S(1)}, u32[]{:S(2)}, u32[]{:S(2)}) collective-permute-start(f32[136,128]{1,0:T(8,128)S(1)} %add.33), channel_id=1, source_target_pairs={{0,1},{1,0},{2,3},{3,2},{4,5},{5,4},{6,7},{7,6},{8,9},{9,8},{10,11... | collective-permute-start | bytes 208904 | tf_op jit(solution)/shard_map/ppermute | solution.py:499
  114.9 6.5 %collective-permute-start.10 = (f32[136,128]{1,0:T(8,128)S(1)}, f32[136,128]{1,0:T(8,128)S(1)}, u32[]{:S(2)}, u32[]{:S(2)}) collective-permute-start(f32[136,128]{1,0:T(8,128)S(1)} %add.34), channel_id=1, source_target_pairs={{0,48},{8,56},{16,32},{24,40},{32,16},{40,24},{48,0},{56,8},{64,11... | collective-permute-start | bytes 208904 | tf_op jit(solution)/shard_map/ppermute | solution.py:499
  117.0 5.9 %collective-permute-start.9 = (f32[136,128]{1,0:T(8,128)S(1)}, f32[136,128]{1,0:T(8,128)S(1)}, u32[]{:S(2)}, u32[]{:S(2)}) collective-permute-start(f32[136,128]{1,0:T(8,128)S(1)} %add.34), channel_id=1, source_target_pairs={{0,32},{8,40},{16,48},{24,56},{32,0},{40,8},{48,16},{56,24},{64,96... | collective-permute-start | bytes 208904 | tf_op jit(solution)/shard_map/ppermute | solution.py:499
  117.0 5.9 %collective-permute-start.8 = (f32[136,128]{1,0:T(8,128)S(1)}, f32[136,128]{1,0:T(8,128)S(1)}, u32[]{:S(2)}, u32[]{:S(2)}) collective-permute-start(f32[136,128]{1,0:T(8,128)S(1)} %add.34), channel_id=1, source_target_pairs={{0,16},{8,24},{16,0},{24,8},{32,48},{40,56},{48,32},{56,40},{64,80... | collective-permute-start | bytes 208904 | tf_op jit(solution)/shard_map/ppermute | solution.py:499
  122.9 6.4 %collective-permute-start.13 = (f32[136,128]{1,0:T(8,128)S(1)}, f32[136,128]{1,0:T(8,128)S(1)}, u32[]{:S(2)}, u32[]{:S(2)}) collective-permute-start(f32[136,128]{1,0:T(8,128)S(1)} %add_add_fusion.2), channel_id=1, source_target_pairs={{0,192},{8,200},{16,208},{24,216},{32,224},{40,232},{48,240},{56,2... | collective-permute-start | bytes 208904 | tf_op jit(solution)/shard_map/ppermute | solution.py:499
  125.6 5.8 %collective-permute-start.12 = (f32[136,128]{1,0:T(8,128)S(1)}, f32[136,128]{1,0:T(8,128)S(1)}, u32[]{:S(2)}, u32[]{:S(2)}) collective-permute-start(f32[136,128]{1,0:T(8,128)S(1)} %add_add_fusion.2), channel_id=1, source_target_pairs={{0,128},{8,136},{16,144},{24,152},{32,160},{40,168},{48,176},{56,1... | collective-permute-start | bytes 208904 | tf_op jit(solution)/shard_map/ppermute | solution.py:499
  126.4 5.0 %collective-permute-start.11 = (f32[136,128]{1,0:T(8,128)S(1)}, f32[136,128]{1,0:T(8,128)S(1)}, u32[]{:S(2)}, u32[]{:S(2)}) collective-permute-start(f32[136,128]{1,0:T(8,128)S(1)} %add_add_fusion.2), channel_id=1, source_target_pairs={{0,64},{8,72},{16,80},{24,88},{32,96},{40,104},{48,112},{56,120},{... | collective-permute-start | bytes 208904 | tf_op jit(solution)/shard_map/ppermute | solution.py:499
  131.4 14.8 %collective-permute-start.16 = (f32[136,128]{1,0:T(8,128)S(1)}, f32[136,128]{1,0:T(8,128)S(1)}, u32[]{:S(2)}, u32[]{:S(2)}) collective-permute-start(f32[136,128]{1,0:T(8,128)S(1)} %add_add_fusion.1), channel_id=1, source_target_pairs={{0,6},{1,7},{2,4},{3,5},{4,2},{5,3},{6,0},{7,1},{8,14},{9,15},{10,... | collective-permute-start | bytes 208904 | tf_op jit(solution)/shard_map/ppermute | solution.py:499
  132.6 13.7 %collective-permute-start.15 = (f32[136,128]{1,0:T(8,128)S(1)}, f32[136,128]{1,0:T(8,128)S(1)}, u32[]{:S(2)}, u32[]{:S(2)}) collective-permute-start(f32[136,128]{1,0:T(8,128)S(1)} %add_add_fusion.1), channel_id=1, source_target_pairs={{0,4},{1,5},{2,6},{3,7},{4,0},{5,1},{6,2},{7,3},{8,12},{9,13},{10,... | collective-permute-start | bytes 208904 | tf_op jit(solution)/shard_map/ppermute | solution.py:499
  133.4 12.9 %collective-permute-start.14 = (f32[136,128]{1,0:T(8,128)S(1)}, f32[136,128]{1,0:T(8,128)S(1)}, u32[]{:S(2)}, u32[]{:S(2)}) collective-permute-start(f32[136,128]{1,0:T(8,128)S(1)} %add_add_fusion.1), channel_id=1, source_target_pairs={{0,2},{1,3},{2,0},{3,1},{4,6},{5,7},{6,4},{7,5},{8,10},{9,11},{10,... | collective-permute-start | bytes 208904 | tf_op jit(solution)/shard_map/ppermute | solution.py:499
  135.6 34.8 %collective-permute-start.18 = (f32[256,256]{1,0:T(8,128)S(1)}, f32[256,256]{1,0:T(8,128)S(1)}, u32[]{:S(2)}, u32[]{:S(2)}) collective-permute-start(f32[256,256]{1,0:T(8,128)S(1)} %get-tuple-element.45), channel_id=1, source_target_pairs={{0,1},{1,2},{2,3},{3,4},{4,5},{5,6},{6,7},{8,9},{9,10},{10,11},{11... | collective-permute-start | bytes 786440 | tf_op jit(solution)/shard_map/ppermute | solution.py:495
  141.6 28.8 %collective-permute-start.19 = (f32[256,256]{1,0:T(8,128)S(1)}, f32[256,256]{1,0:T(8,128)S(1)}, u32[]{:S(2)}, u32[]{:S(2)}) collective-permute-start(f32[256,256]{1,0:T(8,128)S(1)} %get-tuple-element.46), channel_id=1, source_target_pairs={{1,0},{2,1},{3,2},{4,3},{5,4},{6,5},{7,6},{9,8},{10,9},{11,10},{12... | collective-permute-start | bytes 786440 | tf_op jit(solution)/shard_map/ppermute | solution.py:498
  146.3 11.4 %collective-permute-start.17 = (f32[136,128]{1,0:T(8,128)S(1)}, f32[136,128]{1,0:T(8,128)S(1)}, u32[]{:S(2)}, u32[]{:S(2)}) collective-permute-start(f32[136,128]{1,0:T(8,128)S(1)} %add_add_fusion.mine), channel_id=1, source_target_pairs={{0,8},{8,0},{16,24},{24,16},{32,40},{40,32},{48,56},{56,48},{64,72... | collective-permute-start | bytes 208904 | tf_op jit(solution)/shard_map/ppermute | solution.py:502
  (1 other events, 0.7 us)

commit v4 on v3

--- a/solution.py
+++ b/solution.py
@@ -18,7 +18,7 @@
 WIDE = 384
 LANES = 128
 EXT = 2 * COLS
-BATH = EXT + 32
+BATH = EXT + 16
 MSG = BATH + 8
 VM = pltpu.VMEM
 
@@ -38,6 +38,11 @@
 
 def ddx(x):
     return roll(x, -1) - roll(x, 1)
+
+
+def ext_at(block, row):
+    half = pl.ds(pl.multiple_of((block % 2) * LANES, LANES), LANES)
+    return pl.ds(pl.multiple_of(row + (block // 2) * CH, CH), CH), half
 
 
 def lanes_of(shape):
@@ -154,7 +159,7 @@
     zero = jnp.zeros((CH, LANES), jnp.float32)
     exts = each(PER, chunk, 4)((zero, zero))
     for msg, ext in ((msg_n, exts[0]), (msg_s, exts[1])):
-        msg[pl.ds(pl.multiple_of(EXT + step * CH, CH), CH), :LANES] = ext
+        msg[ext_at(step, EXT)] = ext
 
 
 def split(x, pieces):
@@ -231,19 +236,19 @@
 
     @pl.when(step == pl.num_programs(0) - 1)
     def _():
-        seen[...] = observe(index, [(i, height[i]) for i in range(ROWS)])
-
-
-def observe(index, planes):
+        seen[...] = observe(index, [(i, height[i]) for i in range(ROWS)], 3)
+
+
+def observe(index, planes, count):
     slots = index.shape[1]
     sub = lax.broadcasted_iota(jnp.int32, (COLS, slots), 0)
     cell = jnp.broadcast_to(index[...], (COLS, slots))
-    hx = jnp.zeros((planes[0][1].shape[0], slots), jnp.float32)
+    left, right = [], []
     for i, plane in planes:
         pick = jnp.where(sub + i * COLS == cell, 1.0, 0.0).astype(jnp.bfloat16)
-        for p in split(plane, 3):
-            hx = hx + bdot(p, pick)
-    return hx
+        left += split(plane, count)
+        right += [pick] * count
+    return bdot(jnp.concatenate(left, axis=1), jnp.concatenate(right, axis=0))
 
 
 def beyond_rows(msgs, beyond):
@@ -291,7 +296,7 @@
         dst = pl.ds(pl.multiple_of(q * CH, CH), CH)
         for k, fy, msg in ((0, fy_n, msg_n), (1, fy_s, msg_s)):
             far = pl.ds(pl.multiple_of(COLS + q * CH, CH), CH)
-            ext = msg[pl.ds(pl.multiple_of(EXT + (q // PER) * CH, CH), CH), :LANES]
+            ext = msg[ext_at(q // PER, EXT)]
             new = edge_change(
                 k, has[k], q, q % PER, fy[dst, :], msg[dst, :], msg[far, :], ext,
                 flux_edge, height_edge, wide_bath, beyond,
@@ -302,7 +307,7 @@
 
     each(members // CH, chunk, 4)(0)
     rows = (0, 1, 2, ROWS - 1, ROWS - 2, ROWS - 3)
-    hx = seen[...] + observe(index, [(r, change[j]) for j, r in enumerate(rows)])
+    hx = seen[...] + observe(index, [(r, change[j]) for j, r in enumerate(rows)], 2)
     used = jnp.where(lanes_of((1, slots)) < count[0, 0], 1.0, 0.0)
     sigma = sd[...] * scale
     hmean = jnp.mean(hx, axis=0, keepdims=True)
@@ -336,13 +341,14 @@
     def chunk(q, carry):
         loc = pl.ds(pl.multiple_of(q * CH, CH), CH)
         rows = loc
+        full = first // CH + q
         there = pl.ds(pl.multiple_of(first + q * CH, CH), CH)
         for k, sg, e, fy, part, flux, ext in (
             (0, -1, 0, fy_n, part_n, flux_n, ext_n),
             (1, 1, ROWS - 1, fy_s, part_s, flux_s, ext_s),
         ):
             eps, du1, dv_e, dv_n, a, b, d = edge_change(
-                k, has[k], q, q, fy[loc, :], part[loc, :], flux[loc, :], ext[:, :LANES],
+                k, has[k], q, full % PER, fy[loc, :], part[loc, :], flux[loc, :], ext[ext_at((full // PER) % 2, 0)],
                 flux_edge, height_edge, wide_bath, beyond,
             )
             c = sg * 0.25
@@ -369,7 +375,8 @@
                 out[i, j, there, :] = fields[i, j, there, :] + x
         return carry
 
-    each(PER, chunk, 4)(0)
+    trips = fy_n.shape[0] // CH
+    each(trips, chunk, min(4, trips))(0)
 
 
 def elim(a, dst, base):
@@ -382,8 +389,8 @@
 
     def body(live, it, carry):
         A, X = list(carry[:live]), list(carry[live:])
-        cols = [[jnp.broadcast_to(A[g][:, k : k + 1], (8, n)) for k in range(8)] for g in range(live)]
-        C, P, Z = cols[0], A[0], X[0]
+        column = lambda g, k: jnp.broadcast_to(A[g][:, k : k + 1], (8, n))
+        C, P, Z = [column(0, k) for k in range(8)], A[0], X[0]
         rows = Z
         for k in range(8):
             pick = lambda x: jnp.broadcast_to(x[k : k + 1, :], (8, n))
@@ -398,16 +405,18 @@
             P = jnp.where(here, ra, P - C[k] * ra)
             Z = jnp.where(here, rx, Z - C[k] * rx)
         dst[pl.ds(pl.multiple_of(base + it * 8, 8), 8), :] = rows
-        for k in range(8):
-            rp, rz = (jnp.broadcast_to(x[k : k + 1, :], (8, n)) for x in (P, Z))
-            for g in range(1, live):
-                A[g] = A[g] - cols[g][k] * rp
-                X[g] = X[g] - cols[g][k] * rz
+        spread = lambda x: [jnp.broadcast_to(x[k : k + 1, :], (8, n)) for k in range(8)]
+        rp, rz = spread(P), spread(Z)
+        for g in range(1, live):
+            cols = [column(g, k) for k in range(8)]
+            for k in range(8):
+                A[g] = A[g] - cols[k] * rp[k]
+                X[g] = X[g] - cols[k] * rz[k]
         z = jnp.zeros((8, n), jnp.float32)
         A = [roll(A[g], -8) for g in range(1, live)] + [z]
         return tuple(A) + tuple(X[1:]) + (z,)
 
-    seg = 4
+    seg = 2
     for first in range(0, groups, seg):
         live = groups - first
         out = lax.fori_loop(first, first + seg, functools.partial(body, live), tuple(A) + tuple(X))
@@ -452,8 +461,16 @@
     mix[n:, n:] = x22 + (w2 + s2)
 
 
-def apply_kernel(mix, fields, late_n, late_s, out):
-    high, low = split(mix[...], 2)
+def apply_kernel(mix, fields, late_n, late_s, out, left):
+    members = mix.shape[0]
+
+    @pl.when((pl.program_id(0) == 0) & (pl.program_id(1) == 0))
+    def _():
+        high, low = split(mix[...], 2)
+        left[:, :members] = high
+        left[:, members : 2 * members] = high
+        left[:, 2 * members :] = low
+
     wind = jnp.where(pl.program_id(0) == 2, 0.25, 0.0)
     for i in range(ROWS):
         x = fields[0, i]
@@ -462,8 +479,7 @@
         if i == ROWS - 1:
             x = x - wind * late_s[...]
         a, b = split(x, 2)
-        res = bdot(high, a) + (bdot(high, b) + bdot(low, a))
-        out[0, pl.ds(i, x.shape[0], stride=ROWS), :] = res
+        out[0, pl.ds(i, members, stride=ROWS), :] = bdot(left[...], jnp.concatenate([a, b, a], axis=0))
 
 
 def whole(shape):
@@ -570,7 +586,6 @@
     one = lambda x: x.reshape(1, slots)
     obs = whole((1, slots))
     edge = whole((2, members, WIDE))
-    blocks = members // blk
     wb_spec, bey_spec = whole(wide_bath_shape), whole((4, CH, WIDE))
     fields_shape = VM((3, ROWS, members, COLS), jnp.float32)
     fields, flux_edge, height_edge, wind_edge, seen, late_n, late_s = pl.pallas_call(
@@ -613,16 +628,17 @@
         one(obs_index), obs_count, one(obs_value), one(obs_sd),
     )
 
-    for k in range(blocks):
+    pieces = [(64, 64), (32, 32), (16, 16), (128, 128), (0, 8), (8, 8)]
+    for lead, size in pieces:
         at = lambda rows, j: pl.BlockSpec((rows, COLS), lambda s: (j, 0))
-        msg_specs = [at(blk, k), at(blk, COLS // blk + k), at(CH, EXT // CH + k)]
-        edge_k = pl.BlockSpec((2, blk, WIDE), lambda s, k=k: (0, k, 0))
-        wind_k = pl.BlockSpec((2, blk, COLS), lambda s, k=k: (0, k, 0))
+        msg_specs = [at(size, lead // size), at(size, (COLS + lead) // size), at(CH, EXT // CH + lead // (2 * blk))]
+        edge_k = pl.BlockSpec((2, size, WIDE), lambda s, j=lead // size: (0, j, 0))
+        wind_k = pl.BlockSpec((2, size, COLS), lambda s, j=lead // size: (0, j, 0))
         here = pl.BlockSpec(memory_space=VM)
         fields = pl.pallas_call(
-            functools.partial(complete_kernel, ROWS, nlat, k * blk),
+            functools.partial(complete_kernel, ROWS, nlat, lead),
             grid=(1,),
-            in_specs=[wb_spec, bey_spec, smem, at(blk, k), at(blk, k)]
+            in_specs=[wb_spec, bey_spec, smem, at(size, lead // size), at(size, lead // size)]
             + msg_specs * 2
             + [edge_k, edge_k, wind_k, here],
             out_specs=here,
@@ -660,6 +676,7 @@
         ],
         out_specs=pl.BlockSpec((1, members * ROWS, LANES), lambda c, j: (c, 0, j)),
         out_shape=f32(3, members * ROWS, COLS),
+        scratch_shapes=[VM((members, 3 * members), jnp.bfloat16)],
         compiler_params=clip(24),
         name="mix",
     )(mix, fields, *late)

time: 179 us -> 178 us (level)
    pallas_call x4 -> x6, Pallas kernels: 11.2 us -> 12.4 us  [body(): pl.pallas_call(functools.partial(complete_kernel, ROWS, nlat, lead), grid...]
where the time goes in v4:
time: 178 us; the launch traced here: 177 us
  Pallas kernels  67.6 us (38%)
  starting transfers between devices  55.6 us (31%)
  waiting for transfers between devices  52 us (29%)
    ppermute x1, waiting for transfers between devices, body(): fy_n = lax.ppermute(to_south, 'lat', south)  24.6 us
    pallas_call x1, Pallas kernels, body(): pl.pallas_call(functools.partial(local_kernel, ROWS), grid=grid, in_specs...  17.3 us
    ppermute x10, starting transfers between devices, total(): parts = [lax.ppermute(y, axis, flips(n, b)) for b in hops]  17.1 us
    pallas_call x6, Pallas kernels, body(): pl.pallas_call(functools.partial(complete_kernel, ROWS, nlat, lead), grid...  12.4 us
    ppermute x10, waiting for transfers between devices, total(): parts = [lax.ppermute(y, axis, flips(n, b)) for b in hops]  11.8 us
    pallas_call x1, Pallas kernels, body(): pl.pallas_call(functools.partial(factor_kernel, members), out_shape=f32(m...  11.7 us
    pallas_call x1, Pallas kernels, body(): pl.pallas_call(apply_kernel, grid=(3, COLS // LANES), in_specs=[whole((me...  7.66 us
    ppermute x1, starting transfers between devices, body(): got_n = lax.ppermute(msg_s, 'lat', south)  6.4 us
  transfers between devices with their start and end apart: 20, of which 10 were waited for; matrix products, arithmetic and copies ran while one was open for 0% of the time, Pallas kernels for 25%

profile of v4, /device:TPU:8, one launch (start us, length us, event | category | flops | bytes accessed | tf_op | source)
XLA Modules:
  0.0 177.0 jit_solution(15320894082762697336)
XLA Ops:
  0.7 5.3 %edges.1 = (f32[256,128]{1,0:T(8,128)S(1)}, f32[256,128]{1,0:T(8,128)S(1)}) custom-call(f32[3,2048,256]{2,1,0:T(8,128)} %bitcast.9, f32[3,2048,256]{2,1,0:T(8,128)} %bitcast.10, f32[8,256]{1,0:T(8,128)S(1)} %copy-done), custom_call_target="tpu_custom_call" | custom-call | tf_op jit(solution)/shard_map/edges/pallas_call | solution.py:546
  6.0 6.3 %collective-permute-start = (f32[256,128]{1,0:T(8,128)S(1)}, f32[256,128]{1,0:T(8,128)S(1)}, u32[]{:S(2)}, u32[]{:S(2)}) collective-permute-start(f32[256,128]{1,0:T(8,128)S(1)} %get-tuple-element.26), channel_id=1, source_target_pairs={{8,0},{16,8},{24,16},{32,24},{40,32},{48,40},{56,48},{64,56},{72,6... | collective-permute-start | bytes 393224 | tf_op jit(solution)/shard_map/ppermute | solution.py:556
  12.3 2.5 %collective-permute-done.from_east = f32[256,128]{1,0:T(8,128)S(1)} collective-permute-done((f32[256,128]{1,0:T(8,128)S(1)}, f32[256,128]{1,0:T(8,128)S(1)}, u32[]{:S(2)}, u32[]{:S(2)}) %collective-permute-start) | collective-permute-done | bytes 131104 | tf_op jit(solution)/shard_map/ppermute | solution.py:556
  14.8 5.8 %collective-permute-done.1.from_west = f32[256,128]{1,0:T(8,128)S(1)} collective-permute-done((f32[256,128]{1,0:T(8,128)S(1)}, f32[256,128]{1,0:T(8,128)S(1)}, u32[]{:S(2)}, u32[]{:S(2)}) %collective-permute-start.1) | collective-permute-done | bytes 131104 | tf_op jit(solution)/shard_map/ppermute | solution.py:555
  20.6 6.1 %border.1 = (f32[536,256]{1,0:T(8,128)S(1)}, f32[536,256]{1,0:T(8,128)S(1)}, f32[8,8,384]{2,1,0:T(8,128)S(1)}) custom-call(f32[3,2048,256]{2,1,0:T(8,128)} %bitcast.11, f32[3,2048,256]{2,1,0:T(8,128)} %bitcast.12, f32[8,256]{1,0:T(8,128)S(1)} %copy-done, f32[256,128]{1,0:T(8,128)S(1)} %collective-permute-done.from_east, ...), custom_call_target="tpu_custom_call" | custom-call | tf_op jit(solution)/shard_map/border/pallas_call | solution.py:574
  26.7 6.4 %collective-permute-start.4 = (f32[536,256]{1,0:T(8,128)S(1)}, f32[536,256]{1,0:T(8,128)S(1)}, u32[]{:S(2)}, u32[]{:S(2)}) collective-permute-start(f32[536,256]{1,0:T(8,128)S(1)} %get-tuple-element.31), channel_id=1, source_target_pairs={{0,1},{1,2},{2,3},{3,4},{4,5},{5,6},{6,7},{8,9},{9,10},{10,11},{11... | collective-permute-start | bytes 1646600 | tf_op jit(solution)/shard_map/ppermute | solution.py:583
  33.1 4.2 %collective-permute-start.5 = (f32[536,256]{1,0:T(8,128)S(1)}, f32[536,256]{1,0:T(8,128)S(1)}, u32[]{:S(2)}, u32[]{:S(2)}) collective-permute-start(f32[536,256]{1,0:T(8,128)S(1)} %get-tuple-element.32), channel_id=1, source_target_pairs={{1,0},{2,1},{3,2},{4,3},{5,4},{6,5},{7,6},{9,8},{10,9},{11,10},{12... | collective-permute-start | bytes 1646600 | tf_op jit(solution)/shard_map/ppermute | solution.py:584
  37.4 2.4 %flux.1 = (f32[256,256]{1,0:T(8,128)S(1)}, f32[256,256]{1,0:T(8,128)S(1)}) custom-call(f32[3,2048,256]{2,1,0:T(8,128)} %bitcast.13, f32[3,2048,256]{2,1,0:T(8,128)} %bitcast.14, f32[8,256]{1,0:T(8,128)S(1)} %copy-done), custom_call_target="tpu_custom_call" | custom-call | tf_op jit(solution)/shard_map/flux/pallas_call | solution.py:562
  39.8 5.5 %collective-permute-start.2 = (f32[256,256]{1,0:T(8,128)S(1)}, f32[256,256]{1,0:T(8,128)S(1)}, u32[]{:S(2)}, u32[]{:S(2)}) collective-permute-start(f32[256,256]{1,0:T(8,128)S(1)} %get-tuple-element.29), channel_id=1, source_target_pairs={{0,1},{1,2},{2,3},{3,4},{4,5},{5,6},{6,7},{8,9},{9,10},{10,11},{11... | collective-permute-start | bytes 786440 | tf_op jit(solution)/shard_map/ppermute | solution.py:571
  45.3 5.1 %collective-permute-start.3 = (f32[256,256]{1,0:T(8,128)S(1)}, f32[256,256]{1,0:T(8,128)S(1)}, u32[]{:S(2)}, u32[]{:S(2)}) collective-permute-start(f32[256,256]{1,0:T(8,128)S(1)} %get-tuple-element.30), channel_id=1, source_target_pairs={{1,0},{2,1},{3,2},{4,3},{5,4},{6,5},{7,6},{9,8},{10,9},{11,10},{12... | collective-permute-start | bytes 786440 | tf_op jit(solution)/shard_map/ppermute | solution.py:572
  51.1 17.3 %local.1 = (f32[3,8,256,256]{3,2,1,0:T(8,128)S(1)}, f32[2,256,384]{2,1,0:T(8,128)S(1)}, f32[2,256,384]{2,1,0:T(8,128)S(1)}, f32[2,256,256]{2,1,0:T(8,128)S(1)}, ...) custom-call(f32[3,2048,256]{2,1,0:T(8,128)} %bitcast.15, f32[3,2048,256]{2,1,0:T(8,128)} %bitcast.16, ...), custom_call_target="tpu_custom_call" | custom-call | tf_op jit(solution)/shard_map/local/pallas_call | solution.py:591
  68.4 24.6 %collective-permute-done.2.fy_n = f32[256,256]{1,0:T(8,128)S(1)} collective-permute-done((f32[256,256]{1,0:T(8,128)S(1)}, f32[256,256]{1,0:T(8,128)S(1)}, u32[]{:S(2)}, u32[]{:S(2)}) %collective-permute-start.2) | collective-permute-done | bytes 262176 | tf_op jit(solution)/shard_map/ppermute | solution.py:571
  93.0 6.0 %collective-permute-done.3.fy_s = f32[256,256]{1,0:T(8,128)S(1)} collective-permute-done((f32[256,256]{1,0:T(8,128)S(1)}, f32[256,256]{1,0:T(8,128)S(1)}, u32[]{:S(2)}, u32[]{:S(2)}) %collective-permute-start.3) | collective-permute-done | bytes 262176 | tf_op jit(solution)/shard_map/ppermute | solution.py:572
  99.1 4.8 %sums.1 = (f32[136,128]{1,0:T(8,128)S(1)}, f32[136,128]{1,0:T(8,128)S(1)}, f32[4,8,384]{2,1,0:T(8,128)S(1)}) custom-call(f32[8,8,384]{2,1,0:T(8,128)S(1)} %get-tuple-element.28.wide_bath, f32[256,256]{1,0:T(8,128)S(1)} %collective-permute-done.2.fy_n, f32[256,256]{1,0:T(8,128)S(1)} %collective-permute-done.3.fy_s, ...), custom_call_target="tpu_custom_call" | custom-call | tf_op jit(solution)/shard_map/sums/pallas_call | solution.py:614
  105.1 4.3 %collective-permute-start.7 = (f32[136,128]{1,0:T(8,128)S(1)}, f32[136,128]{1,0:T(8,128)S(1)}, u32[]{:S(2)}, u32[]{:S(2)}) collective-permute-start(f32[136,128]{1,0:T(8,128)S(1)} %add.33), channel_id=1, source_target_pairs={{0,1},{1,0},{2,3},{3,2},{4,5},{5,4},{6,7},{7,6},{8,9},{9,8},{10,11... | collective-permute-start | bytes 208904 | tf_op jit(solution)/shard_map/ppermute | solution.py:515
  109.4 4.0 %collective-permute-done.7 = f32[136,128]{1,0:T(8,128)S(1)} collective-permute-done((f32[136,128]{1,0:T(8,128)S(1)}, f32[136,128]{1,0:T(8,128)S(1)}, u32[]{:S(2)}, u32[]{:S(2)}) %collective-permute-start.7) | collective-permute-done | bytes 69664 | tf_op jit(solution)/shard_map/ppermute | solution.py:515
  115.5 2.4 %collective-permute-start.8 = (f32[136,128]{1,0:T(8,128)S(1)}, f32[136,128]{1,0:T(8,128)S(1)}, u32[]{:S(2)}, u32[]{:S(2)}) collective-permute-start(f32[136,128]{1,0:T(8,128)S(1)} %add.34), channel_id=1, source_target_pairs={{0,16},{8,24},{16,0},{24,8},{32,48},{40,56},{48,32},{56,40},{64,80... | collective-permute-start | bytes 208904 | tf_op jit(solution)/shard_map/ppermute | solution.py:515
  121.5 2.6 %collective-permute-start.13 = (f32[136,128]{1,0:T(8,128)S(1)}, f32[136,128]{1,0:T(8,128)S(1)}, u32[]{:S(2)}, u32[]{:S(2)}) collective-permute-start(f32[136,128]{1,0:T(8,128)S(1)} %add_add_fusion.2), channel_id=1, source_target_pairs={{0,192},{8,200},{16,208},{24,216},{32,224},{40,232},{48,240},{56,2... | collective-permute-start | bytes 208904 | tf_op jit(solution)/shard_map/ppermute | solution.py:515
  134.1 6.0 %collective-permute-start.18 = (f32[256,256]{1,0:T(8,128)S(1)}, f32[256,256]{1,0:T(8,128)S(1)}, u32[]{:S(2)}, u32[]{:S(2)}) collective-permute-start(f32[256,256]{1,0:T(8,128)S(1)} %get-tuple-element.45), channel_id=1, source_target_pairs={{0,1},{1,2},{2,3},{3,4},{4,5},{5,6},{6,7},{8,9},{9,10},{10,11},{11... | collective-permute-start | bytes 786440 | tf_op jit(solution)/shard_map/ppermute | solution.py:511
  140.1 4.6 %collective-permute-start.19 = (f32[256,256]{1,0:T(8,128)S(1)}, f32[256,256]{1,0:T(8,128)S(1)}, u32[]{:S(2)}, u32[]{:S(2)}) collective-permute-start(f32[256,256]{1,0:T(8,128)S(1)} %get-tuple-element.46), channel_id=1, source_target_pairs={{1,0},{2,1},{3,2},{4,3},{5,4},{6,5},{7,6},{9,8},{10,9},{11,10},{12... | collective-permute-start | bytes 786440 | tf_op jit(solution)/shard_map/ppermute | solution.py:514
  145.1 2.8 %complete.6.fields = f32[3,8,256,256]{3,2,1,0:T(8,128)S(1)} custom-call(f32[8,8,384]{2,1,0:T(8,128)S(1)} %get-tuple-element.28.wide_bath, f32[4,8,384]{2,1,0:T(8,128)S(1)} %get-tuple-element.42.beyond, f32[64]{0:T(128)S(1)} %copy-done.1, f32[256,256]{1,0:T(8,128)S(1)} %collective-permute-done.2.fy_n, ...), custom_call_target="tpu_custom_call", output_to_operand_aliasing={{}: (14, {})} | custom-call | tf_op jit(solution)/shard_map/complete/pallas_call | solution.py:638
  150.6 5.1 %complete.9.fields = f32[3,8,256,256]{3,2,1,0:T(8,128)S(1)} custom-call(f32[8,8,384]{2,1,0:T(8,128)S(1)} %get-tuple-element.28.wide_bath, f32[4,8,384]{2,1,0:T(8,128)S(1)} %get-tuple-element.42.beyond, f32[64]{0:T(128)S(1)} %copy-done.1, f32[256,256]{1,0:T(8,128)S(1)} %collective-permute-done.2.fy_n, ...), custom_call_target="tpu_custom_call", output_to_operand_aliasing={{}: (14, {})} | custom-call | tf_op jit(solution)/shard_map/complete/pallas_call | solution.py:638
  157.6 11.7 %factor.1.mix = f32[256,256]{1,0:T(8,128)S(1)} custom-call(f32[136,128]{1,0:T(8,128)S(1)} %add_add_fusion.mine, f32[136,128]{1,0:T(8,128)S(1)} %collective-permute-done.17.other), custom_call_target="tpu_custom_call" | custom-call | tf_op jit(solution)/shard_map/factor/pallas_call | solution.py:657
  169.3 7.7 %mix.1 = f32[3,2048,256]{2,1,0:T(8,128)} custom-call(f32[256,256]{1,0:T(8,128)S(1)} %factor.1.mix, f32[3,8,256,256]{3,2,1,0:T(8,128)S(1)} %complete.11.fields, f32[256,256]{1,0:T(8,128)S(1)} %collective-permute-done.18.late_n, f32[256,256]{1,0:T(8,128)S(1)} %collective-permute-done.19.late_s), custom_call_target="tpu_custom_call" | custom-call | tf_op jit(solution)/shard_map/mix/pallas_call | solution.py:668
  (44 shorter events, 22.4 us)
Async XLA Ops:
  0.7 19.9 %copy-start.1 = (f32[64]{0:T(128)S(1)}, f32[64]{0:T(128)}, u32[]{:S(2)}) copy-start(f32[64]{0:T(128)} %constant.2.clone.fcor) | copy-start | bytes 772
  6.0 8.9 %collective-permute-start = (f32[256,128]{1,0:T(8,128)S(1)}, f32[256,128]{1,0:T(8,128)S(1)}, u32[]{:S(2)}, u32[]{:S(2)}) collective-permute-start(f32[256,128]{1,0:T(8,128)S(1)} %get-tuple-element.26), channel_id=1, source_target_pairs={{8,0},{16,8},{24,16},{32,24},{40,32},{48,40},{56,48},{64,56},{72,6... | collective-permute-start | bytes 393224 | tf_op jit(solution)/shard_map/ppermute | solution.py:556
  12.3 8.3 %collective-permute-start.1 = (f32[256,128]{1,0:T(8,128)S(1)}, f32[256,128]{1,0:T(8,128)S(1)}, u32[]{:S(2)}, u32[]{:S(2)}) collective-permute-start(f32[256,128]{1,0:T(8,128)S(1)} %get-tuple-element.27), channel_id=1, source_target_pairs={{0,8},{8,16},{16,24},{24,32},{32,40},{40,48},{48,56},{56,64},{64,7... | collective-permute-start | bytes 393224 | tf_op jit(solution)/shard_map/ppermute | solution.py:555
  26.7 72.3 %collective-permute-start.4 = (f32[536,256]{1,0:T(8,128)S(1)}, f32[536,256]{1,0:T(8,128)S(1)}, u32[]{:S(2)}, u32[]{:S(2)}) collective-permute-start(f32[536,256]{1,0:T(8,128)S(1)} %get-tuple-element.31), channel_id=1, source_target_pairs={{0,1},{1,2},{2,3},{3,4},{4,5},{5,6},{6,7},{8,9},{9,10},{10,11},{11... | collective-permute-start | bytes 1646600 | tf_op jit(solution)/shard_map/ppermute | solution.py:583
  33.1 17.9 %copy-start.2 = (s32[1,1,256]{2,1,0:T(1,128)S(1)}, s32[1,1,256]{2,1,0:T(1,128)}, u32[]{:S(2)}) copy-start(s32[1,1,256]{2,1,0:T(1,128)} %param.9) | copy-start | bytes 3076
  33.1 65.9 %collective-permute-start.5 = (f32[536,256]{1,0:T(8,128)S(1)}, f32[536,256]{1,0:T(8,128)S(1)}, u32[]{:S(2)}, u32[]{:S(2)}) collective-permute-start(f32[536,256]{1,0:T(8,128)S(1)} %get-tuple-element.32), channel_id=1, source_target_pairs={{1,0},{2,1},{3,2},{4,3},{5,4},{6,5},{7,6},{9,8},{10,9},{11,10},{12... | collective-permute-start | bytes 1646600 | tf_op jit(solution)/shard_map/ppermute | solution.py:584
  39.8 53.3 %collective-permute-start.2 = (f32[256,256]{1,0:T(8,128)S(1)}, f32[256,256]{1,0:T(8,128)S(1)}, u32[]{:S(2)}, u32[]{:S(2)}) collective-permute-start(f32[256,256]{1,0:T(8,128)S(1)} %get-tuple-element.29), channel_id=1, source_target_pairs={{0,1},{1,2},{2,3},{3,4},{4,5},{5,6},{6,7},{8,9},{9,10},{10,11},{11... | collective-permute-start | bytes 786440 | tf_op jit(solution)/shard_map/ppermute | solution.py:571
  45.3 53.8 %collective-permute-start.3 = (f32[256,256]{1,0:T(8,128)S(1)}, f32[256,256]{1,0:T(8,128)S(1)}, u32[]{:S(2)}, u32[]{:S(2)}) collective-permute-start(f32[256,256]{1,0:T(8,128)S(1)} %get-tuple-element.30), channel_id=1, source_target_pairs={{1,0},{2,1},{3,2},{4,3},{5,4},{6,5},{7,6},{9,8},{10,9},{11,10},{12... | collective-permute-start | bytes 786440 | tf_op jit(solution)/shard_map/ppermute | solution.py:572
  51.1 48.0 %copy-start.3 = (f32[1,1,256]{2,1,0:T(1,128)S(1)}, f32[1,1,256]{2,1,0:T(1,128)}, u32[]{:S(2)}) copy-start(f32[1,1,256]{2,1,0:T(1,128)} %param.11) | copy-start | bytes 3076
  51.1 48.0 %copy-start.4 = (f32[1,1,256]{2,1,0:T(1,128)S(1)}, f32[1,1,256]{2,1,0:T(1,128)}, u32[]{:S(2)}) copy-start(f32[1,1,256]{2,1,0:T(1,128)} %param.12) | copy-start | bytes 3076
  103.8 1.3 collective-permute-start.6
  105.1 8.3 %collective-permute-start.7 = (f32[136,128]{1,0:T(8,128)S(1)}, f32[136,128]{1,0:T(8,128)S(1)}, u32[]{:S(2)}, u32[]{:S(2)}) collective-permute-start(f32[136,128]{1,0:T(8,128)S(1)} %add.33), channel_id=1, source_target_pairs={{0,1},{1,0},{2,3},{3,2},{4,5},{5,4},{6,7},{7,6},{8,9},{9,8},{10,11... | collective-permute-start | bytes 208904 | tf_op jit(solution)/shard_map/ppermute | solution.py:515
  113.5 6.5 %collective-permute-start.10 = (f32[136,128]{1,0:T(8,128)S(1)}, f32[136,128]{1,0:T(8,128)S(1)}, u32[]{:S(2)}, u32[]{:S(2)}) collective-permute-start(f32[136,128]{1,0:T(8,128)S(1)} %add.34), channel_id=1, source_target_pairs={{0,48},{8,56},{16,32},{24,40},{32,16},{40,24},{48,0},{56,8},{64,11... | collective-permute-start | bytes 208904 | tf_op jit(solution)/shard_map/ppermute | solution.py:515
  115.5 5.9 %collective-permute-start.9 = (f32[136,128]{1,0:T(8,128)S(1)}, f32[136,128]{1,0:T(8,128)S(1)}, u32[]{:S(2)}, u32[]{:S(2)}) collective-permute-start(f32[136,128]{1,0:T(8,128)S(1)} %add.34), channel_id=1, source_target_pairs={{0,32},{8,40},{16,48},{24,56},{32,0},{40,8},{48,16},{56,24},{64,96... | collective-permute-start | bytes 208904 | tf_op jit(solution)/shard_map/ppermute | solution.py:515
  115.5 5.9 %collective-permute-start.8 = (f32[136,128]{1,0:T(8,128)S(1)}, f32[136,128]{1,0:T(8,128)S(1)}, u32[]{:S(2)}, u32[]{:S(2)}) collective-permute-start(f32[136,128]{1,0:T(8,128)S(1)} %add.34), channel_id=1, source_target_pairs={{0,16},{8,24},{16,0},{24,8},{32,48},{40,56},{48,32},{56,40},{64,80... | collective-permute-start | bytes 208904 | tf_op jit(solution)/shard_map/ppermute | solution.py:515
  121.5 6.4 %collective-permute-start.13 = (f32[136,128]{1,0:T(8,128)S(1)}, f32[136,128]{1,0:T(8,128)S(1)}, u32[]{:S(2)}, u32[]{:S(2)}) collective-permute-start(f32[136,128]{1,0:T(8,128)S(1)} %add_add_fusion.2), channel_id=1, source_target_pairs={{0,192},{8,200},{16,208},{24,216},{32,224},{40,232},{48,240},{56,2... | collective-permute-start | bytes 208904 | tf_op jit(solution)/shard_map/ppermute | solution.py:515
  124.1 5.8 %collective-permute-start.12 = (f32[136,128]{1,0:T(8,128)S(1)}, f32[136,128]{1,0:T(8,128)S(1)}, u32[]{:S(2)}, u32[]{:S(2)}) collective-permute-start(f32[136,128]{1,0:T(8,128)S(1)} %add_add_fusion.2), channel_id=1, source_target_pairs={{0,128},{8,136},{16,144},{24,152},{32,160},{40,168},{48,176},{56,1... | collective-permute-start | bytes 208904 | tf_op jit(solution)/shard_map/ppermute | solution.py:515
  124.9 5.0 %collective-permute-start.11 = (f32[136,128]{1,0:T(8,128)S(1)}, f32[136,128]{1,0:T(8,128)S(1)}, u32[]{:S(2)}, u32[]{:S(2)}) collective-permute-start(f32[136,128]{1,0:T(8,128)S(1)} %add_add_fusion.2), channel_id=1, source_target_pairs={{0,64},{8,72},{16,80},{24,88},{32,96},{40,104},{48,112},{56,120},{... | collective-permute-start | bytes 208904 | tf_op jit(solution)/shard_map/ppermute | solution.py:515
  129.9 14.8 %collective-permute-start.16 = (f32[136,128]{1,0:T(8,128)S(1)}, f32[136,128]{1,0:T(8,128)S(1)}, u32[]{:S(2)}, u32[]{:S(2)}) collective-permute-start(f32[136,128]{1,0:T(8,128)S(1)} %add_add_fusion.1), channel_id=1, source_target_pairs={{0,6},{1,7},{2,4},{3,5},{4,2},{5,3},{6,0},{7,1},{8,14},{9,15},{10,... | collective-permute-start | bytes 208904 | tf_op jit(solution)/shard_map/ppermute | solution.py:515
  131.1 13.7 %collective-permute-start.15 = (f32[136,128]{1,0:T(8,128)S(1)}, f32[136,128]{1,0:T(8,128)S(1)}, u32[]{:S(2)}, u32[]{:S(2)}) collective-permute-start(f32[136,128]{1,0:T(8,128)S(1)} %add_add_fusion.1), channel_id=1, source_target_pairs={{0,4},{1,5},{2,6},{3,7},{4,0},{5,1},{6,2},{7,3},{8,12},{9,13},{10,... | collective-permute-start | bytes 208904 | tf_op jit(solution)/shard_map/ppermute | solution.py:515
  131.9 12.9 %collective-permute-start.14 = (f32[136,128]{1,0:T(8,128)S(1)}, f32[136,128]{1,0:T(8,128)S(1)}, u32[]{:S(2)}, u32[]{:S(2)}) collective-permute-start(f32[136,128]{1,0:T(8,128)S(1)} %add_add_fusion.1), channel_id=1, source_target_pairs={{0,2},{1,3},{2,0},{3,1},{4,6},{5,7},{6,4},{7,5},{8,10},{9,11},{10,... | collective-permute-start | bytes 208904 | tf_op jit(solution)/shard_map/ppermute | solution.py:515
  134.1 35.2 %collective-permute-start.18 = (f32[256,256]{1,0:T(8,128)S(1)}, f32[256,256]{1,0:T(8,128)S(1)}, u32[]{:S(2)}, u32[]{:S(2)}) collective-permute-start(f32[256,256]{1,0:T(8,128)S(1)} %get-tuple-element.45), channel_id=1, source_target_pairs={{0,1},{1,2},{2,3},{3,4},{4,5},{5,6},{6,7},{8,9},{9,10},{10,11},{11... | collective-permute-start | bytes 786440 | tf_op jit(solution)/shard_map/ppermute | solution.py:511
  140.1 29.2 %collective-permute-start.19 = (f32[256,256]{1,0:T(8,128)S(1)}, f32[256,256]{1,0:T(8,128)S(1)}, u32[]{:S(2)}, u32[]{:S(2)}) collective-permute-start(f32[256,256]{1,0:T(8,128)S(1)} %get-tuple-element.46), channel_id=1, source_target_pairs={{1,0},{2,1},{3,2},{4,3},{5,4},{6,5},{7,6},{9,8},{10,9},{11,10},{12... | collective-permute-start | bytes 786440 | tf_op jit(solution)/shard_map/ppermute | solution.py:514
  144.8 12.7 %collective-permute-start.17 = (f32[136,128]{1,0:T(8,128)S(1)}, f32[136,128]{1,0:T(8,128)S(1)}, u32[]{:S(2)}, u32[]{:S(2)}) collective-permute-start(f32[136,128]{1,0:T(8,128)S(1)} %add_add_fusion.mine), channel_id=1, source_target_pairs={{0,8},{8,0},{16,24},{24,16},{32,40},{40,32},{48,56},{56,48},{64,72... | collective-permute-start | bytes 208904 | tf_op jit(solution)/shard_map/ppermute | solution.py:518
  (1 other events, 0.7 us)

commit v5 on v4

--- a/solution.py
+++ b/solution.py
@@ -472,8 +472,9 @@
         left[:, 2 * members :] = low
 
     wind = jnp.where(pl.program_id(0) == 2, 0.25, 0.0)
+    lanes = pl.ds(pl.multiple_of(pl.program_id(1) * LANES, LANES), LANES)
     for i in range(ROWS):
-        x = fields[0, i]
+        x = fields[pl.program_id(0), i, :, lanes]
         if i == 0:
             x = x + wind * late_n[...]
         if i == ROWS - 1:
@@ -670,7 +671,7 @@
         grid=(3, COLS // LANES),
         in_specs=[
             whole((members, members)),
-            pl.BlockSpec((1, ROWS, members, LANES), lambda c, j: (c, 0, 0, j)),
+            pl.BlockSpec(memory_space=VM),
             half,
             half,
         ],

time: 178 us -> 178 us (level)
  no operation moved by 1% of the time
where the time goes in v5:
time: 178 us; the launch traced here: 177 us
  Pallas kernels  67.3 us (38%)
  starting transfers between devices  55.6 us (31%)
  waiting for transfers between devices  52 us (29%)
    ppermute x1, waiting for transfers between devices, body(): fy_n = lax.ppermute(to_south, 'lat', south)  24.6 us
    pallas_call x1, Pallas kernels, body(): pl.pallas_call(functools.partial(local_kernel, ROWS), grid=grid, in_specs...  17.3 us
    ppermute x10, starting transfers between devices, total(): parts = [lax.ppermute(y, axis, flips(n, b)) for b in hops]  17.1 us
    pallas_call x6, Pallas kernels, body(): pl.pallas_call(functools.partial(complete_kernel, ROWS, nlat, lead), grid...  12.4 us
    ppermute x10, waiting for transfers between devices, total(): parts = [lax.ppermute(y, axis, flips(n, b)) for b in hops]  11.8 us
    pallas_call x1, Pallas kernels, body(): pl.pallas_call(functools.partial(factor_kernel, members), out_shape=f32(m...  11.7 us
    pallas_call x1, Pallas kernels, body(): pl.pallas_call(apply_kernel, grid=(3, COLS // LANES), in_specs=[whole((me...  7.38 us
    ppermute x1, starting transfers between devices, body(): got_n = lax.ppermute(msg_s, 'lat', south)  6.4 us
  transfers between devices with their start and end apart: 20, of which 10 were waited for; matrix products, arithmetic and copies ran while one was open for 0% of the time, Pallas kernels for 25%

profile of v5, /device:TPU:8, one launch (start us, length us, event | category | flops | bytes accessed | tf_op | source)
XLA Modules:
  0.0 176.7 jit_solution(17725118256265383221)
XLA Ops:
  0.7 5.3 %edges.1 = (f32[256,128]{1,0:T(8,128)S(1)}, f32[256,128]{1,0:T(8,128)S(1)}) custom-call(f32[3,2048,256]{2,1,0:T(8,128)} %bitcast.9, f32[3,2048,256]{2,1,0:T(8,128)} %bitcast.10, f32[8,256]{1,0:T(8,128)S(1)} %copy-done), custom_call_target="tpu_custom_call" | custom-call | tf_op jit(solution)/shard_map/edges/pallas_call | solution.py:547
  6.0 6.3 %collective-permute-start = (f32[256,128]{1,0:T(8,128)S(1)}, f32[256,128]{1,0:T(8,128)S(1)}, u32[]{:S(2)}, u32[]{:S(2)}) collective-permute-start(f32[256,128]{1,0:T(8,128)S(1)} %get-tuple-element.26), channel_id=1, source_target_pairs={{8,0},{16,8},{24,16},{32,24},{40,32},{48,40},{56,48},{64,56},{72,6... | collective-permute-start | bytes 393224 | tf_op jit(solution)/shard_map/ppermute | solution.py:557
  12.3 2.5 %collective-permute-done.from_east = f32[256,128]{1,0:T(8,128)S(1)} collective-permute-done((f32[256,128]{1,0:T(8,128)S(1)}, f32[256,128]{1,0:T(8,128)S(1)}, u32[]{:S(2)}, u32[]{:S(2)}) %collective-permute-start) | collective-permute-done | bytes 131104 | tf_op jit(solution)/shard_map/ppermute | solution.py:557
  14.8 5.8 %collective-permute-done.1.from_west = f32[256,128]{1,0:T(8,128)S(1)} collective-permute-done((f32[256,128]{1,0:T(8,128)S(1)}, f32[256,128]{1,0:T(8,128)S(1)}, u32[]{:S(2)}, u32[]{:S(2)}) %collective-permute-start.1) | collective-permute-done | bytes 131104 | tf_op jit(solution)/shard_map/ppermute | solution.py:556
  20.6 6.1 %border.1 = (f32[536,256]{1,0:T(8,128)S(1)}, f32[536,256]{1,0:T(8,128)S(1)}, f32[8,8,384]{2,1,0:T(8,128)S(1)}) custom-call(f32[3,2048,256]{2,1,0:T(8,128)} %bitcast.11, f32[3,2048,256]{2,1,0:T(8,128)} %bitcast.12, f32[8,256]{1,0:T(8,128)S(1)} %copy-done, f32[256,128]{1,0:T(8,128)S(1)} %collective-permute-done.from_east, ...), custom_call_target="tpu_custom_call" | custom-call | tf_op jit(solution)/shard_map/border/pallas_call | solution.py:575
  26.7 6.4 %collective-permute-start.4 = (f32[536,256]{1,0:T(8,128)S(1)}, f32[536,256]{1,0:T(8,128)S(1)}, u32[]{:S(2)}, u32[]{:S(2)}) collective-permute-start(f32[536,256]{1,0:T(8,128)S(1)} %get-tuple-element.31), channel_id=1, source_target_pairs={{0,1},{1,2},{2,3},{3,4},{4,5},{5,6},{6,7},{8,9},{9,10},{10,11},{11... | collective-permute-start | bytes 1646600 | tf_op jit(solution)/shard_map/ppermute | solution.py:584
  33.1 4.2 %collective-permute-start.5 = (f32[536,256]{1,0:T(8,128)S(1)}, f32[536,256]{1,0:T(8,128)S(1)}, u32[]{:S(2)}, u32[]{:S(2)}) collective-permute-start(f32[536,256]{1,0:T(8,128)S(1)} %get-tuple-element.32), channel_id=1, source_target_pairs={{1,0},{2,1},{3,2},{4,3},{5,4},{6,5},{7,6},{9,8},{10,9},{11,10},{12... | collective-permute-start | bytes 1646600 | tf_op jit(solution)/shard_map/ppermute | solution.py:585
  37.4 2.4 %flux.1 = (f32[256,256]{1,0:T(8,128)S(1)}, f32[256,256]{1,0:T(8,128)S(1)}) custom-call(f32[3,2048,256]{2,1,0:T(8,128)} %bitcast.13, f32[3,2048,256]{2,1,0:T(8,128)} %bitcast.14, f32[8,256]{1,0:T(8,128)S(1)} %copy-done), custom_call_target="tpu_custom_call" | custom-call | tf_op jit(solution)/shard_map/flux/pallas_call | solution.py:563
  39.8 5.5 %collective-permute-start.2 = (f32[256,256]{1,0:T(8,128)S(1)}, f32[256,256]{1,0:T(8,128)S(1)}, u32[]{:S(2)}, u32[]{:S(2)}) collective-permute-start(f32[256,256]{1,0:T(8,128)S(1)} %get-tuple-element.29), channel_id=1, source_target_pairs={{0,1},{1,2},{2,3},{3,4},{4,5},{5,6},{6,7},{8,9},{9,10},{10,11},{11... | collective-permute-start | bytes 786440 | tf_op jit(solution)/shard_map/ppermute | solution.py:572
  45.3 5.1 %collective-permute-start.3 = (f32[256,256]{1,0:T(8,128)S(1)}, f32[256,256]{1,0:T(8,128)S(1)}, u32[]{:S(2)}, u32[]{:S(2)}) collective-permute-start(f32[256,256]{1,0:T(8,128)S(1)} %get-tuple-element.30), channel_id=1, source_target_pairs={{1,0},{2,1},{3,2},{4,3},{5,4},{6,5},{7,6},{9,8},{10,9},{11,10},{12... | collective-permute-start | bytes 786440 | tf_op jit(solution)/shard_map/ppermute | solution.py:573
  51.1 17.3 %local.1 = (f32[3,8,256,256]{3,2,1,0:T(8,128)S(1)}, f32[2,256,384]{2,1,0:T(8,128)S(1)}, f32[2,256,384]{2,1,0:T(8,128)S(1)}, f32[2,256,256]{2,1,0:T(8,128)S(1)}, ...) custom-call(f32[3,2048,256]{2,1,0:T(8,128)} %bitcast.15, f32[3,2048,256]{2,1,0:T(8,128)} %bitcast.16, ...), custom_call_target="tpu_custom_call" | custom-call | tf_op jit(solution)/shard_map/local/pallas_call | solution.py:592
  68.4 24.6 %collective-permute-done.2.fy_n = f32[256,256]{1,0:T(8,128)S(1)} collective-permute-done((f32[256,256]{1,0:T(8,128)S(1)}, f32[256,256]{1,0:T(8,128)S(1)}, u32[]{:S(2)}, u32[]{:S(2)}) %collective-permute-start.2) | collective-permute-done | bytes 262176 | tf_op jit(solution)/shard_map/ppermute | solution.py:572
  93.0 6.0 %collective-permute-done.3.fy_s = f32[256,256]{1,0:T(8,128)S(1)} collective-permute-done((f32[256,256]{1,0:T(8,128)S(1)}, f32[256,256]{1,0:T(8,128)S(1)}, u32[]{:S(2)}, u32[]{:S(2)}) %collective-permute-start.3) | collective-permute-done | bytes 262176 | tf_op jit(solution)/shard_map/ppermute | solution.py:573
  99.1 4.8 %sums.1 = (f32[136,128]{1,0:T(8,128)S(1)}, f32[136,128]{1,0:T(8,128)S(1)}, f32[4,8,384]{2,1,0:T(8,128)S(1)}) custom-call(f32[8,8,384]{2,1,0:T(8,128)S(1)} %get-tuple-element.28.wide_bath, f32[256,256]{1,0:T(8,128)S(1)} %collective-permute-done.2.fy_n, f32[256,256]{1,0:T(8,128)S(1)} %collective-permute-done.3.fy_s, ...), custom_call_target="tpu_custom_call" | custom-call | tf_op jit(solution)/shard_map/sums/pallas_call | solution.py:615
  105.1 4.3 %collective-permute-start.7 = (f32[136,128]{1,0:T(8,128)S(1)}, f32[136,128]{1,0:T(8,128)S(1)}, u32[]{:S(2)}, u32[]{:S(2)}) collective-permute-start(f32[136,128]{1,0:T(8,128)S(1)} %add.33), channel_id=1, source_target_pairs={{0,1},{1,0},{2,3},{3,2},{4,5},{5,4},{6,7},{7,6},{8,9},{9,8},{10,11... | collective-permute-start | bytes 208904 | tf_op jit(solution)/shard_map/ppermute | solution.py:516
  109.4 4.0 %collective-permute-done.7 = f32[136,128]{1,0:T(8,128)S(1)} collective-permute-done((f32[136,128]{1,0:T(8,128)S(1)}, f32[136,128]{1,0:T(8,128)S(1)}, u32[]{:S(2)}, u32[]{:S(2)}) %collective-permute-start.7) | collective-permute-done | bytes 69664 | tf_op jit(solution)/shard_map/ppermute | solution.py:516
  115.5 2.4 %collective-permute-start.8 = (f32[136,128]{1,0:T(8,128)S(1)}, f32[136,128]{1,0:T(8,128)S(1)}, u32[]{:S(2)}, u32[]{:S(2)}) collective-permute-start(f32[136,128]{1,0:T(8,128)S(1)} %add.34), channel_id=1, source_target_pairs={{0,16},{8,24},{16,0},{24,8},{32,48},{40,56},{48,32},{56,40},{64,80... | collective-permute-start | bytes 208904 | tf_op jit(solution)/shard_map/ppermute | solution.py:516
  121.5 2.6 %collective-permute-start.13 = (f32[136,128]{1,0:T(8,128)S(1)}, f32[136,128]{1,0:T(8,128)S(1)}, u32[]{:S(2)}, u32[]{:S(2)}) collective-permute-start(f32[136,128]{1,0:T(8,128)S(1)} %add_add_fusion.2), channel_id=1, source_target_pairs={{0,192},{8,200},{16,208},{24,216},{32,224},{40,232},{48,240},{56,2... | collective-permute-start | bytes 208904 | tf_op jit(solution)/shard_map/ppermute | solution.py:516
  134.1 6.0 %collective-permute-start.18 = (f32[256,256]{1,0:T(8,128)S(1)}, f32[256,256]{1,0:T(8,128)S(1)}, u32[]{:S(2)}, u32[]{:S(2)}) collective-permute-start(f32[256,256]{1,0:T(8,128)S(1)} %get-tuple-element.45), channel_id=1, source_target_pairs={{0,1},{1,2},{2,3},{3,4},{4,5},{5,6},{6,7},{8,9},{9,10},{10,11},{11... | collective-permute-start | bytes 786440 | tf_op jit(solution)/shard_map/ppermute | solution.py:512
  140.1 4.6 %collective-permute-start.19 = (f32[256,256]{1,0:T(8,128)S(1)}, f32[256,256]{1,0:T(8,128)S(1)}, u32[]{:S(2)}, u32[]{:S(2)}) collective-permute-start(f32[256,256]{1,0:T(8,128)S(1)} %get-tuple-element.46), channel_id=1, source_target_pairs={{1,0},{2,1},{3,2},{4,3},{5,4},{6,5},{7,6},{9,8},{10,9},{11,10},{12... | collective-permute-start | bytes 786440 | tf_op jit(solution)/shard_map/ppermute | solution.py:515
  145.1 2.8 %complete.6.fields = f32[3,8,256,256]{3,2,1,0:T(8,128)S(1)} custom-call(f32[8,8,384]{2,1,0:T(8,128)S(1)} %get-tuple-element.28.wide_bath, f32[4,8,384]{2,1,0:T(8,128)S(1)} %get-tuple-element.42.beyond, f32[64]{0:T(128)S(1)} %copy-done.1, f32[256,256]{1,0:T(8,128)S(1)} %collective-permute-done.2.fy_n, ...), custom_call_target="tpu_custom_call", output_to_operand_aliasing={{}: (14, {})} | custom-call | tf_op jit(solution)/shard_map/complete/pallas_call | solution.py:639
  150.6 5.1 %complete.9.fields = f32[3,8,256,256]{3,2,1,0:T(8,128)S(1)} custom-call(f32[8,8,384]{2,1,0:T(8,128)S(1)} %get-tuple-element.28.wide_bath, f32[4,8,384]{2,1,0:T(8,128)S(1)} %get-tuple-element.42.beyond, f32[64]{0:T(128)S(1)} %copy-done.1, f32[256,256]{1,0:T(8,128)S(1)} %collective-permute-done.2.fy_n, ...), custom_call_target="tpu_custom_call", output_to_operand_aliasing={{}: (14, {})} | custom-call | tf_op jit(solution)/shard_map/complete/pallas_call | solution.py:639
  157.6 11.7 %factor.1.mix = f32[256,256]{1,0:T(8,128)S(1)} custom-call(f32[136,128]{1,0:T(8,128)S(1)} %add_add_fusion.mine, f32[136,128]{1,0:T(8,128)S(1)} %collective-permute-done.17.other), custom_call_target="tpu_custom_call" | custom-call | tf_op jit(solution)/shard_map/factor/pallas_call | solution.py:658
  169.3 7.4 %mix.1 = f32[3,2048,256]{2,1,0:T(8,128)} custom-call(f32[256,256]{1,0:T(8,128)S(1)} %factor.1.mix, f32[3,8,256,256]{3,2,1,0:T(8,128)S(1)} %complete.11.fields, f32[256,256]{1,0:T(8,128)S(1)} %collective-permute-done.18.late_n, f32[256,256]{1,0:T(8,128)S(1)} %collective-permute-done.19.late_s), custom_call_target="tpu_custom_call" | custom-call | tf_op jit(solution)/shard_map/mix/pallas_call | solution.py:669
  (44 shorter events, 22.4 us)
Async XLA Ops:
  0.7 19.9 %copy-start.1 = (f32[64]{0:T(128)S(1)}, f32[64]{0:T(128)}, u32[]{:S(2)}) copy-start(f32[64]{0:T(128)} %constant.2.clone.fcor) | copy-start | bytes 772
  6.0 8.9 %collective-permute-start = (f32[256,128]{1,0:T(8,128)S(1)}, f32[256,128]{1,0:T(8,128)S(1)}, u32[]{:S(2)}, u32[]{:S(2)}) collective-permute-start(f32[256,128]{1,0:T(8,128)S(1)} %get-tuple-element.26), channel_id=1, source_target_pairs={{8,0},{16,8},{24,16},{32,24},{40,32},{48,40},{56,48},{64,56},{72,6... | collective-permute-start | bytes 393224 | tf_op jit(solution)/shard_map/ppermute | solution.py:557
  12.3 8.3 %collective-permute-start.1 = (f32[256,128]{1,0:T(8,128)S(1)}, f32[256,128]{1,0:T(8,128)S(1)}, u32[]{:S(2)}, u32[]{:S(2)}) collective-permute-start(f32[256,128]{1,0:T(8,128)S(1)} %get-tuple-element.27), channel_id=1, source_target_pairs={{0,8},{8,16},{16,24},{24,32},{32,40},{40,48},{48,56},{56,64},{64,7... | collective-permute-start | bytes 393224 | tf_op jit(solution)/shard_map/ppermute | solution.py:556
  26.7 72.3 %collective-permute-start.4 = (f32[536,256]{1,0:T(8,128)S(1)}, f32[536,256]{1,0:T(8,128)S(1)}, u32[]{:S(2)}, u32[]{:S(2)}) collective-permute-start(f32[536,256]{1,0:T(8,128)S(1)} %get-tuple-element.31), channel_id=1, source_target_pairs={{0,1},{1,2},{2,3},{3,4},{4,5},{5,6},{6,7},{8,9},{9,10},{10,11},{11... | collective-permute-start | bytes 1646600 | tf_op jit(solution)/shard_map/ppermute | solution.py:584
  33.1 17.9 %copy-start.2 = (s32[1,1,256]{2,1,0:T(1,128)S(1)}, s32[1,1,256]{2,1,0:T(1,128)}, u32[]{:S(2)}) copy-start(s32[1,1,256]{2,1,0:T(1,128)} %param.9) | copy-start | bytes 3076
  33.1 65.9 %collective-permute-start.5 = (f32[536,256]{1,0:T(8,128)S(1)}, f32[536,256]{1,0:T(8,128)S(1)}, u32[]{:S(2)}, u32[]{:S(2)}) collective-permute-start(f32[536,256]{1,0:T(8,128)S(1)} %get-tuple-element.32), channel_id=1, source_target_pairs={{1,0},{2,1},{3,2},{4,3},{5,4},{6,5},{7,6},{9,8},{10,9},{11,10},{12... | collective-permute-start | bytes 1646600 | tf_op jit(solution)/shard_map/ppermute | solution.py:585
  39.8 53.3 %collective-permute-start.2 = (f32[256,256]{1,0:T(8,128)S(1)}, f32[256,256]{1,0:T(8,128)S(1)}, u32[]{:S(2)}, u32[]{:S(2)}) collective-permute-start(f32[256,256]{1,0:T(8,128)S(1)} %get-tuple-element.29), channel_id=1, source_target_pairs={{0,1},{1,2},{2,3},{3,4},{4,5},{5,6},{6,7},{8,9},{9,10},{10,11},{11... | collective-permute-start | bytes 786440 | tf_op jit(solution)/shard_map/ppermute | solution.py:572
  45.3 53.8 %collective-permute-start.3 = (f32[256,256]{1,0:T(8,128)S(1)}, f32[256,256]{1,0:T(8,128)S(1)}, u32[]{:S(2)}, u32[]{:S(2)}) collective-permute-start(f32[256,256]{1,0:T(8,128)S(1)} %get-tuple-element.30), channel_id=1, source_target_pairs={{1,0},{2,1},{3,2},{4,3},{5,4},{6,5},{7,6},{9,8},{10,9},{11,10},{12... | collective-permute-start | bytes 786440 | tf_op jit(solution)/shard_map/ppermute | solution.py:573
  51.1 48.0 %copy-start.3 = (f32[1,1,256]{2,1,0:T(1,128)S(1)}, f32[1,1,256]{2,1,0:T(1,128)}, u32[]{:S(2)}) copy-start(f32[1,1,256]{2,1,0:T(1,128)} %param.11) | copy-start | bytes 3076
  51.1 48.0 %copy-start.4 = (f32[1,1,256]{2,1,0:T(1,128)S(1)}, f32[1,1,256]{2,1,0:T(1,128)}, u32[]{:S(2)}) copy-start(f32[1,1,256]{2,1,0:T(1,128)} %param.12) | copy-start | bytes 3076
  103.8 1.3 collective-permute-start.6
  105.1 8.3 %collective-permute-start.7 = (f32[136,128]{1,0:T(8,128)S(1)}, f32[136,128]{1,0:T(8,128)S(1)}, u32[]{:S(2)}, u32[]{:S(2)}) collective-permute-start(f32[136,128]{1,0:T(8,128)S(1)} %add.33), channel_id=1, source_target_pairs={{0,1},{1,0},{2,3},{3,2},{4,5},{5,4},{6,7},{7,6},{8,9},{9,8},{10,11... | collective-permute-start | bytes 208904 | tf_op jit(solution)/shard_map/ppermute | solution.py:516
  113.5 6.5 %collective-permute-start.10 = (f32[136,128]{1,0:T(8,128)S(1)}, f32[136,128]{1,0:T(8,128)S(1)}, u32[]{:S(2)}, u32[]{:S(2)}) collective-permute-start(f32[136,128]{1,0:T(8,128)S(1)} %add.34), channel_id=1, source_target_pairs={{0,48},{8,56},{16,32},{24,40},{32,16},{40,24},{48,0},{56,8},{64,11... | collective-permute-start | bytes 208904 | tf_op jit(solution)/shard_map/ppermute | solution.py:516
  115.5 5.9 %collective-permute-start.9 = (f32[136,128]{1,0:T(8,128)S(1)}, f32[136,128]{1,0:T(8,128)S(1)}, u32[]{:S(2)}, u32[]{:S(2)}) collective-permute-start(f32[136,128]{1,0:T(8,128)S(1)} %add.34), channel_id=1, source_target_pairs={{0,32},{8,40},{16,48},{24,56},{32,0},{40,8},{48,16},{56,24},{64,96... | collective-permute-start | bytes 208904 | tf_op jit(solution)/shard_map/ppermute | solution.py:516
  115.5 5.9 %collective-permute-start.8 = (f32[136,128]{1,0:T(8,128)S(1)}, f32[136,128]{1,0:T(8,128)S(1)}, u32[]{:S(2)}, u32[]{:S(2)}) collective-permute-start(f32[136,128]{1,0:T(8,128)S(1)} %add.34), channel_id=1, source_target_pairs={{0,16},{8,24},{16,0},{24,8},{32,48},{40,56},{48,32},{56,40},{64,80... | collective-permute-start | bytes 208904 | tf_op jit(solution)/shard_map/ppermute | solution.py:516
  121.5 6.4 %collective-permute-start.13 = (f32[136,128]{1,0:T(8,128)S(1)}, f32[136,128]{1,0:T(8,128)S(1)}, u32[]{:S(2)}, u32[]{:S(2)}) collective-permute-start(f32[136,128]{1,0:T(8,128)S(1)} %add_add_fusion.2), channel_id=1, source_target_pairs={{0,192},{8,200},{16,208},{24,216},{32,224},{40,232},{48,240},{56,2... | collective-permute-start | bytes 208904 | tf_op jit(solution)/shard_map/ppermute | solution.py:516
  124.1 5.8 %collective-permute-start.12 = (f32[136,128]{1,0:T(8,128)S(1)}, f32[136,128]{1,0:T(8,128)S(1)}, u32[]{:S(2)}, u32[]{:S(2)}) collective-permute-start(f32[136,128]{1,0:T(8,128)S(1)} %add_add_fusion.2), channel_id=1, source_target_pairs={{0,128},{8,136},{16,144},{24,152},{32,160},{40,168},{48,176},{56,1... | collective-permute-start | bytes 208904 | tf_op jit(solution)/shard_map/ppermute | solution.py:516
  124.9 5.0 %collective-permute-start.11 = (f32[136,128]{1,0:T(8,128)S(1)}, f32[136,128]{1,0:T(8,128)S(1)}, u32[]{:S(2)}, u32[]{:S(2)}) collective-permute-start(f32[136,128]{1,0:T(8,128)S(1)} %add_add_fusion.2), channel_id=1, source_target_pairs={{0,64},{8,72},{16,80},{24,88},{32,96},{40,104},{48,112},{56,120},{... | collective-permute-start | bytes 208904 | tf_op jit(solution)/shard_map/ppermute | solution.py:516
  129.9 14.8 %collective-permute-start.16 = (f32[136,128]{1,0:T(8,128)S(1)}, f32[136,128]{1,0:T(8,128)S(1)}, u32[]{:S(2)}, u32[]{:S(2)}) collective-permute-start(f32[136,128]{1,0:T(8,128)S(1)} %add_add_fusion.1), channel_id=1, source_target_pairs={{0,6},{1,7},{2,4},{3,5},{4,2},{5,3},{6,0},{7,1},{8,14},{9,15},{10,... | collective-permute-start | bytes 208904 | tf_op jit(solution)/shard_map/ppermute | solution.py:516
  131.1 13.7 %collective-permute-start.15 = (f32[136,128]{1,0:T(8,128)S(1)}, f32[136,128]{1,0:T(8,128)S(1)}, u32[]{:S(2)}, u32[]{:S(2)}) collective-permute-start(f32[136,128]{1,0:T(8,128)S(1)} %add_add_fusion.1), channel_id=1, source_target_pairs={{0,4},{1,5},{2,6},{3,7},{4,0},{5,1},{6,2},{7,3},{8,12},{9,13},{10,... | collective-permute-start | bytes 208904 | tf_op jit(solution)/shard_map/ppermute | solution.py:516
  131.9 12.9 %collective-permute-start.14 = (f32[136,128]{1,0:T(8,128)S(1)}, f32[136,128]{1,0:T(8,128)S(1)}, u32[]{:S(2)}, u32[]{:S(2)}) collective-permute-start(f32[136,128]{1,0:T(8,128)S(1)} %add_add_fusion.1), channel_id=1, source_target_pairs={{0,2},{1,3},{2,0},{3,1},{4,6},{5,7},{6,4},{7,5},{8,10},{9,11},{10,... | collective-permute-start | bytes 208904 | tf_op jit(solution)/shard_map/ppermute | solution.py:516
  134.1 35.2 %collective-permute-start.18 = (f32[256,256]{1,0:T(8,128)S(1)}, f32[256,256]{1,0:T(8,128)S(1)}, u32[]{:S(2)}, u32[]{:S(2)}) collective-permute-start(f32[256,256]{1,0:T(8,128)S(1)} %get-tuple-element.45), channel_id=1, source_target_pairs={{0,1},{1,2},{2,3},{3,4},{4,5},{5,6},{6,7},{8,9},{9,10},{10,11},{11... | collective-permute-start | bytes 786440 | tf_op jit(solution)/shard_map/ppermute | solution.py:512
  140.1 29.2 %collective-permute-start.19 = (f32[256,256]{1,0:T(8,128)S(1)}, f32[256,256]{1,0:T(8,128)S(1)}, u32[]{:S(2)}, u32[]{:S(2)}) collective-permute-start(f32[256,256]{1,0:T(8,128)S(1)} %get-tuple-element.46), channel_id=1, source_target_pairs={{1,0},{2,1},{3,2},{4,3},{5,4},{6,5},{7,6},{9,8},{10,9},{11,10},{12... | collective-permute-start | bytes 786440 | tf_op jit(solution)/shard_map/ppermute | solution.py:515
  144.8 12.7 %collective-permute-start.17 = (f32[136,128]{1,0:T(8,128)S(1)}, f32[136,128]{1,0:T(8,128)S(1)}, u32[]{:S(2)}, u32[]{:S(2)}) collective-permute-start(f32[136,128]{1,0:T(8,128)S(1)} %add_add_fusion.mine), channel_id=1, source_target_pairs={{0,8},{8,0},{16,24},{24,16},{32,40},{40,32},{48,56},{56,48},{64,72... | collective-permute-start | bytes 208904 | tf_op jit(solution)/shard_map/ppermute | solution.py:519
  (1 other events, 0.7 us)
